TPU v7x, 32 devices: a whole 2x2x4 slice. The times are simulated.
32 devices in a mesh: ctx: 16 (over z, y, core), wt: 2 (over x).
Axes of the slice: x: 2, y: 2, z: 4, core: 2. Of those that a mesh axis runs over, the one named last changes fastest.
Arguments:
- hidden_in: bfloat16 [2, 2048, 1024], P('wt', 'ctx'), may hold values from -6 to 6
- doc_start: int32 [2, 2048], P('wt', 'ctx'), may hold values from 0 to 1, as said below
- qkv_master: float32 [1024, 3072], P(('ctx', 'wt')), may hold values from -0.25 to 0.25
- out_master: float32 [1024, 1024], P(('ctx', 'wt')), may hold values from -0.75 to 0.75
- up_master: float32 [1024, 4096], P(('ctx', 'wt')), may hold values from -0.1875 to 0.1875
- down_master: float32 [4096, 1024], P(('ctx', 'wt')), may hold values from -0.125 to 0.125
- norm1_gain: float32 [1024], replicated, may hold values from 0.5 to 1.5
- norm1_bias: float32 [1024], replicated, may hold values from -3 to 3
- norm2_gain: float32 [1024], replicated, may hold values from 0.5 to 1.5
- norm2_bias: float32 [1024], replicated, may hold values from -3 to 3
- grad_out: bfloat16 [2, 2048, 1024], P('wt', 'ctx'), may hold values from -6 to 6
Outputs:
- layer_out: bfloat16 [2, 2048, 1024], P('wt', 'ctx')
- grad_in: bfloat16 [2, 2048, 1024], P('wt', 'ctx')
- qkv_grad: float32 [1024, 3072], P(('ctx', 'wt'))
- out_grad: float32 [1024, 1024], P(('ctx', 'wt'))
- up_grad: float32 [1024, 4096], P(('ctx', 'wt'))
- down_grad: float32 [4096, 1024], P(('ctx', 'wt'))
- norm1_gain_grad: float32 [1024], P(('ctx', 'wt'))
- norm1_bias_grad: float32 [1024], P(('ctx', 'wt'))
- norm2_gain_grad: float32 [1024], P(('ctx', 'wt'))
- norm2_bias_grad: float32 [1024], P(('ctx', 'wt'))
Inputs may be any that keep to these rules, and one draw needn't show every extreme that they name: `doc_start`: 1 marks the first token of a document, rows in storage order; position 0 of every stream starts a document; every document has 1 to 1024 tokens, and each stream has one of exactly 1024.
All inputs are finite; a program needn't handle non-finite values.
Results may differ from a plain program's by a relative error of at most 0.017.
Values may be sent and summed in bfloat16 or wider, within the bound.
No kernel may reach another device: no remote copies, remote signals or barrier semaphores. Data moves between devices by JAX's collectives and lax.ppermute only.
A program may use at most 192 MiB of HBM per device.

v0:
```python
from functools import partial

import jax
import jax.numpy as jnp
from jax import lax
from jax.experimental import pallas as pl
from jax.experimental.pallas import tpu as pltpu
from jax.sharding import Mesh
from jax.sharding import PartitionSpec as P

HEADS = 16
HD = 64
TRIPLE = 3 * HD
EPS = 1e-05
FAR = -1e30
TILE = 256
TEAM = 8
TAIL = 8
BF = jnp.bfloat16
F32 = jnp.float32
ALL = ("r", "zh", "zl", "y", "c", "x")
CTX = ("r", "zh", "zl", "y", "c")
PART = ("zh", "zl", "y", "c")
CHIPS = ("r", "zh", "zl", "y")
TP = ("zl", "y", "c")
GROUP = ("r", "zh", "x")
SWAP = [(0, 1), (1, 0)]
MASKS = [
    z * 8 + y * 4 + c * 2 + x for c in range(2) for y in range(2) for x in range(2) for z in range(4)
]
NN = ((1,), (0,))
NT = ((1,), (1,))
TN = ((0,), (0,))


def dot(one, two, dims):
    return lax.dot_general(one, two, (dims, ((), ())), preferred_element_type=F32)


def normalise(rows):
    centred = rows - jnp.mean(rows, axis=-1, keepdims=True)
    spread = lax.rsqrt(jnp.mean(centred * centred, axis=-1, keepdims=True) + EPS)
    return centred * spread, spread


def norm_back(grad, normed, spread, gain):
    scaled = grad * gain
    inner = (
        scaled
        - jnp.mean(scaled, axis=-1, keepdims=True)
        - normed * jnp.mean(scaled * normed, axis=-1, keepdims=True)
    )
    return inner * spread


def gelu_both(up):
    root = 0.7978845608028654
    square = up * up
    inner = jnp.tanh(root * up * (1.0 + 0.044715 * square))
    plus = 0.5 * (1.0 + inner)
    slope = plus + 0.5 * up * (1.0 - inner * inner) * root * (1.0 + 3.0 * 0.044715 * square)
    return up * plus, slope


def block_home(block, shards):
    return (block, 0) if block < shards else (2 * shards - 1 - block, 1)


def split_two(values):
    high = values.astype(BF)
    return high, (values - high.astype(F32)).astype(BF)


def after(array, *others):
    return lax.optimization_barrier((array, *others))[0]


class Place:
    def __init__(self, table):
        self.r, self.zh, self.zl, self.y, self.c, self.x = (table[at] for at in range(6))
        self.mate = self.zl * 4 + self.y * 2 + self.c
        self.ctx = self.zh * TEAM + self.mate

    def flat(self, wide):
        return (self.r * HEADS + self.ctx) * wide + self.x


def call(body, arrays, outs, scratch=(), smem=1, smem_outs=(), far=0, sems=0, limit=12, micros=0):
    vector = pl.BlockSpec(memory_space=pltpu.VMEM)
    scalar = pl.BlockSpec(memory_space=pltpu.SMEM)
    there = pl.BlockSpec(memory_space=pl.ANY)
    scratch = [pltpu.VMEM(shape, kind) for shape, kind in scratch]
    if sems:
        scratch.append(pltpu.SemaphoreType.DMA((sems,)))
    return pl.pallas_call(
        body,
        out_shape=[jax.ShapeDtypeStruct(shape, kind) for shape, kind in outs],
        in_specs=[scalar] * smem + [there] * far + [vector] * (len(arrays) - smem - far),
        out_specs=[scalar if at in smem_outs else vector for at in range(len(outs))],
        scratch_shapes=scratch,
        compiler_params=pltpu.CompilerParams(vmem_limit_bytes=limit << 20),
        cost_estimate=pl.CostEstimate(flops=micros * 10**9 + 1000, bytes_accessed=1 << 10, transcendentals=0),
    )(*arrays)


def start_copies(pairs, sems):
    copies = [pltpu.make_async_copy(source, target, sems.at[at]) for at, (source, target) in enumerate(pairs)]
    for copy in copies:
        copy.start()
    return copies


def first_kernel(table, hidden_ref, gain_ref, bias_ref, qkv_ref, out_ref, up_ref, down_ref, start_ref, *refs, runs):
    (
        norm_out, *heads, out_b, one_ref, two_ref, three_ref, four_ref, down_b,
        hidden_at, gain_at, bias_at, qkv_at, out_at, up_at, down_at, start_at, made_ref, sems,
    ) = refs
    ups = one_ref, two_ref, three_ref, four_ref
    place = Place(table)
    copies = start_copies(
        (
            (hidden_ref, hidden_at), (gain_ref, gain_at), (bias_ref, bias_at), (start_ref, start_at), (qkv_ref, qkv_at),
            (out_ref, out_at), (up_ref, up_at), (down_ref, down_at),
        ),
        sems,
    )
    for copy in copies[:3]:
        copy.wait()
    normed, _ = normalise(hidden_at[...].astype(F32))
    norm_out[...] = (normed * gain_at[...] + bias_at[...]).astype(BF)
    for copy in copies[3:]:
        copy.wait()
    rows = qkv_at.shape[0]
    half = rows // 2
    width = HEADS * HD
    starts = start_at[...].astype(F32).astype(BF)
    for head in range(HEADS):
        part = [qkv_at[:, at * width + head * HD : at * width + (head + 1) * HD].astype(BF) for at in range(3)]
        made_ref[head, :rows] = jnp.concatenate(part[:2], axis=1)
        made_ref[head, rows : rows + half] = jnp.concatenate([part[2][:half], part[2][half:]], axis=1)
        made_ref[head, rows + half :] = jnp.broadcast_to(starts, (TAIL, 2 * HD))
    for near in range(4):
        for far in range(4):
            heads[near][far] = made_ref[place.ctx ^ (far * 4 + near)]
    out_b[...] = out_at[...].astype(BF)
    piece = ups[0].shape[2] // runs
    for near in range(4):
        for high in range(2):
            mate = place.mate ^ (high * 4 + near)
            for at in range(runs):
                first = pl.multiple_of((at * TEAM + mate) * piece, piece)
                ups[near][high, :, at * piece : (at + 1) * piece] = up_at[:, pl.ds(first, piece)].astype(BF)
    rows, half = down_at.shape[0], down_at.shape[1] // 2
    down_b[:rows] = down_at[:, :half].astype(BF)
    down_b[rows:] = down_at[:, half:].astype(BF)


def settle_kernel(table, *refs):
    place = Place(table)
    for far in range(4):
        for near in range(4):
            refs[4][place.ctx ^ (far * 4 + near)] = refs[far][near]


def head_weights(packs, w_ref, wrows, wide):
    whalf = wrows // 2
    for x in range(wide):
        for at in range(packs[x].shape[0]):
            first = (at * wide + x) * wrows
            w_ref[first : first + wrows, : 2 * HD] = packs[x][at, :wrows]
            pair = packs[x][at, wrows : wrows + whalf]
            w_ref[first : first + whalf, 2 * HD :] = pair[:, :HD]
            w_ref[first + whalf : first + wrows, 2 * HD :] = pair[:, HD:]


def unstacked(refs):
    return [ref.at[at] for ref in refs for at in range(ref.shape[0])]


def in_order(place, packs, one_ref, two_ref):
    for at in range(packs[0].shape[0]):
        one_ref[at] = jnp.where(place.x == 0, packs[0][at], packs[1][at])
        two_ref[at] = jnp.where(place.x == 0, packs[1][at], packs[0][at])


def join_kernel(table, one_ref, two_ref, _, out_ref):
    place = Place(table)
    rows = one_ref.shape[1]
    for at in range(TEAM):
        mate = place.mate ^ at
        part = (one_ref if at < 4 else two_ref)[at % 4]
        if rows % 16 == 0:
            out_ref[pl.ds(pl.multiple_of(mate * rows, rows), rows), :] = part
        else:
            for to in range(TEAM):

                @pl.when(mate == to)
                def _(to=to, part=part):
                    out_ref[to * rows : (to + 1) * rows, :] = part


def mix_kernel(*refs):
    count = len(refs) - refs[0].shape[0]
    for near in range(count):
        for far, out in enumerate(refs[count:]):
            out[near] = refs[near][far]


def ring_shifts(chips):
    shifts = [0]
    for hop in range(1, chips // 2 + 1):
        shifts += [-hop, hop] if hop < chips // 2 else [-hop]
    return shifts


def ring_order(chips, place):
    long = chips // 2
    along = (place.r * 2 + place.zh) * 2 + place.zl
    spot = jnp.where(place.y == 0, along, chips - 1 - along)
    order = []
    for shift in ring_shifts(chips):
        at = lax.rem(spot + shift + chips, chips)
        order.append(jnp.where(at < long, 2 * at, 2 * (chips - 1 - at) + 1))
    return order


def forward_kernel(table, *refs, wrows, chips, others, wide):
    pieces, others, refs = refs[:chips], refs[chips : chips + others], refs[chips + others :]
    pieces = list(pieces) + unstacked(others)
    own_ref, *refs = refs
    packs, refs = ([own_ref, refs[0]], refs[1:]) if wide == 2 else (refs[:wide], refs[wide:])
    outs, seconds = refs[:4], refs[16:]
    lse_ref, begin_ref, lo_ref, w_top, w_low, q_ref, k_ref, v_ref, ot_ref, vt_ref, att_ref, w_ref = refs[4:16]
    place = Place(table)
    if wide == 2:
        in_order(place, packs, *seconds)
        packs = seconds
    head_weights(packs, w_ref, wrows, wide)
    w_top[...] = w_ref[: w_top.shape[0], :]
    w_low[...] = w_ref[w_top.shape[0] :, :]
    shards, half, _ = att_ref.shape
    rows = 2 * half
    total = shards * rows
    blocks = 2 * shards
    order = ring_order(chips, place)
    whalf = wrows // 2
    flags = []
    for block in range(blocks):
        shard, side = block_home(block, shards)
        row = own_ref[shard, wrows + whalf : wrows + whalf + 1].astype(F32)
        flags.append(row[:, side * half : (side + 1) * half])
    flags = jnp.concatenate(flags, axis=0)
    spots = half * lax.broadcasted_iota(jnp.int32, flags.shape, 0) + lax.broadcasted_iota(
        jnp.int32, flags.shape, 1
    )
    marks = jnp.where(flags > 0.5, spots.astype(F32), -1.0)
    lane = lax.broadcasted_iota(jnp.int32, marks.shape, 1)
    hop = 1
    while hop < half:
        moved = jnp.concatenate([marks[:, half - hop :], marks[:, : half - hop]], axis=1)
        marks = jnp.maximum(marks, jnp.where(lane >= hop, moved, -1.0))
        hop *= 2
    last = jnp.broadcast_to(marks[:, half - 1 :], marks.shape)
    line = lax.broadcasted_iota(jnp.int32, marks.shape, 0)
    hop = 1
    while hop < blocks:
        moved = jnp.concatenate([last[blocks - hop :], last[: blocks - hop]], axis=0)
        last = jnp.maximum(last, jnp.where(line >= hop, moved, -1.0))
        hop *= 2
    moved = jnp.concatenate([last[blocks - 1 :], last[: blocks - 1]], axis=0)
    begins = jnp.maximum(marks, jnp.where(line >= 1, moved, -1.0))
    group = TILE // half
    for tile in range(total // TILE):
        row = jnp.concatenate([begins[tile * group + at : tile * group + at + 1] for at in range(group)], axis=1)
        begin_ref[tile : tile + 1, :] = row.astype(jnp.int32)
        lo_ref[tile] = jnp.min(row).astype(jnp.int32) // TILE
    for which in range(2):
        for at in range(chips):
            made = dot(pieces[which * chips + at][...], w_ref[...], NN).astype(BF)
            shard = 2 * order[at] + (place.c if which == 0 else 1 - place.c)
            one = pl.multiple_of(shard * half, half)
            two = pl.multiple_of((blocks - 1 - shard) * half, half)
            scaled = made[:, :HD] * BF(HD**-0.5)
            for first, part in ((one, slice(0, half)), (two, slice(half, rows))):
                q_ref[pl.ds(first, half), :] = scaled[part]
                k_ref[pl.ds(first, half), :] = made[part, HD : 2 * HD]
                v_ref[pl.ds(first, half), :] = made[part, 2 * HD :]
    for at in range(0, total, 128):
        vt_ref[:, at : at + 128] = v_ref[at : at + 128, :].astype(F32).T.astype(BF)
    for tile in range(total // TILE):
        query = q_ref[tile * TILE : (tile + 1) * TILE, :]
        begin = begin_ref[tile : tile + 1, :]
        query_pos = tile * TILE + lax.broadcasted_iota(jnp.int32, (TILE, TILE), 1)

        def step(at, state):
            top, sums, accum = state
            first = pl.multiple_of(at * TILE, TILE)
            scores = dot(k_ref[pl.ds(first, TILE), :], query, NT)
            key_pos = first + lax.broadcasted_iota(jnp.int32, (TILE, TILE), 0)
            scores = jnp.where((key_pos >= begin) & (key_pos <= query_pos), scores, FAR)
            higher = jnp.maximum(top, jnp.max(scores, axis=0, keepdims=True))
            weights = jnp.exp(scores - higher)
            factor = jnp.exp(top - higher)
            sums = sums * factor + jnp.sum(weights, axis=0, keepdims=True)
            accum = accum * factor + dot(vt_ref[:, pl.ds(first, TILE)], weights.astype(BF), NN)
            return higher, sums, accum

        top, sums, accum = lax.fori_loop(
            lo_ref[tile],
            tile + 1,
            step,
            (jnp.full((1, TILE), FAR, F32), jnp.zeros((1, TILE), F32), jnp.zeros((HD, TILE), F32)),
        )
        out = accum / sums
        ot_ref[:, tile * TILE : (tile + 1) * TILE] = out
        lse_ref[tile : tile + 1, :] = top + jnp.log(sums)
        turned = out.T.astype(BF)
        for piece in range(group):
            shard, side = block_home(tile * group + piece, shards)
            att_ref[shard, :, side * HD : (side + 1) * HD] = turned[piece * half : (piece + 1) * half]
    for near in range(4):
        for far in range(4):
            outs[near][far] = att_ref[place.r * HEADS + (place.ctx ^ (far * 4 + near))]


def middle_kernel(table, *refs, count):
    weights, atts, refs = refs[:count], refs[count : count + 4], refs[count + 4 :]
    hidden_ref, gain_ref, bias_ref, att_out, mid_out, norm_out, w_ref, heads_ref = refs
    place = Place(table)
    if count > 1:
        for at, ref in enumerate(unstacked(weights)):
            rows = ref.shape[0]
            first = (place.flat(2) ^ MASKS[at]) * rows
            w_ref[pl.ds(pl.multiple_of(first, rows), rows), :] = ref[...]
    else:
        w_ref[...] = weights[0][...]
    for far in range(4):
        for near in range(4):
            heads_ref[place.ctx ^ (far * 4 + near)] = atts[far][near]
    half = heads_ref.shape[1]
    for head in range(0, HEADS, 2):
        for side in range(2):
            lanes = slice(side * HD, (side + 1) * HD)
            att_out[side * half : (side + 1) * half, head * HD : (head + 2) * HD] = jnp.concatenate(
                [heads_ref[head, :, lanes], heads_ref[head + 1, :, lanes]], axis=1
            )
    mid = hidden_ref[...].astype(F32) + dot(att_out[...], w_ref[...], NN)
    mid_out[...] = mid
    normed, _ = normalise(mid)
    norm_out[...] = (normed * gain_ref[...] + bias_ref[...]).astype(BF)


def feed_kernel(table, *refs, grads, mids, wide, groups):
    grads, mids, refs = refs[:grads], refs[grads : grads + mids], refs[grads + mids :]
    *weights, lay_keep, lay_send, mnd_keep, mnd_send, mid_out, act_out, delta_out, grad_out, up_ref, down_ref = refs
    place = Place(table)
    for out, arrays in ((grad_out, grads), (mid_out, mids)):
        first = 0
        for ref in arrays:
            for part in unstacked([ref]) if len(ref.shape) == 3 else [ref]:
                out[first : first + part.shape[0], :] = part[...]
                first += part.shape[0]
    width = mid_out.shape[1]
    own = width // (TEAM * groups)
    ffn = down_ref.shape[0] // groups
    moving = len(weights) > 2
    count = len(weights) // 2
    ups, downs = weights[:count], weights[count:]
    if not moving:
        ups, downs = unstacked(ups), unstacked(downs)
    for at in range(groups):
        if moving:
            high, x = place.zh ^ (at & 1), place.x ^ (at >> 1)
        else:
            high, x = at // wide, at % wide
        for mate in range(TEAM):
            first = ((high * TEAM + mate) * wide + x) * own
            if moving:
                first = pl.multiple_of(first, own)
            up_ref[pl.ds(first, own), :] = ups[at][mate * own : (mate + 1) * own, :]
        first = (high * wide + x) * ffn
        if moving:
            first = pl.multiple_of(first, ffn)
        down_ref[pl.ds(first, ffn), : width // 2] = downs[at][:ffn, :]
        down_ref[pl.ds(first, ffn), width // 2 :] = downs[at][ffn:, :]
    total = mid_out.shape[0]
    run = 256
    half = total // 2
    for first in list(range(half, total, run)) + list(range(0, half, run)):
        here = slice(first, first + run)
        up = dot(mid_out[here, :], up_ref[...], NN)
        value, slope = gelu_both(up)
        act = value.astype(BF)
        act_out[here, :] = act
        delta = (dot(grad_out[here, :], down_ref[...], NT) * slope).astype(BF)
        delta_out[here, :] = delta
        back = dot(delta, up_ref[...], NT)
        fore = dot(act, down_ref[...], NN)
        if first < half:
            mnd_keep[here, :] = back
            lay_keep[here, :] = fore.astype(BF)
        else:
            there = slice(first - half, first - half + run)
            mnd_send[there, :] = back.astype(BF)
            lay_send[there, :] = fore.astype(BF)


def turn_kernel(
    table, grad_ref, mid_ref, w_ref, keep_top, got_top, keep_low, got_low, gain_ref, delta_out, bf_out, *refs
):
    *outs, made_ref = refs
    mnd = jnp.concatenate(
        [keep_top[...] + got_top[...].astype(F32), keep_low[...] + got_low[...].astype(F32)], axis=0
    )
    normed, spread = normalise(mid_ref[...])
    delta = grad_ref[...].astype(F32) + norm_back(mnd, normed, spread, gain_ref[...])
    delta_out[...] = delta
    narrow = delta.astype(BF)
    bf_out[...] = narrow
    back = dot(narrow, w_ref[...], NT).astype(BF)
    half = made_ref.shape[1]
    for head in range(HEADS):
        cols = slice(head * HD, (head + 1) * HD)
        made_ref[head] = jnp.concatenate([back[:half, cols], back[half:, cols]], axis=1)
    place = Place(table)
    for near in range(4):
        for far in range(4):
            outs[near][far] = made_ref[place.ctx ^ (far * 4 + near)]


TEAM_ORDER = (0, 4, 2, 6, 1, 5, 3, 7)


def out_grad_kernel(table, lay_keep, lay_send, att_ref, delta_ref, keep_out, send_out, part_ref, *, wide, wrows):
    turned = att_ref[...].astype(F32).T.astype(BF)
    part_ref[...] = dot(turned, delta_ref[...], NN).astype(BF).reshape(part_ref.shape)
    place = Place(table)
    rows = lay_keep.shape[0] // 4
    highs = part_ref.shape[0] // (TEAM * wide)
    for at in range(TEAM):
        mate = place.mate ^ TEAM_ORDER[at]
        out, lay = (keep_out, lay_keep) if at < 4 else (send_out, lay_send)
        first = (at % 4) * 2 * rows
        out[first : first + rows, :] = lay[(at % 4) * rows : (at % 4 + 1) * rows, :]
        first += rows
        for x in range(wide):
            for high in range(highs):
                out[first : first + wrows, :] = part_ref[(high * TEAM + mate) * wide + x]
                first += wrows


def up_pack_kernel(table, part_ref, delta_ref, *outs, wide):
    _, tall, _ = outs[0].shape
    rows = tall - TAIL
    tail = sum_lines(jnp.sum(delta_ref[...].astype(F32), axis=0, keepdims=True))
    place = Place(table)
    highs = len(outs) // wide
    for at, out in enumerate(outs):
        if wide == 2:
            x, high = place.x ^ (at >> 1), place.zh ^ (at & 1)
        else:
            x, high = at // highs, at % highs
        for mate in range(TEAM):
            first = ((high * TEAM + mate) * wide + x) * rows
            if wide == 2:
                first = pl.multiple_of(first, rows)
            out[mate, :rows] = part_ref[pl.ds(first, rows), :].astype(BF)
            out[mate, rows:] = tail


def down_pack_kernel(table, part_ref, *outs, wide):
    rows = outs[0].shape[0]
    place = Place(table)
    highs = len(outs) // wide
    for at, out in enumerate(outs):
        if wide == 2:
            x, high = place.x ^ (at >> 1), place.zh ^ (at & 1)
        else:
            x, high = at // highs, at % highs
        first = (high * wide + x) * rows
        if wide == 2:
            first = pl.multiple_of(first, rows)
        out[...] = part_ref[pl.ds(first, rows), :].astype(BF)


def up_add_kernel(own_ref, got_ref, out_ref):
    rows = out_ref.shape[1] - TAIL
    for mate in range(TEAM):
        out_ref[mate, :rows], out_ref[mate, rows:] = add_lines(own_ref[mate], got_ref[mate])


def sum_kernel(own_ref, got_ref, out_ref):
    out_ref[...] = (own_ref[...].astype(F32) + got_ref[...].astype(F32)).astype(out_ref.dtype)


def up_share_kernel(table, own_ref, got_ref, *outs):
    place = Place(table)
    rows = own_ref.shape[1] - TAIL
    for near in range(4):
        for high in range(2):
            mate = place.mate ^ (high * 4 + near)
            out = outs[near]
            out[high, :rows], out[high, rows:] = add_lines(own_ref[mate], got_ref[mate])


def sum_lines(sums):
    high, low = split_two(sums)
    line = lax.broadcasted_iota(jnp.int32, (8, sums.shape[1]), 0)
    return jnp.where(line == 0, high.astype(F32), jnp.where(line == 1, low.astype(F32), 0.0)).astype(BF)


def add_lines(own, got):
    rows = own.shape[0] - TAIL
    total = own.astype(F32) + got.astype(F32)
    return total[:rows].astype(BF), sum_lines(total[rows : rows + 1] + total[rows + 1 : rows + 2])


def owner_column(row_ref, first, rows):
    shape = (rows, row_ref.shape[1])
    hit = lax.broadcasted_iota(jnp.int32, shape, 1) == first + lax.broadcasted_iota(jnp.int32, shape, 0)
    return jnp.sum(jnp.where(hit, row_ref[...], 0.0), axis=1, keepdims=True)


def as_row(column):
    shape = (column.shape[0],) * 2
    hit = lax.broadcasted_iota(jnp.int32, shape, 0) == lax.broadcasted_iota(jnp.int32, shape, 1)
    return jnp.sum(jnp.where(hit, column, 0.0), axis=0, keepdims=True)


def norm_grads(place, master_ref, grad_ref, sums, gain_ref, bias_ref, gain_out, bias_out, wide):
    rows = master_ref.shape[0]
    first = place.flat(wide) * rows
    own = master_ref[...].astype(BF).astype(F32)
    bias_grad = jnp.sum(own * sums, axis=1, keepdims=True)
    bias_out[...] = as_row(bias_grad)
    gain_grad = jnp.sum(own * grad_ref[...], axis=1, keepdims=True) - owner_column(bias_ref, first, rows) * bias_grad
    gain_out[...] = as_row(gain_grad / owner_column(gain_ref, first, rows))


def up_end_kernel(table, one_ref, two_ref, own_ref, gain_ref, bias_ref, grad_out, gain_out, bias_out, sum_ref, *, runs, wide):
    place = Place(table)
    rows = own_ref.shape[0]
    piece = one_ref.shape[2] // runs
    for high, ref in ((0, one_ref), (1, two_ref)):
        for near in range(4):
            mate = place.mate ^ (high * 4 + near)
            for at in range(runs):
                there = pl.ds(pl.multiple_of((at * TEAM + mate) * piece, piece), piece)
                part = ref[near, :, at * piece : (at + 1) * piece].astype(F32)
                grad_out[:, there] = part[:rows]
                sum_ref[:, there] = part[rows : rows + 1] + part[rows + 1 : rows + 2]
    norm_grads(place, own_ref, grad_out, sum_ref[...], gain_ref, bias_ref, gain_out, bias_out, wide)


def qkv_end_kernel(table, *refs, wide):
    parts, (own_ref, gain_ref, bias_ref, grad_out, gain_out, bias_out, all_ref) = refs[:4], refs[4:]
    place = Place(table)
    for far in range(4):
        for near in range(4):
            all_ref[place.ctx ^ (far * 4 + near)] = parts[far][near]
    rows = own_ref.shape[0]
    half = rows // 2
    width = HEADS * HD
    body = rows + half
    for head in range(0, HEADS, 2):
        for at in range(2):
            lanes = slice(at * HD, (at + 1) * HD)
            grad_out[:, at * width + head * HD : at * width + (head + 2) * HD] = jnp.concatenate(
                [all_ref[head, :rows, lanes], all_ref[head + 1, :rows, lanes]], axis=1
            ).astype(F32)
        for side in range(2):
            lanes = slice(side * HD, (side + 1) * HD)
            grad_out[side * half : (side + 1) * half, 2 * width + head * HD : 2 * width + (head + 2) * HD] = (
                jnp.concatenate([all_ref[head, rows:body, lanes], all_ref[head + 1, rows:body, lanes]], axis=1).astype(
                    F32
                )
            )
    lines = [[], [], []]
    for head in range(HEADS):
        tail = all_ref[head, body:, :].astype(F32)
        pair = tail[0:1] + tail[1:2]
        lines[0].append(pair[:, :HD])
        lines[1].append(pair[:, HD:])
        lines[2].append(tail[2:3, :HD] + tail[2:3, HD:])
    sums = jnp.concatenate(lines[0] + lines[1] + lines[2], axis=1)
    norm_grads(place, own_ref, grad_out, sums, gain_ref, bias_ref, gain_out, bias_out, wide)


def backward_kernel(table, lo_ref, *refs):
    douts, refs = refs[:4], refs[4:]
    (
        q_ref, k_ref, v_ref, ot_ref, lse_ref, begin_ref, own_out, mate_out, dn_ref, sum_ref,
        do_ref, dop_ref, kt_ref, dq_ref, dk_ref, dv_ref, da_ref,
    ) = refs
    place = Place(table)
    for part in range(douts[0].shape[0]):
        for far in range(4):
            for near in range(4):
                do_ref[part * HEADS + (place.ctx ^ (far * 4 + near))] = douts[far][part, near]
    shards, half, _ = do_ref.shape
    rows = 2 * half
    total = shards * rows
    for block in range(2 * shards):
        shard, side = block_home(block, shards)
        dop_ref[block * half : (block + 1) * half, :] = do_ref[shard, :, side * HD : (side + 1) * HD]
    for at in range(0, total, 128):
        kt_ref[:, at : at + 128] = k_ref[at : at + 128, :].astype(F32).T.astype(BF)
    dk_ref[...] = jnp.zeros_like(dk_ref)
    dv_ref[...] = jnp.zeros_like(dv_ref)
    for tile in range(total // TILE):
        here = slice(tile * TILE, (tile + 1) * TILE)
        query = q_ref[here, :]
        dout = dop_ref[here, :]
        begin = begin_ref[tile : tile + 1, :]
        lse = lse_ref[tile : tile + 1, :]
        row_dot = jnp.sum(dout.astype(F32).T * ot_ref[:, here], axis=0, keepdims=True)
        query_pos = tile * TILE + lax.broadcasted_iota(jnp.int32, (TILE, TILE), 1)

        def step(at, accum):
            first = pl.multiple_of(at * TILE, TILE)
            there = pl.ds(first, TILE)
            scores = dot(k_ref[there, :], query, NT)
            key_pos = first + lax.broadcasted_iota(jnp.int32, (TILE, TILE), 0)
            allowed = (key_pos >= begin) & (key_pos <= query_pos)
            probs = jnp.where(allowed, jnp.exp(scores - lse), 0.0)
            dprobs = dot(v_ref[there, :], dout, NT)
            delta = (probs * (dprobs - row_dot)).astype(BF)
            dv_ref[there, :] += dot(probs.astype(BF), dout, NN)
            dk_ref[there, :] += dot(delta, query, NN)
            return accum + dot(kt_ref[:, there], delta, NN)

        accum = lax.fori_loop(lo_ref[tile], tile + 1, step, jnp.zeros((HD, TILE), F32))
        dq_ref[here, :] = (accum * HD**-0.5).T
    sums = jnp.zeros((1, TRIPLE), F32)
    for block in range(2 * shards):
        shard, side = block_home(block, shards)
        at = slice(block * half, (block + 1) * half)
        pair = jnp.concatenate([dq_ref[at, :], dk_ref[at, :]], axis=1).astype(BF)
        last = dv_ref[at, :].astype(BF)
        da_ref[shard, side * half : (side + 1) * half, :] = pair
        da_ref[shard, rows : rows + half, side * HD : (side + 1) * HD] = last
        to = slice(side * half, (side + 1) * half)
        joined = jnp.concatenate([pair, last], axis=1)
        dn_ref[shard, to, :] = joined
        sums = sums + jnp.sum(joined.astype(F32), axis=0, keepdims=True)
    sum_ref[...] = sums
    base = place.r * HEADS
    for at in range(TEAM):
        own_out[at] = da_ref[base + place.zh * TEAM + at]
        mate_out[at] = da_ref[base + (1 - place.zh) * TEAM + at]


def qkv_lines(pair, last):
    line = lax.broadcasted_iota(jnp.int32, (8, 2 * HD), 0)
    high, low = split_two(pair)
    both = jnp.concatenate(split_two(last), axis=1)
    lines = jnp.where(line == 0, high.astype(F32), jnp.where(line == 1, low.astype(F32), both.astype(F32)))
    return lines.astype(BF)


def qkv_grad_kernel(table, *refs, repeats, chips, others, wide):
    pieces, stacks, (dn_ref, sum_ref, *outs, acc_ref) = refs[:chips], refs[chips : chips + others], refs[chips + others :]
    pieces = list(pieces) + unstacked(stacks)
    place = Place(table)
    order = ring_order(chips, place)
    total = None
    for which in range(2):
        for at in range(chips):
            shard = 2 * order[at] + (place.c if which == 0 else 1 - place.c)
            turned = dn_ref[shard].astype(F32).T.astype(BF)
            step = dot(turned, pieces[which * chips + at][...], NN)
            total = step if total is None else total + step
    acc_ref[...] = total.T
    owners, tall, _ = outs[0].shape
    rows = (tall - TAIL) * 2 // 3
    half = rows // 2
    sums = sum_ref[...]
    lines = qkv_lines(sums[:, : 2 * HD], sums[:, 2 * HD :])

    def write(base):
        for at, out in enumerate(outs):
            x = place.x ^ at if wide == 2 else at
            for owner in range(owners):
                first = base + (owner * wide + x) * rows
                if wide == 2:
                    first = pl.multiple_of(first, rows)
                grad = acc_ref[pl.ds(first, rows), :]
                out[owner, :rows] = grad[:, : 2 * HD].astype(BF)
                out[owner, rows : rows + half] = jnp.concatenate(
                    [grad[:half, 2 * HD :], grad[half:, 2 * HD :]], axis=1
                ).astype(BF)
                out[owner, rows + half :] = lines

    if repeats == 1:
        write(0)
    else:
        for at in range(repeats):
            pl.when(place.r == at)(partial(write, at * owners * wide * rows))


def qkv_add_kernel(table, own_ref, got_ref, *outs):
    place = Place(table)
    body = own_ref.shape[1] - TAIL
    for near in range(4):
        for far in range(4):
            at = place.ctx ^ (far * 4 + near)
            total = own_ref[at].astype(F32) + got_ref[at].astype(F32)
            outs[near][far, :body] = total[:body].astype(BF)
            tail = total[body:]
            outs[near][far, body:] = qkv_lines(tail[0:1] + tail[1:2], tail[2:3, :HD] + tail[2:3, HD:])


def spread_kernel(_, keep_ref, got_ref, send_z, send_y, top_out, low_out):
    rows = keep_ref.shape[0] // 4
    half = rows // 2
    for at in range(4):
        for side in range(2):
            here = slice(at * rows + side * half, at * rows + (side + 1) * half)
            total = keep_ref[here, :].astype(F32) + got_ref[here, :].astype(F32)
            if side == 0:
                if at % 2 == 0:
                    top_out[at // 2] = total
                else:
                    send_z[at // 2] = total.astype(BF)
            elif at < 2:
                low_out[at] = total
            else:
                send_y[at - 2] = total.astype(BF)


def narrow_kernel(_, top_ref, got_z, low_ref, got_y, send_y, send_z, top_out, low_out):
    top_out[...] = top_ref[0] + got_z[0].astype(F32)
    low_out[...] = low_ref[0] + got_y[0].astype(F32)
    send_y[...] = (top_ref[1] + got_z[1].astype(F32)).astype(BF)
    send_z[...] = (low_ref[1] + got_y[1].astype(F32)).astype(BF)


def input_kernel(table, own_ref, got_ref, *refs):
    tall = own_ref.shape[1]
    rows = tall * 2 // 3
    half = rows // 2
    place = Place(table)
    *weights, keep_out, send_out, lhs_ref, rhs_ref = refs
    first = 0
    for w_own, w_got in zip(weights[:2], weights[2:], strict=True):
        here = slice(first, first + w_got.shape[0])
        rhs_ref[here, : 2 * HD] = w_own[:, : 2 * HD]
        rhs_ref[here, 2 * HD : 3 * HD] = w_own[:, 2 * HD :]
        rhs_ref[here, 3 * HD : 4 * HD] = w_got[:, 2 * HD :]
        rhs_ref[here, 4 * HD :] = w_got[:, : 2 * HD]
        first += w_got.shape[0]
    for at in range(TEAM):
        mate = place.mate ^ TEAM_ORDER[at]
        first = at * rows
        one, two = own_ref[mate], got_ref[mate]
        lhs_ref[first : first + rows, : 2 * HD] = one[:rows]
        lhs_ref[first : first + rows, 4 * HD :] = two[:rows]
        for side in range(2):
            lanes = slice(side * HD, (side + 1) * HD)
            lhs_ref[first + side * half : first + (side + 1) * half, 2 * HD : 4 * HD] = jnp.concatenate(
                [one[rows:, lanes], two[rows:, lanes]], axis=1
            )
    middle = TEAM * rows // 2
    send_out[...] = dot(lhs_ref[middle:, :], rhs_ref[...], NT).astype(BF)
    keep_out[...] = dot(lhs_ref[:middle, :], rhs_ref[...], NT)


def last_kernel(_, keep_top, got_top, keep_low, got_low, mid_delta_ref, hidden_ref, gain_ref, out_ref):
    grad = jnp.concatenate(
        [keep_top[...] + got_top[...].astype(F32), keep_low[...] + got_low[...].astype(F32)], axis=0
    )
    normed, spread = normalise(hidden_ref[...].astype(F32))
    out_ref[...] = (mid_delta_ref[...] + norm_back(grad, normed, spread, gain_ref[...])).astype(BF)


def outs_kernel(table, mid_ref, lay_ref, got_lay, part_ref, got_part, lay_out, *outs, wide):
    lay_out[...] = (mid_ref[...] + lay_ref[...] + got_lay[...].astype(F32)).astype(BF)
    rows = outs[0].shape[0]
    place = Place(table)
    highs = len(outs) // wide
    for at, out in enumerate(outs):
        if wide == 2:
            x, high = place.x ^ (at >> 1), place.zh ^ (at & 1)
        else:
            x, high = at // highs, at % highs
        first = (x * highs + high) * rows
        if wide == 2:
            first = pl.multiple_of(first, rows)
        out[...] = (part_ref[pl.ds(first, rows), :] + got_part[pl.ds(first, rows), :].astype(F32)).astype(BF)


def after(array, *others):
    return lax.optimization_barrier((array, *others))[0]


def apart(count, mask):
    return [(at, at ^ mask) for at in range(count)]


def stack(arrays):
    count = sum(array.shape[0] if array.ndim == 3 else 1 for array in arrays)
    return call(stack_kernel, arrays, [((count,) + arrays[0].shape[-2:], arrays[0].dtype)], smem=0)[0]


def meet(*arrays):
    return lax.optimization_barrier(arrays)


def near(arrays):
    return [lax.ppermute(arrays[at], ("y", "c"), apart(4, at)) for at in range(1, 4)]


def far(arrays):
    return [lax.ppermute(arrays[at], ("zh", "zl"), apart(4, at)) for at in range(1, 4)]


def swap(array, axis):
    return lax.ppermute(array, axis, SWAP)


def mix(arrays):
    shape = arrays[0].shape
    return call(mix_kernel, arrays, [((len(arrays),) + shape[1:], arrays[0].dtype)] * shape[0], smem=0)


def stack_kernel(*refs):
    at = 0
    for ref in refs[:-1]:
        count = ref.shape[0] if len(ref.shape) == 3 else 1
        for part in range(count):
            refs[-1][at] = ref[part] if len(ref.shape) == 3 else ref[...]
            at += 1


def spread(table, keep, got):
    shape = (keep.shape[0] // 8, keep.shape[1])
    return call(spread_kernel, (table, keep, got), [((2, *shape), BF)] * 2 + [((2, *shape), F32)] * 2)


def narrow(table, top, got_z, low, got_y):
    shape = top.shape[1:]
    return call(narrow_kernel, (table, top, got_z, low, got_y), [(shape, BF)] * 2 + [(shape, F32)] * 2)


def add(one, two, kind):
    return call(sum_kernel, (one, two), [(one.shape, kind)], smem=0)[0]


class Steps:
    def __init__(self, arrays, sizes):
        (
            self.hidden, self.start, self.qkv, self.out, self.up, self.down,
            gain1, bias1, gain2, bias2, self.grad,
        ) = arrays
        self.hidden, self.grad = self.hidden[0], self.grad[0]
        self.gain1, self.bias1, self.gain2, self.bias2 = (a[None] for a in (gain1, bias1, gain2, bias2))
        self.repeats, self.wide = sizes["r"], sizes["x"]
        self.rows, self.width = self.hidden.shape
        self.half = self.rows // 2
        self.shards = self.repeats * HEADS
        self.total = self.shards * self.rows
        self.wrows, self.ffn = self.qkv.shape[0], self.down.shape[0]
        self.highs = 2 * self.repeats
        self.cols = self.highs * self.wide * self.ffn
        self.many = TEAM * self.rows
        self.qkv_tall = self.wrows * 3 // 2 + TAIL
        self.up_tall = self.wrows + TAIL
        self.sides = self.wide * self.highs
        self.piece = ((4, self.half, 2 * HD), BF)
        self.table = jnp.stack([lax.axis_index(axis).astype(jnp.int32) for axis in ALL])

    def first(self):
        masters = (self.qkv, self.out, self.up, self.down)
        row = ((1, self.width), F32)
        outs = call(
            partial(first_kernel, runs=self.highs),
            (self.table, self.hidden, self.gain1, self.bias1, *masters, self.start),
            [
                ((self.rows, self.width), BF),
                *[((4, self.qkv_tall, 2 * HD), BF)] * 4,
                ((self.wrows, self.width), BF),
                *[((2, self.wrows, self.cols), BF)] * 4,
                ((2 * self.ffn, self.width // 2), BF),
            ],
            [
                ((self.rows, self.width), BF), row, row,
                *[(a.shape, F32) for a in masters],
                (self.start.shape, jnp.int32),
                ((HEADS, self.qkv_tall, 2 * HD), BF),
            ],
            far=8,
            sems=8,
            limit=58,
        )
        return outs[0], list(outs[1:5]), outs[5], list(outs[6:10]), outs[10]

    def forward(self, pieces, others, packs):
        tokens = ((self.total, HD), BF)
        tiles = (self.total // TILE, TILE)
        whalf = ((self.width // 2, TRIPLE), BF)
        outs = call(
            partial(forward_kernel, wrows=self.wrows, chips=len(pieces), others=len(others), wide=self.wide),
            (self.table, *pieces, *others, *packs),
            [
                *[self.piece] * 4,
                (tiles, F32), (tiles, jnp.int32), (tiles[:1], jnp.int32),
                whalf, whalf,
                tokens, tokens, tokens,
                ((HD, self.total), F32),
            ],
            [((HD, self.total), BF), ((self.shards, self.half, 2 * HD), BF), ((self.width, TRIPLE), BF)]
            + [((self.shards, self.qkv_tall, 2 * HD), BF)] * (2 if self.wide == 2 else 0),
            smem_outs=(6,),
            limit=12 * self.repeats,
            micros=14,
        )
        lse, begin, low = outs[4:7]
        return list(outs[:4]), list(outs[7:9]), (low, *outs[9:], lse, begin)

    def middle(self, weights, heads):
        return call(
            partial(middle_kernel, count=len(weights)),
            (self.table, *weights, *heads, self.hidden, self.gain2, self.bias2),
            [
                ((self.rows, self.width), BF),
                ((self.rows, self.width), F32),
                ((self.rows, self.width), BF),
                ((self.width, self.width), BF),
            ],
            [((HEADS, self.half, 2 * HD), BF)],
        )

    def feed(self, grads, mids, weights):
        half, full = (self.many // 2, self.width), (self.many, self.width)
        inner = ((self.many, self.cols), BF)
        return call(
            partial(
                feed_kernel, grads=len(grads), mids=len(mids), wide=self.wide, groups=self.highs * self.wide
            ),
            (self.table, *grads, *mids, *weights),
            [(half, BF), (half, BF), (half, F32), (half, BF), (full, BF), inner, inner, (full, BF)],
            [((self.width, self.cols), BF), ((self.cols, self.width), BF)],
            micros=6,
        )

    def up_gradient(self, mids, delta):
        return call(
            partial(up_pack_kernel, wide=self.wide),
            (self.table, dot(mids, delta, TN), delta),
            [((TEAM, self.up_tall, self.cols), BF)] * self.sides,
        )

    def down_gradient(self, acts, grads):
        return call(
            partial(down_pack_kernel, wide=self.wide),
            (self.table, dot(acts, grads, TN)),
            [((self.ffn, self.width), BF)] * self.sides,
        )

    def turn(self, mid, w_out, ends):
        outs = call(
            turn_kernel,
            (self.table, self.grad, mid, w_out, *ends, self.gain2),
            [((self.rows, self.width), F32), ((self.rows, self.width), BF), *[self.piece] * 4],
            [((HEADS, self.half, 2 * HD), BF)],
        )
        return outs[0], outs[1], list(outs[2:])

    def out_gradient(self, lay_keep, lay_send, attended, delta):
        return call(
            partial(out_grad_kernel, wide=self.wide, wrows=self.wrows),
            (self.table, lay_keep, lay_send, attended, delta),
            [((self.many, self.width), BF)] * 2,
            [((self.shards * self.wide, self.wrows, self.width), BF)],
        )

    def backward(self, kept, douts):
        low, query, keys, values, out_t, lse, begin = kept
        tall = self.rows + self.half
        total = ((self.total, HD), F32)
        return call(
            backward_kernel,
            (self.table, low, *douts, query, keys, values, out_t, lse, begin),
            [
                ((TEAM, tall, 2 * HD), BF),
                ((TEAM, tall, 2 * HD), BF),
                ((self.shards, self.rows, TRIPLE), BF),
                ((1, TRIPLE), F32),
            ],
            [
                ((self.shards, self.half, 2 * HD), BF),
                ((self.total, HD), BF),
                ((HD, self.total), BF),
                total, total, total,
                ((self.shards, tall, 2 * HD), BF),
            ],
            smem=2,
            limit=12 * self.repeats,
            micros=12,
        )

    def qkv_gradient(self, pieces, others, by_shard, sums):
        return call(
            partial(
                qkv_grad_kernel,
                repeats=self.repeats, chips=len(pieces), others=len(others), wide=self.wide,
            ),
            (self.table, *pieces, *others, by_shard, sums),
            [((HEADS, self.qkv_tall, 2 * HD), BF)] * self.wide,
            [((self.width, TRIPLE), F32)],
        )

    def up_share(self, own, got):
        return list(call(up_share_kernel, (self.table, own, got), [((2, self.up_tall, self.cols), BF)] * 4))

    def qkv_share(self, own, got):
        return list(call(qkv_add_kernel, (self.table, own, got), [((4, self.qkv_tall, 2 * HD), BF)] * 4))

    def outputs(self, mid, ends):
        return call(
            partial(outs_kernel, wide=self.wide),
            (self.table, mid, *ends),
            [((self.rows, self.width), BF)] + [((self.wrows, self.width), BF)] * self.sides,
        )

    def inputs(self, to_own, from_mate, weights, mates):
        return call(
            input_kernel,
            (self.table, to_own, from_mate, *weights, *mates),
            [((self.many // 2, self.width), F32), ((self.many // 2, self.width), BF)],
            [((self.many, 2 * TRIPLE), BF), ((self.width, 2 * TRIPLE), BF)],
        )

    def last(self, ends, mid_delta):
        return call(
            last_kernel,
            (self.table, *ends, mid_delta, self.hidden, self.gain1),
            [((self.rows, self.width), BF)],
        )[0]

    def up_end(self, ends):
        line = ((1, self.wrows), F32)
        return call(
            partial(up_end_kernel, runs=self.highs, wide=self.wide),
            (self.table, *ends, self.up, self.gain2, self.bias2),
            [(self.up.shape, F32), line, line],
            [((1, self.up.shape[1]), F32)],
        )

    def qkv_end(self, ends):
        line = ((1, self.wrows), F32)
        return call(
            partial(qkv_end_kernel, wide=self.wide),
            (self.table, *ends, self.qkv, self.gain1, self.bias1),
            [(self.qkv.shape, F32), line, line],
            [((HEADS, self.qkv_tall, 2 * HD), BF)],
        )


def ring_moves(long):
    count = 2 * long
    order = [2 * at for at in range(long)] + [2 * at + 1 for at in reversed(range(long))]
    right = [(order[at], order[(at + 1) % count]) for at in range(count)]
    return right, [(two, one) for one, two in right]


def results(layer_out, grad_in, qkv, out, up, down):
    return (
        layer_out[None], grad_in[None], qkv[0], out, up[0], down,
        qkv[1][0], qkv[2][0], up[1][0], up[2][0],
    )


def local(*arrays, sizes):
    s = Steps(arrays, sizes)
    right, left = ring_moves(4)

    def ahead(array):
        return lax.ppermute(array, CHIPS, right)

    def behind(array):
        return lax.ppermute(array, CHIPS, left)

    norm_in, by_head, out_b, up_b, down_b = s.first()
    a1, b1, *got = meet(ahead(norm_in), behind(norm_in), *near(by_head))
    packs = mix([by_head[0], *got])
    a2, b2, *got = meet(ahead(a1), behind(b1), *far(packs))
    (packed,) = call(settle_kernel, (s.table, packs[0], *got), [((HEADS, s.qkv_tall, 2 * HD), BF)])
    first = stack([norm_in, a1, b1, a2, b2])
    ups = [after(up, a2) for up in up_b]
    a3, b3, packed_x, *got = meet(ahead(a2), behind(b2), swap(packed, "x"), *near(ups))
    ups = mix([ups[0], *got])
    a4, up_z, first, down_x = meet(
        ahead(a3), swap(ups[1], "zl"), swap(after(first, a3), "c"), swap(after(down_b, a3), "x")
    )
    second = stack([a3, b3])
    (up_t,) = call(join_kernel, (s.table, ups[0], up_z, down_b), [((TEAM * s.wrows, s.cols), BF)])
    pieces = [norm_in, a1, b1, a2, b2, a3, b3, a4]
    others = [first, *meet(swap(second, "c"), swap(a4[None], "c"))]

    out = after(out_b, a4)
    out_z = [lax.ppermute(out, ("zh", "zl"), apart(4, at)) for at in range(1, 4)]
    up_z = swap(after(up_t, a4), "zh")
    grad = after(s.grad, a4)
    grad_z = swap(grad, "zl")
    att, w_head, kept = s.forward(pieces, others, [packed, packed_x])
    *att, grad_z, up_z, o1, o2, o3 = meet(*att, grad_z, up_z, *out_z)
    out_4 = stack([out, o1, o2, o3])
    grad_2 = stack([grad, grad_z])
    *got, out_x, out_y, down_z = meet(
        *near(att), swap(out_4, "x"), swap(out_4, "y"), swap(after(down_b, att[0]), "zh")
    )
    att = mix([att[0], *got])
    out_12 = stack([out_4, out_x, out_y])
    *got, o1, o2, out_12c, up_x = meet(
        *far(att),
        swap(after(out_y[:2], att[0]), "x"),
        swap(after(out_x[2:], att[0]), "y"),
        swap(out_12, "c"),
        swap(after(up_t, att[0]), "x"),
    )
    out_xy = stack([o1, o2])
    grad_2y, out_xyc = swap(after(grad_2, out_xy), "y"), swap(out_xy, "c")
    attended, mid, norm_mid, w_out = s.middle([out_12, out_xy, out_12c, out_xyc], [att[0], *got])

    half = s.half
    by_z, by_y, up_zx, grad_2y = meet(
        swap(norm_mid, "zl"), swap(norm_mid, "y"), swap(after(up_z, norm_mid), "x"), grad_2y
    )
    three = stack([norm_mid, by_z, by_y])
    grad_4 = stack([grad_2, grad_2y])
    both_one, both_two, three, down_zx, grad_4c = meet(
        swap(by_y[:half], "zl"), swap(by_z[half:], "y"), swap(three, "c"), swap(after(down_z, by_z), "x"), swap(grad_4, "c")
    )
    both = stack([both_one, both_two])
    mids = [norm_mid, by_z, by_y, both_one, both_two, three, swap(both, "c")]
    mate_1 = swap(after(w_head[0], both_one), "zh")
    lay_keep, lay_send, keep, send, mids, acts, delta, grads = s.feed(
        [grad_4, grad_4c], mids, [up_t, up_z, up_x, up_zx, down_b, down_z, down_x, down_zx]
    )
    send, mate_1 = meet(send, mate_1)
    got = swap(send, "c")
    send_z, send_y, top, low = spread(s.table, keep, got)
    up_parts = s.up_gradient(mids, after(delta, send_z))
    got_z, got_y, *up_parts = meet(swap(send_z, "zl"), swap(send_y, "y"), *up_parts)
    send_y, send_z, top, low = narrow(s.table, top, got_z, low, got_y)
    down_parts = s.down_gradient(after(acts, send_y), grads)
    end_top, end_low, up_far, *down_parts = meet(
        swap(send_y, "y"), swap(send_z, "zl"), swap(after(up_parts[3], send_y), "x"), *down_parts
    )
    mid_delta, mid_delta_b, by_head = s.turn(mid, w_out, (top, end_top, low, end_low))
    *got, up_near, mate_2 = meet(
        *near(by_head),
        swap(after(up_parts[2], mid_delta), "x"),
        swap(after(w_head[1], mid_delta), "zh"),
    )
    by_head = mix([by_head[0], *got])
    up_shape = (TEAM, s.up_tall, s.cols)
    (up_send,) = call(up_add_kernel, (up_parts[1], after(up_far, by_head[0])), [(up_shape, BF)], smem=0)
    keep, send = s.out_gradient(after(lay_keep, by_head[0]), lay_send, attended, mid_delta_b)
    *got, send, down_far, up_send = meet(
        *far(by_head), swap(send, "c"), swap(after(down_parts[3], by_head[0]), "x"), up_send
    )

    douts = [array[None] for array in (by_head[0], *got)]
    send_z, send_y, top, low = spread(s.table, keep, send)
    got_z, got_y = swap(send_z, "zl"), swap(send_y, "y")
    up_got = swap(up_send, "zh")
    down_near = swap(after(down_parts[2], send), "x")
    kept = (after(kept[0], send_z), *kept[1:])
    to_own, to_mate, by_shard, sums = s.backward(kept, douts)
    to_own, to_mate, got_z, got_y, up_got, down_near = meet(to_own, to_mate, got_z, got_y, up_got, down_near)
    send_y, send_z, top, low = narrow(s.table, top, got_z, low, got_y)
    from_mate = swap(to_mate, "zh")
    (up_keep,) = call(up_add_kernel, (up_parts[0], after(up_near, to_own)), [(up_shape, BF)], smem=0)
    ups = s.up_share(up_keep, up_got)
    qkv_own, qkv_send = s.qkv_gradient(pieces, others, after(by_shard, ups[0]), sums)
    end_top, end_low, qkv_send, *got = meet(
        swap(send_y, "y"), swap(send_z, "zl"), qkv_send, *near(ups)
    )
    ups = mix([ups[0], *got])
    layer_out, *outs = s.outputs(mid, (top, end_top, low, end_low))
    down_keep = add(down_parts[0], after(down_near, end_top), F32)
    down_send = add(down_parts[1], after(down_far, end_top), BF)
    from_mate, qkv_got, ups_z, down_send, layer_out = meet(
        from_mate, swap(after(qkv_send, end_top), "x"), swap(ups[1], "zl"), down_send, layer_out
    )
    keep, send = s.inputs(to_own, from_mate, w_head, [mate_1, mate_2])
    qkv = s.qkv_share(qkv_own, qkv_got)

    down_got = swap(after(down_send, send), "zh")
    send, out_near, out_far, *qkv = meet(
        swap(send, "c"), swap(after(outs[2], send), "x"), swap(after(outs[3], send), "x"), *qkv
    )
    send_z, send_y, top, low = spread(s.table, keep, send)
    out_keep, out_send = add(outs[0], after(out_near, send_z), F32), add(outs[1], after(out_far, send_z), BF)
    got_z, got_y, out_send, *got = meet(
        swap(send_z, "zl"), swap(send_y, "y"), out_send, *near([after(a, send_z) for a in qkv])
    )
    send_y, send_z, top, low = narrow(s.table, top, got_z, low, got_y)
    qkv = mix([after(qkv[0], send_y), *got])
    up = s.up_end((after(ups[0], send_y), ups_z))
    end_top, end_low, down_got, up_grad, *got = meet(
        swap(send_y, "y"), swap(send_z, "zl"), down_got, up[0], *far(qkv)
    )
    out_got = swap(after(out_send, end_top), "zh")
    grad_in = s.last((top, end_top, low, end_low), mid_delta)
    down = add(down_keep, down_got, F32)
    end = s.qkv_end([qkv[0], *got])
    out = add(out_keep, out_got, F32)
    return results(layer_out, grad_in, end, out, (up_grad, *up[1:]), down)


def local_any(*arrays, sizes):
    s = Steps(arrays, sizes)
    repeats, wide = s.repeats, s.wide
    long = 4 * repeats
    right, left = ring_moves(long)
    norm_in, by_head, out_b, up_b, down_b = s.first()
    one = two = norm_in
    pieces = [norm_in]
    for hop in range(1, long + 1):
        one = lax.ppermute(one, CHIPS, right)
        pieces.append(one)
        if hop < long:
            two = lax.ppermute(two, CHIPS, left)
            pieces.append(two)
    others = [swap(piece[None], "c") for piece in pieces]

    def by_parts(arrays):
        return [lax.all_gather(array, "r", axis=0, tiled=False) for array in arrays]

    def share(arrays):
        got = mix([arrays[0], *near(arrays)])
        return [got[0], *far(got)]

    def team_gather(array):
        half = array.shape[0] // 2
        by_z, by_y = swap(array, "zl"), swap(array, "y")
        chip = [array, by_z, by_y, swap(by_y[:half], "zl"), swap(by_z[half:], "y")]
        return chip + [swap(piece, "c") for piece in chip]

    def team_scatter(keep, send):
        send_z, send_y, top, low = spread(s.table, keep, swap(send, "c"))
        send_y, send_z, top, low = narrow(s.table, top, swap(send_z, "zl"), low, swap(send_y, "y"))
        return top, swap(send_y, "y"), low, swap(send_z, "zl")

    def to_owners(parts):
        array = jnp.stack(parts).reshape((wide, s.highs) + parts[0].shape).swapaxes(0, 1)
        array = array.reshape((wide * s.highs,) + parts[0].shape)
        return jnp.sum(lax.all_to_all(array, GROUP, 0, 0, tiled=True).astype(F32), axis=0)

    packs = share(by_head)
    (packed,) = call(settle_kernel, (s.table, *packs), [((HEADS, s.qkv_tall, 2 * HD), BF)])
    packed = lax.all_gather(packed, "r", axis=0, tiled=True)
    packs = [packed, *lax.all_gather(packed, "x", axis=0, tiled=False)]
    if wide == 2:
        packs = [packed, swap(packed, "x")]
    ups = mix([up_b[0], *near(up_b)])
    up_t = call(
        join_kernel, (s.table, ups[0], swap(ups[1], "zl"), down_b), [((TEAM * s.wrows, s.cols), BF)]
    )[0]
    weights = [lax.all_gather(array, GROUP, axis=0, tiled=False) for array in (up_t, down_b)]
    att, w_head, kept = s.forward(pieces, others, packs)

    def mine(arrays):
        return share(arrays)

    w_out = lax.all_gather(out_b, ALL, axis=0, tiled=True)
    attended, mid, norm_mid, w_out = s.middle([w_out], mine(att))
    lay_keep, lay_send, keep, send, mids, acts, delta, grads = s.feed(
        team_gather(s.grad), team_gather(norm_mid), weights
    )
    mid_delta, mid_delta_b, by_head = s.turn(mid, w_out, team_scatter(keep, send))
    up = to_owners(s.up_gradient(mids, delta)).astype(BF)
    down = to_owners(s.down_gradient(acts, grads))
    to_own, to_mate, by_shard, sums = s.backward(kept, by_parts(share(by_head)))
    layer_out, *outs = s.outputs(
        mid, team_scatter(*s.out_gradient(lay_keep, lay_send, attended, mid_delta_b))
    )
    keep, send = s.inputs(to_own, swap(to_mate, "zh"), w_head, [swap(array, "zh") for array in w_head])
    grad_in = s.last(team_scatter(keep, send), mid_delta)
    parts = s.qkv_gradient(pieces, others, by_shard, sums)
    own, *got = list(lax.all_to_all(jnp.stack(parts), "x", 0, 0, tiled=True))
    while len(got) > 1:
        own, got = own.astype(F32) + got[0].astype(F32), got[1:]
    ups = s.up_share(up, jnp.zeros_like(up))
    ups = mix([ups[0], *near(ups)])
    return results(
        layer_out,
        grad_in,
        s.qkv_end(share(s.qkv_share(own, got[0]))),
        to_owners(outs),
        s.up_end((ups[0], swap(ups[1], "zl"))),
        down,
    )


def solution(mesh):
    ctx, wide = mesh.shape["ctx"], mesh.shape["wt"]
    sizes = {"r": ctx // HEADS, "zh": 2, "zl": 2, "y": 2, "c": 2, "x": wide}
    grid = Mesh(mesh.devices.reshape(tuple(sizes.values())), ALL)
    tokens, weights = P("x", CTX, None), P(ALL, None)
    return jax.shard_map(
        partial(local if sizes["r"] == 1 and wide == 2 else local_any, sizes=sizes),
        mesh=grid,
        in_specs=(tokens, P("x", CTX)) + (weights,) * 4 + (P(),) * 4 + (tokens,),
        out_specs=(tokens, tokens) + (weights,) * 4 + (P(ALL),) * 4,
        check_vma=False,
    )
```

profile of v0, /device:TPU:0, one launch (start us, length us, event | category | flops | bytes accessed | tf_op | source)
XLA Modules:
  0.0 284.3 jit_solution(12765757802285508785)
XLA Ops:
  1.2 3.3 %shard_map.186 = (bf16[128,1024]{1,0:T(8,128)(2,1)}, bf16[4,56,128]{2,1,0:T(8,128)(2,1)}, bf16[4,56,128]{2,1,0:T(8,128)(2,1)}, bf16[4,56,128]{2,1,0:T(8,128)(2,1...) custom-call(s32[6]{0:T(128)} %stack.24.table._, ...), custom_call_target="tpu_custom_call" | custom-call | flops 1000 | bytes 1024 | tf_op jit(solution)/shard_map/pallas_call | solution.py:95
  4.6 3.1 %collective-permute-start = (bf16[128,1024]{1,0:T(8,128)(2,1)}, bf16[128,1024]{1,0:T(8,128)(2,1)S(1)}, u32[]{:S(2)}, u32[]{:S(2)}) collective-permute-start(bf16[128,1024]{1,0:T(8,128)(2,1)} %get-tuple-element.292.refs_0_), channel_id=1, source_target_pairs={{0,8},{8,16},{16,24},{24,28},{28,20},{20,12},{12,4},{4,0},{1,9},{9... | collective-permute-start | bytes 786440 | tf_op jit(solution)/shard_map/ppermute | solution.py:1079
  9.8 6.2 %collective-permute-done.3.refs_2_ = bf16[4,56,128]{2,1,0:T(8,128)(2,1)S(1)} collective-permute-done((bf16[4,56,128]{2,1,0:T(8,128)(2,1)}, bf16[4,56,128]{2,1,0:T(8,128)(2,1)S(1)}, u32[]{:S(2)}, u32[]{:S(2)}) %collective-permute-start.3) | collective-permute-done | bytes 57376 | tf_op jit(solution)/shard_map/ppermute | solution.py:810
  20.2 4.5 %collective-permute-start.8 = (bf16[4,56,128]{2,1,0:T(8,128)(2,1)S(1)}, bf16[4,56,128]{2,1,0:T(8,128)(2,1)S(1)}, u32[]{:S(2)}, u32[]{:S(2)}) collective-permute-start(bf16[4,56,128]{2,1,0:T(8,128)(2,1)S(1)} %get-tuple-element.303), channel_id=1, source_target_pairs={{0,16},{8,24},{16,0},{24,8},{1,17},{9,25},{17,1},{25,9},{2,18},{10... | collective-permute-start | bytes 172040 | tf_op jit(solution)/shard_map/ppermute | solution.py:814
  25.9 4.3 %collective-permute-done.8.refs_2_ = bf16[4,56,128]{2,1,0:T(8,128)(2,1)S(1)} collective-permute-done((bf16[4,56,128]{2,1,0:T(8,128)(2,1)S(1)}, bf16[4,56,128]{2,1,0:T(8,128)(2,1)S(1)}, u32[]{:S(2)}, u32[]{:S(2)}) %collective-permute-start.8) | collective-permute-done | bytes 57376 | tf_op jit(solution)/shard_map/ppermute | solution.py:814
  44.7 7.8 %collective-permute-done.17.two_ref = bf16[4,32,512]{2,1,0:T(8,128)(2,1)S(1)} collective-permute-done((bf16[4,32,512]{2,1,0:T(8,128)(2,1)S(1)}, bf16[4,32,512]{2,1,0:T(8,128)(2,1)S(1)}, u32[]{:S(2)}, u32[]{:S(2)}) %collective-permute-start.17) | collective-permute-done | bytes 131104 | tf_op jit(solution)/shard_map/ppermute | solution.py:818
  61.2 14.3 %shard_map.192 = (bf16[4,64,128]{2,1,0:T(8,128)(2,1)S(1)}, bf16[4,64,128]{2,1,0:T(8,128)(2,1)S(1)}, bf16[4,64,128]{2,1,0:T(8,128)(2,1)S(1)}, bf16[4,64,128]{2,1,...) custom-call(s32[6]{0:T(128)S(1)} %copy-done.6, ...), custom_call_target="tpu_custom_call" | custom-call | flops 14000001024 | bytes 1024 | tf_op jit(solution)/shard_map/pallas_call | solution.py:95
  81.9 4.7 %collective-permute-done.28.refs_2_ = bf16[4,64,128]{2,1,0:T(8,128)(2,1)S(1)} collective-permute-done((bf16[4,64,128]{2,1,0:T(8,128)(2,1)S(1)}, bf16[4,64,128]{2,1,0:T(8,128)(2,1)S(1)}, u32[]{:S(2)}, u32[]{:S(2)}) %collective-permute-start.28) | collective-permute-done | bytes 65568 | tf_op jit(solution)/shard_map/ppermute | solution.py:810
  86.6 5.4 %collective-permute-done.32.refs_14_ = bf16[256,512]{1,0:T(8,128)(2,1)S(1)} collective-permute-done((bf16[256,512]{1,0:T(8,128)(2,1)S(1)}, bf16[256,512]{1,0:T(8,128)(2,1)S(1)}, u32[]{:S(2)}, u32[]{:S(2)}) %collective-permute-start.32) | collective-permute-done | bytes 262176 | tf_op jit(solution)/shard_map/ppermute | solution.py:818
  92.8 3.1 %collective-permute-start.34 = (bf16[4,64,128]{2,1,0:T(8,128)(2,1)S(1)}, bf16[4,64,128]{2,1,0:T(8,128)(2,1)S(1)}, u32[]{:S(2)}, u32[]{:S(2)}) collective-permute-start(bf16[4,64,128]{2,1,0:T(8,128)(2,1)S(1)} %get-tuple-element.359), channel_id=1, source_target_pairs={{0,16},{8,24},{16,0},{24,8},{1,17},{9,25},{17,1},{25,9},{2,18},{10... | collective-permute-start | bytes 196616 | tf_op jit(solution)/shard_map/ppermute | solution.py:814
  101.1 4.4 %collective-permute-done.35.refs_7_ = bf16[4,64,128]{2,1,0:T(8,128)(2,1)S(1)} collective-permute-done((bf16[4,64,128]{2,1,0:T(8,128)(2,1)S(1)}, bf16[4,64,128]{2,1,0:T(8,128)(2,1)S(1)}, u32[]{:S(2)}, u32[]{:S(2)}) %collective-permute-start.35) | collective-permute-done | bytes 65568 | tf_op jit(solution)/shard_map/ppermute | solution.py:814
  111.0 9.5 %collective-permute-done.44.refs_1_ = bf16[2,128,1024]{2,1,0:T(8,128)(2,1)S(1)} collective-permute-done((bf16[2,128,1024]{2,1,0:T(8,128)(2,1)S(1)}, bf16[2,128,1024]{2,1,0:T(8,128)(2,1)S(1)}, u32[]{:S(2)}, u32[]{:S(2)}) %collective-permute-start.44) | collective-permute-done | bytes 524320 | tf_op jit(solution)/shard_map/ppermute | solution.py:818
  120.5 5.2 %collective-permute-done.42.refs_2_.refs_4_ = bf16[128,1024]{1,0:T(8,128)(2,1)S(1)} collective-permute-done((bf16[128,1024]{1,0:T(8,128)(2,1)S(1)}, bf16[128,1024]{1,0:T(8,128)(2,1)S(1)}, u32[]{:S(2)}, u32[]{:S(2)}) %collective-permute-start.42) | collective-permute-done | bytes 262176 | tf_op jit(solution)/shard_map/ppermute | solution.py:818
  128.9 4.4 %collective-permute-done.45.refs_0_.refs_5_ = bf16[64,1024]{1,0:T(8,128)(2,1)S(1)} collective-permute-done((bf16[64,1024]{1,0:T(8,128)(2,1)S(1)}, bf16[64,1024]{1,0:T(8,128)(2,1)S(1)}, u32[]{:S(2)}, u32[]{:S(2)}) %collective-permute-start.45) | collective-permute-done | bytes 131104 | tf_op jit(solution)/shard_map/ppermute | solution.py:818
  136.4 6.2 %shard_map.203 = (bf16[512,1024]{1,0:T(8,128)(2,1)S(1)}, bf16[512,1024]{1,0:T(8,128)(2,1)S(1)}, f32[512,1024]{1,0:T(8,128)S(1)}, bf16[512,1024]{1,0:T(8,128)(2,1...) custom-call(s32[6]{0:T(128)S(1)} %copy-done.6, ...), custom_call_target="tpu_custom_call" | custom-call | flops 6000001024 | bytes 1024 | tf_op jit(solution)/shard_map/pallas_call | solution.py:95
  142.7 7.2 %collective-permute-done.51.refs_2_ = bf16[512,192]{1,0:T(8,128)(2,1)S(1)} collective-permute-done((bf16[512,192]{1,0:T(8,128)(2,1)S(1)}, bf16[512,192]{1,0:T(8,128)(2,1)S(1)}, u32[]{:S(2)}, u32[]{:S(2)}) %collective-permute-start.51) | collective-permute-done | bytes 196640 | tf_op jit(solution)/shard_map/ppermute | solution.py:818
  156.3 5.4 %collective-permute-done.53.got_z = bf16[2,64,1024]{2,1,0:T(8,128)(2,1)S(1)} collective-permute-done((bf16[2,64,1024]{2,1,0:T(8,128)(2,1)S(1)}, bf16[2,64,1024]{2,1,0:T(8,128)(2,1)S(1)}, u32[]{:S(2)}, u32[]{:S(2)}) %collective-permute-start.53) | collective-permute-done | bytes 262176 | tf_op jit(solution)/shard_map/ppermute | solution.py:818
  168.4 4.6 %collective-permute-done.57.got_ref = bf16[8,40,512]{2,1,0:T(8,128)(2,1)S(1)} collective-permute-done((bf16[8,40,512]{2,1,0:T(8,128)(2,1)S(1)}, bf16[8,40,512]{2,1,0:T(8,128)(2,1)S(1)}, u32[]{:S(2)}, u32[]{:S(2)}) %collective-permute-start.57) | collective-permute-done | bytes 327712 | tf_op jit(solution)/shard_map/ppermute | solution.py:818
  179.0 3.0 %collective-permute-done.59.refs_2_ = bf16[4,64,128]{2,1,0:T(8,128)(2,1)S(1)} collective-permute-done((bf16[4,64,128]{2,1,0:T(8,128)(2,1)S(1)}, bf16[4,64,128]{2,1,0:T(8,128)(2,1)S(1)}, u32[]{:S(2)}, u32[]{:S(2)}) %collective-permute-start.59) | collective-permute-done | bytes 65568 | tf_op jit(solution)/shard_map/ppermute | solution.py:810
  182.7 5.8 %collective-permute-done.62.refs_3_ = bf16[512,192]{1,0:T(8,128)(2,1)S(1)} collective-permute-done((bf16[512,192]{1,0:T(8,128)(2,1)S(1)}, bf16[512,192]{1,0:T(8,128)(2,1)S(1)}, u32[]{:S(2)}, u32[]{:S(2)}) %collective-permute-start.62) | collective-permute-done | bytes 196640 | tf_op jit(solution)/shard_map/ppermute | solution.py:818
  190.7 2.9 %collective-permute-start.64 = (bf16[4,64,128]{2,1,0:T(8,128)(2,1)S(1)}, bf16[4,64,128]{2,1,0:T(8,128)(2,1)S(1)}, u32[]{:S(2)}, u32[]{:S(2)}) collective-permute-start(bf16[4,64,128]{2,1,0:T(8,128)(2,1)S(1)} %get-tuple-element.443), channel_id=1, source_target_pairs={{0,16},{8,24},{16,0},{24,8},{1,17},{9,25},{17,1},{25,9},{2,18},{10... | collective-permute-start | bytes 196616 | tf_op jit(solution)/shard_map/ppermute | solution.py:814
  205.1 12.1 %shard_map.213 = (bf16[8,192,128]{2,1,0:T(8,128)(2,1)S(1)}, bf16[8,192,128]{2,1,0:T(8,128)(2,1)S(1)}, bf16[16,128,192]{2,1,0:T(8,128)(2,1)S(1)}, f32[1,192]{1,0:T(1,128)S(1)}) custom-call(s32[6]{0:T(128)S(1)} %copy-done.6, s32[8]{0:T(128)S(1)} %get-tuple-element.453.lo_ref, bf16[1,4,64,128]{3,2,1,0:T(8,128)(2,1)S(1)} %bitcast.43, ...), custom_call_target="tpu_custom_call" | custom-call | flops 12000001024 | bytes 1024 | tf_op jit(solution)/shard_map/pallas_call | solution.py:95
  235.9 9.3 %collective-permute-done.72.got_ref = bf16[8,192,128]{2,1,0:T(8,128)(2,1)S(1)} collective-permute-done((bf16[8,192,128]{2,1,0:T(8,128)(2,1)S(1)}, bf16[8,192,128]{2,1,0:T(8,128)(2,1)S(1)}, u32[]{:S(2)}, u32[]{:S(2)}) %collective-permute-start.72) | collective-permute-done | bytes 393248 | tf_op jit(solution)/shard_map/ppermute | solution.py:818
  260.3 3.9 %collective-permute-done.86.refs_2_ = bf16[4,56,128]{2,1,0:T(8,128)(2,1)S(1)} collective-permute-done((bf16[4,56,128]{2,1,0:T(8,128)(2,1)S(1)}, bf16[4,56,128]{2,1,0:T(8,128)(2,1)S(1)}, u32[]{:S(2)}, u32[]{:S(2)}) %collective-permute-start.86) | collective-permute-done | bytes 57376 | tf_op jit(solution)/shard_map/ppermute | solution.py:810
  (251 shorter events, 142.4 us)
Async XLA Ops:
  16.0 17.1 %collective-permute-start.5 = (bf16[128,1024]{1,0:T(8,128)(2,1)S(1)}, bf16[128,1024]{1,0:T(8,128)(2,1)S(1)}, u32[]{:S(2)}, u32[]{:S(2)}) collective-permute-start(bf16[128,1024]{1,0:T(8,128)(2,1)S(1)} %collective-permute-done.refs_1_), channel_id=1, source_target_pairs={{0,8},{8,16},{16,24},{24,28},{28,20},{20,12},{12,4},{4,0},{1,9},{9... | collective-permute-start | bytes 786440 | tf_op jit(solution)/shard_map/ppermute | solution.py:1079
  17.2 15.9 %collective-permute-start.6 = (bf16[128,1024]{1,0:T(8,128)(2,1)S(1)}, bf16[128,1024]{1,0:T(8,128)(2,1)S(1)}, u32[]{:S(2)}, u32[]{:S(2)}) collective-permute-start(bf16[128,1024]{1,0:T(8,128)(2,1)S(1)} %collective-permute-done.1.refs_2_), channel_id=1, source_target_pairs={{8,0},{16,8},{24,16},{28,24},{20,28},{12,20},{4,12},{0,4},{9,1},{1... | collective-permute-start | bytes 786440 | tf_op jit(solution)/shard_map/ppermute | solution.py:1082
  44.5 13.7 %collective-permute-start.20 = (bf16[2,128,1024]{2,1,0:T(8,128)(2,1)S(1)}, bf16[2,128,1024]{2,1,0:T(8,128)(2,1)S(1)}, u32[]{:S(2)}, u32[]{:S(2)}) collective-permute-start(bf16[2,128,1024]{2,1,0:T(8,128)(2,1)S(1)} %shard_map.191), channel_id=1, source_target_pairs={{0,2},{2,0},{1,3},{3,1},{4,6},{6,4},{5,7},{7,5},{8,10},{10,8},{9,1... | collective-permute-start | bytes 1572872 | tf_op jit(solution)/shard_map/ppermute | solution.py:818
  52.7 22.8 %collective-permute-start.24 = (bf16[32,1024]{1,0:T(8,128)(2,1)S(1)}, bf16[32,1024]{1,0:T(8,128)(2,1)S(1)}, u32[]{:S(2)}, u32[]{:S(2)}) collective-permute-start(bf16[32,1024]{1,0:T(8,128)(2,1)S(1)} %copy-done.9), channel_id=1, source_target_pairs={{0,8},{8,0},{16,24},{24,16},{1,9},{9,1},{17,25},{25,17},{2,10},{10... | collective-permute-start | bytes 196616 | tf_op jit(solution)/shard_map/ppermute | solution.py:1102
  55.2 20.3 %collective-permute-start.25 = (bf16[32,1024]{1,0:T(8,128)(2,1)S(1)}, bf16[32,1024]{1,0:T(8,128)(2,1)S(1)}, u32[]{:S(2)}, u32[]{:S(2)}) collective-permute-start(bf16[32,1024]{1,0:T(8,128)(2,1)S(1)} %copy-done.9), channel_id=1, source_target_pairs={{0,16},{8,24},{16,0},{24,8},{1,17},{9,25},{17,1},{25,9},{2,18},{10... | collective-permute-start | bytes 196616 | tf_op jit(solution)/shard_map/ppermute | solution.py:1102
  56.1 19.4 %collective-permute-start.26 = (bf16[32,1024]{1,0:T(8,128)(2,1)S(1)}, bf16[32,1024]{1,0:T(8,128)(2,1)S(1)}, u32[]{:S(2)}, u32[]{:S(2)}) collective-permute-start(bf16[32,1024]{1,0:T(8,128)(2,1)S(1)} %copy-done.9), channel_id=1, source_target_pairs={{0,24},{8,16},{16,8},{24,0},{1,25},{9,17},{17,9},{25,1},{2,26},{10... | collective-permute-start | bytes 196616 | tf_op jit(solution)/shard_map/ppermute | solution.py:1102
  58.2 17.3 %collective-permute-start.22 = (bf16[128,1024]{1,0:T(8,128)(2,1)S(1)}, bf16[128,1024]{1,0:T(8,128)(2,1)S(1)}, u32[]{:S(2)}, u32[]{:S(2)}) collective-permute-start(bf16[128,1024]{1,0:T(8,128)(2,1)S(1)} %bitcast.29), channel_id=1, source_target_pairs={{0,8},{8,0},{1,9},{9,1},{2,10},{10,2},{3,11},{11,3},{4,12},{12,4},... | collective-permute-start | bytes 786440 | tf_op jit(solution)/shard_map/ppermute | solution.py:818
  59.4 16.1 %collective-permute-start.23 = (bf16[256,512]{1,0:T(8,128)(2,1)S(1)}, bf16[256,512]{1,0:T(8,128)(2,1)S(1)}, u32[]{:S(2)}, u32[]{:S(2)}) collective-permute-start(bf16[256,512]{1,0:T(8,128)(2,1)S(1)} %shard_map.193.refs_9_), channel_id=1, source_target_pairs={{0,16},{16,0},{1,17},{17,1},{2,18},{18,2},{3,19},{19,3},{4,20},{20... | collective-permute-start | bytes 786440 | tf_op jit(solution)/shard_map/ppermute | solution.py:818
  78.4 13.6 %collective-permute-start.32 = (bf16[256,512]{1,0:T(8,128)(2,1)S(1)}, bf16[256,512]{1,0:T(8,128)(2,1)S(1)}, u32[]{:S(2)}, u32[]{:S(2)}) collective-permute-start(bf16[256,512]{1,0:T(8,128)(2,1)S(1)} %copy-done.7), channel_id=1, source_target_pairs={{0,16},{16,0},{1,17},{17,1},{2,18},{18,2},{3,19},{19,3},{4,20},{20... | collective-permute-start | bytes 786440 | tf_op jit(solution)/shard_map/ppermute | solution.py:818
  92.0 13.5 %collective-permute-start.38 = (bf16[12,32,1024]{2,1,0:T(8,128)(2,1)S(1)}, bf16[12,32,1024]{2,1,0:T(8,128)(2,1)S(1)}, u32[]{:S(2)}, u32[]{:S(2)}) collective-permute-start(bf16[12,32,1024]{2,1,0:T(8,128)(2,1)S(1)} %shard_map.196.refs_0_), channel_id=1, source_target_pairs={{0,2},{2,0},{1,3},{3,1},{4,6},{6,4},{5,7},{7,5},{8,10},{10,8},{9,1... | collective-permute-start | bytes 2359304 | tf_op jit(solution)/shard_map/ppermute | solution.py:818
  92.2 13.4 %collective-permute-start.39 = (bf16[256,512]{1,0:T(8,128)(2,1)S(1)}, bf16[256,512]{1,0:T(8,128)(2,1)S(1)}, u32[]{:S(2)}, u32[]{:S(2)}) collective-permute-start(bf16[256,512]{1,0:T(8,128)(2,1)S(1)} %shard_map.193.refs_9_), channel_id=1, source_target_pairs={{0,1},{1,0},{2,3},{3,2},{4,5},{5,4},{6,7},{7,6},{8,9},{9,8},{10,11... | collective-permute-start | bytes 786440 | tf_op jit(solution)/shard_map/ppermute | solution.py:818
  105.7 14.8 %collective-permute-start.44 = (bf16[2,128,1024]{2,1,0:T(8,128)(2,1)S(1)}, bf16[2,128,1024]{2,1,0:T(8,128)(2,1)S(1)}, u32[]{:S(2)}, u32[]{:S(2)}) collective-permute-start(bf16[2,128,1024]{2,1,0:T(8,128)(2,1)S(1)} %shard_map.194.refs_0_), channel_id=1, source_target_pairs={{0,4},{4,0},{1,5},{5,1},{2,6},{6,2},{3,7},{7,3},{8,12},{12,8},{9,1... | collective-permute-start | bytes 1572872 | tf_op jit(solution)/shard_map/ppermute | solution.py:818
  108.7 17.0 %collective-permute-start.42 = (bf16[128,1024]{1,0:T(8,128)(2,1)S(1)}, bf16[128,1024]{1,0:T(8,128)(2,1)S(1)}, u32[]{:S(2)}, u32[]{:S(2)}) collective-permute-start(bf16[128,1024]{1,0:T(8,128)(2,1)S(1)} %get-tuple-element.371.refs_0_.refs_2_), channel_id=1, source_target_pairs={{0,4},{4,0},{1,5},{5,1},{2,6},{6,2},{3,7},{7,3},{8,12},{12,8},{9,1... | collective-permute-start | bytes 786440 | tf_op jit(solution)/shard_map/ppermute | solution.py:818
  109.5 16.2 %collective-permute-start.43 = (bf16[256,512]{1,0:T(8,128)(2,1)S(1)}, bf16[256,512]{1,0:T(8,128)(2,1)S(1)}, u32[]{:S(2)}, u32[]{:S(2)}) collective-permute-start(bf16[256,512]{1,0:T(8,128)(2,1)S(1)} %collective-permute-done.23.refs_10_), channel_id=1, source_target_pairs={{0,1},{1,0},{2,3},{3,2},{4,5},{5,4},{6,7},{7,6},{8,9},{9,8},{10,11... | collective-permute-start | bytes 786440 | tf_op jit(solution)/shard_map/ppermute | solution.py:818
  134.9 15.0 %collective-permute-start.51 = (bf16[512,192]{1,0:T(8,128)(2,1)S(1)}, bf16[512,192]{1,0:T(8,128)(2,1)S(1)}, u32[]{:S(2)}, u32[]{:S(2)}) collective-permute-start(bf16[512,192]{1,0:T(8,128)(2,1)S(1)} %get-tuple-element.394.refs_0_), channel_id=1, source_target_pairs={{0,16},{16,0},{1,17},{17,1},{2,18},{18,2},{3,19},{19,3},{4,20},{20... | collective-permute-start | bytes 589832 | tf_op jit(solution)/shard_map/ppermute | solution.py:818
  174.9 13.5 %collective-permute-start.61 = (bf16[8,40,512]{2,1,0:T(8,128)(2,1)S(1)}, bf16[8,40,512]{2,1,0:T(8,128)(2,1)S(1)}, u32[]{:S(2)}, u32[]{:S(2)}) collective-permute-start(bf16[8,40,512]{2,1,0:T(8,128)(2,1)S(1)} %get-tuple-element.430), channel_id=1, source_target_pairs={{0,1},{1,0},{2,3},{3,2},{4,5},{5,4},{6,7},{7,6},{8,9},{9,8},{10,11... | collective-permute-start | bytes 983048 | tf_op jit(solution)/shard_map/ppermute | solution.py:818
  200.9 19.6 %collective-permute-start.68 = (bf16[2,128,1024]{2,1,0:T(8,128)(2,1)S(1)}, bf16[2,128,1024]{2,1,0:T(8,128)(2,1)S(1)}, u32[]{:S(2)}, u32[]{:S(2)}) collective-permute-start(bf16[2,128,1024]{2,1,0:T(8,128)(2,1)S(1)} %get-tuple-element.452), channel_id=1, source_target_pairs={{0,8},{8,0},{1,9},{9,1},{2,10},{10,2},{3,11},{11,3},{4,12},{12,4},... | collective-permute-start | bytes 1572872 | tf_op jit(solution)/shard_map/ppermute | solution.py:818
  201.8 18.7 %collective-permute-start.69 = (bf16[2,128,1024]{2,1,0:T(8,128)(2,1)S(1)}, bf16[2,128,1024]{2,1,0:T(8,128)(2,1)S(1)}, u32[]{:S(2)}, u32[]{:S(2)}) collective-permute-start(bf16[2,128,1024]{2,1,0:T(8,128)(2,1)S(1)} %get-tuple-element.465), channel_id=1, source_target_pairs={{0,4},{4,0},{1,5},{5,1},{2,6},{6,2},{3,7},{7,3},{8,12},{12,8},{9,1... | collective-permute-start | bytes 1572872 | tf_op jit(solution)/shard_map/ppermute | solution.py:818
  202.9 16.3 %collective-permute-start.70 = (bf16[8,40,512]{2,1,0:T(8,128)(2,1)S(1)}, bf16[8,40,512]{2,1,0:T(8,128)(2,1)S(1)}, u32[]{:S(2)}, u32[]{:S(2)}) collective-permute-start(bf16[8,40,512]{2,1,0:T(8,128)(2,1)S(1)} %shard_map.211), channel_id=1, source_target_pairs={{0,16},{16,0},{1,17},{17,1},{2,18},{18,2},{3,19},{19,3},{4,20},{20... | collective-permute-start | bytes 983048 | tf_op jit(solution)/shard_map/ppermute | solution.py:818
  204.1 13.0 %collective-permute-start.71 = (bf16[128,1024]{1,0:T(8,128)(2,1)S(1)}, bf16[128,1024]{1,0:T(8,128)(2,1)S(1)}, u32[]{:S(2)}, u32[]{:S(2)}) collective-permute-start(bf16[128,1024]{1,0:T(8,128)(2,1)S(1)} %get-tuple-element.468), channel_id=1, source_target_pairs={{0,1},{1,0},{2,3},{3,2},{4,5},{5,4},{6,7},{7,6},{8,9},{9,8},{10,11... | collective-permute-start | bytes 786440 | tf_op jit(solution)/shard_map/ppermute | solution.py:818
  224.6 20.6 %collective-permute-start.72 = (bf16[8,192,128]{2,1,0:T(8,128)(2,1)S(1)}, bf16[8,192,128]{2,1,0:T(8,128)(2,1)S(1)}, u32[]{:S(2)}, u32[]{:S(2)}) collective-permute-start(bf16[8,192,128]{2,1,0:T(8,128)(2,1)S(1)} %get-tuple-element.469), channel_id=1, source_target_pairs={{0,16},{16,0},{1,17},{17,1},{2,18},{18,2},{3,19},{19,3},{4,20},{20... | collective-permute-start | bytes 1179656 | tf_op jit(solution)/shard_map/ppermute | solution.py:818
  231.2 14.0 %collective-permute-start.78 = (bf16[16,56,128]{2,1,0:T(8,128)(2,1)S(1)}, bf16[16,56,128]{2,1,0:T(8,128)(2,1)S(1)}, u32[]{:S(2)}, u32[]{:S(2)}) collective-permute-start(bf16[16,56,128]{2,1,0:T(8,128)(2,1)S(1)} %get-tuple-element.491), channel_id=1, source_target_pairs={{0,1},{1,0},{2,3},{3,2},{4,5},{5,4},{6,7},{7,6},{8,9},{9,8},{10,11... | collective-permute-start | bytes 688136 | tf_op jit(solution)/shard_map/ppermute | solution.py:818
  232.5 12.8 %collective-permute-start.79 = (bf16[4,40,512]{2,1,0:T(8,128)(2,1)S(1)}, bf16[4,40,512]{2,1,0:T(8,128)(2,1)S(1)}, u32[]{:S(2)}, u32[]{:S(2)}) collective-permute-start(bf16[4,40,512]{2,1,0:T(8,128)(2,1)S(1)} %get-tuple-element.495), channel_id=1, source_target_pairs={{0,8},{8,0},{1,9},{9,1},{2,10},{10,2},{3,11},{11,3},{4,12},{12,4},... | collective-permute-start | bytes 491528 | tf_op jit(solution)/shard_map/ppermute | solution.py:818
  256.3 14.5 %collective-permute-start.90 = (bf16[128,1024]{1,0:T(8,128)(2,1)S(1)}, bf16[128,1024]{1,0:T(8,128)(2,1)S(1)}, u32[]{:S(2)}, u32[]{:S(2)}) collective-permute-start(bf16[128,1024]{1,0:T(8,128)(2,1)S(1)} %shard_map.219), channel_id=1, source_target_pairs={{0,16},{16,0},{1,17},{17,1},{2,18},{18,2},{3,19},{19,3},{4,20},{20... | collective-permute-start | bytes 786440 | tf_op jit(solution)/shard_map/ppermute | solution.py:818
  (86 other events, 787.4 us)
where the time goes:
time: 284 us
  waiting for transfers between devices  126 us (44%)
  starting transfers between devices  89.8 us (32%)
  Pallas kernels  62.4 us (22%)
    ppermute x55, waiting for transfers between devices, swap(): return lax.ppermute(array, axis, SWAP)  78 us
    pallas_call x48, Pallas kernels, call(): pl.pallas_call(body, out_shape=[jax.ShapeDtypeStruct(shape, kind) for sha...  62.4 us
    ppermute x55, starting transfers between devices, swap(): return lax.ppermute(array, axis, SWAP)  49.4 us
    ppermute x18, waiting for transfers between devices, near(): lax.ppermute(arrays[at], ('y', 'c'), apart(4, at))  25.5 us
    ppermute x12, waiting for transfers between devices, far(): lax.ppermute(arrays[at], ('zh', 'zl'), apart(4, at))  22.2 us
    ppermute x12, starting transfers between devices, far(): lax.ppermute(arrays[at], ('zh', 'zl'), apart(4, at))  19.3 us
    ppermute x18, starting transfers between devices, near(): lax.ppermute(arrays[at], ('y', 'c'), apart(4, at))  8.97 us
  transfers between devices with their start and end apart: 95, of which 45 were waited for; matrix products, arithmetic and copies ran while one was open for 1% of the time, Pallas kernels for 17%

commit v1 on v0

--- a/solution.py
+++ b/solution.py
@@ -229,15 +229,18 @@
     pieces = list(pieces) + unstacked(others)
     own_ref, *refs = refs
     packs, refs = ([own_ref, refs[0]], refs[1:]) if wide == 2 else (refs[:wide], refs[wide:])
-    outs, seconds = refs[:4], refs[16:]
-    lse_ref, begin_ref, lo_ref, w_top, w_low, q_ref, k_ref, v_ref, ot_ref, vt_ref, att_ref, w_ref = refs[4:16]
+    outs, seconds = refs[:4], refs[14:]
+    lse_ref, begin_ref, w_ref, w_send, q_ref, k_ref, v_ref, ot_ref, vt_ref, att_ref = refs[4:14]
     place = Place(table)
     if wide == 2:
         in_order(place, packs, *seconds)
         packs = seconds
     head_weights(packs, w_ref, wrows, wide)
-    w_top[...] = w_ref[: w_top.shape[0], :]
-    w_low[...] = w_ref[w_top.shape[0] :, :]
+    count = w_send.shape[0]
+    if count < w_ref.shape[0]:
+        w_send[...] = w_ref[pl.ds(pl.multiple_of(place.x * count, count), count), :]
+    else:
+        w_send[...] = w_ref[...]
     shards, half, _ = att_ref.shape
     rows = 2 * half
     total = shards * rows
@@ -273,7 +276,6 @@
     for tile in range(total // TILE):
         row = jnp.concatenate([begins[tile * group + at : tile * group + at + 1] for at in range(group)], axis=1)
         begin_ref[tile : tile + 1, :] = row.astype(jnp.int32)
-        lo_ref[tile] = jnp.min(row).astype(jnp.int32) // TILE
     for which in range(2):
         for at in range(chips):
             made = dot(pieces[which * chips + at][...], w_ref[...], NN).astype(BF)
@@ -287,36 +289,27 @@
                 v_ref[pl.ds(first, half), :] = made[part, 2 * HD :]
     for at in range(0, total, 128):
         vt_ref[:, at : at + 128] = v_ref[at : at + 128, :].astype(F32).T.astype(BF)
-    for tile in range(total // TILE):
-        query = q_ref[tile * TILE : (tile + 1) * TILE, :]
-        begin = begin_ref[tile : tile + 1, :]
-        query_pos = tile * TILE + lax.broadcasted_iota(jnp.int32, (TILE, TILE), 1)
-
-        def step(at, state):
-            top, sums, accum = state
-            first = pl.multiple_of(at * TILE, TILE)
-            scores = dot(k_ref[pl.ds(first, TILE), :], query, NT)
-            key_pos = first + lax.broadcasted_iota(jnp.int32, (TILE, TILE), 0)
-            scores = jnp.where((key_pos >= begin) & (key_pos <= query_pos), scores, FAR)
-            higher = jnp.maximum(top, jnp.max(scores, axis=0, keepdims=True))
-            weights = jnp.exp(scores - higher)
-            factor = jnp.exp(top - higher)
-            sums = sums * factor + jnp.sum(weights, axis=0, keepdims=True)
-            accum = accum * factor + dot(vt_ref[:, pl.ds(first, TILE)], weights.astype(BF), NN)
-            return higher, sums, accum
-
-        top, sums, accum = lax.fori_loop(
-            lo_ref[tile],
-            tile + 1,
-            step,
-            (jnp.full((1, TILE), FAR, F32), jnp.zeros((1, TILE), F32), jnp.zeros((HD, TILE), F32)),
-        )
-        out = accum / sums
-        ot_ref[:, tile * TILE : (tile + 1) * TILE] = out
-        lse_ref[tile : tile + 1, :] = top + jnp.log(sums)
+    wide_tile = 2 * TILE
+    for tile in range(total // wide_tile):
+        low = max(0, tile - total // 2 // wide_tile) * wide_tile
+        high = (tile + 1) * wide_tile
+        query = q_ref[high - wide_tile : high, :]
+        begin = jnp.concatenate([begin_ref[2 * tile : 2 * tile + 1, :], begin_ref[2 * tile + 1 : 2 * tile + 2, :]], axis=1)
+        query_pos = high - wide_tile + lax.broadcasted_iota(jnp.int32, (1, wide_tile), 1)
+        scores = dot(k_ref[low:high, :], query, NT)
+        key_pos = low + lax.broadcasted_iota(jnp.int32, scores.shape, 0)
+        scores = jnp.where((key_pos >= begin) & (key_pos <= query_pos), scores, FAR)
+        top = jnp.max(scores, axis=0, keepdims=True)
+        weights = jnp.exp(scores - top)
+        sums = jnp.sum(weights, axis=0, keepdims=True)
+        out = dot(vt_ref[:, low:high], weights.astype(BF), NN) / sums
+        ot_ref[:, high - wide_tile : high] = out
+        lse = top + jnp.log(sums)
+        lse_ref[2 * tile : 2 * tile + 1, :] = lse[:, :TILE]
+        lse_ref[2 * tile + 1 : 2 * tile + 2, :] = lse[:, TILE:]
         turned = out.T.astype(BF)
-        for piece in range(group):
-            shard, side = block_home(tile * group + piece, shards)
+        for piece in range(2 * group):
+            shard, side = block_home(tile * 2 * group + piece, shards)
             att_ref[shard, :, side * HD : (side + 1) * HD] = turned[piece * half : (piece + 1) * half]
     for near in range(4):
         for far in range(4):
@@ -450,8 +443,7 @@
 
 
 def up_pack_kernel(table, part_ref, delta_ref, *outs, wide):
-    _, tall, _ = outs[0].shape
-    rows = tall - TAIL
+    rows = (outs[0].shape[0] - TAIL) // TEAM
     tail = sum_lines(jnp.sum(delta_ref[...].astype(F32), axis=0, keepdims=True))
     place = Place(table)
     highs = len(outs) // wide
@@ -464,8 +456,8 @@
             first = ((high * TEAM + mate) * wide + x) * rows
             if wide == 2:
                 first = pl.multiple_of(first, rows)
-            out[mate, :rows] = part_ref[pl.ds(first, rows), :].astype(BF)
-            out[mate, rows:] = tail
+            out[mate * rows : (mate + 1) * rows] = part_ref[pl.ds(first, rows), :].astype(BF)
+        out[TEAM * rows :] = tail
 
 
 def down_pack_kernel(table, part_ref, *outs, wide):
@@ -484,23 +476,27 @@
 
 
 def up_add_kernel(own_ref, got_ref, out_ref):
-    rows = out_ref.shape[1] - TAIL
-    for mate in range(TEAM):
-        out_ref[mate, :rows], out_ref[mate, rows:] = add_lines(own_ref[mate], got_ref[mate])
+    body, tail = add_lines(own_ref[...], got_ref[...])
+    out_ref[: body.shape[0]] = body
+    out_ref[body.shape[0] :] = tail
 
 
 def sum_kernel(own_ref, got_ref, out_ref):
     out_ref[...] = (own_ref[...].astype(F32) + got_ref[...].astype(F32)).astype(out_ref.dtype)
 
 
-def up_share_kernel(table, own_ref, got_ref, *outs):
-    place = Place(table)
-    rows = own_ref.shape[1] - TAIL
+def up_share_kernel(table, own_ref, got_ref, *refs):
+    *outs, all_ref = refs
+    place = Place(table)
+    rows = outs[0].shape[1] - TAIL
+    body, tail = add_lines(own_ref[...], got_ref[...])
+    for mate in range(TEAM):
+        all_ref[mate] = body[mate * rows : (mate + 1) * rows]
     for near in range(4):
         for high in range(2):
-            mate = place.mate ^ (high * 4 + near)
             out = outs[near]
-            out[high, :rows], out[high, rows:] = add_lines(own_ref[mate], got_ref[mate])
+            out[high, :rows] = all_ref[place.mate ^ (high * 4 + near)]
+            out[high, rows:] = tail
 
 
 def sum_lines(sums):
@@ -586,7 +582,7 @@
     norm_grads(place, own_ref, grad_out, sums, gain_ref, bias_ref, gain_out, bias_out, wide)
 
 
-def backward_kernel(table, lo_ref, *refs):
+def backward_kernel(table, *refs):
     douts, refs = refs[:4], refs[4:]
     (
         q_ref, k_ref, v_ref, ot_ref, lse_ref, begin_ref, own_out, mate_out, dn_ref, sum_ref,
@@ -614,22 +610,18 @@
         begin = begin_ref[tile : tile + 1, :]
         lse = lse_ref[tile : tile + 1, :]
         row_dot = jnp.sum(dout.astype(F32).T * ot_ref[:, here], axis=0, keepdims=True)
-        query_pos = tile * TILE + lax.broadcasted_iota(jnp.int32, (TILE, TILE), 1)
-
-        def step(at, accum):
-            first = pl.multiple_of(at * TILE, TILE)
-            there = pl.ds(first, TILE)
-            scores = dot(k_ref[there, :], query, NT)
-            key_pos = first + lax.broadcasted_iota(jnp.int32, (TILE, TILE), 0)
-            allowed = (key_pos >= begin) & (key_pos <= query_pos)
-            probs = jnp.where(allowed, jnp.exp(scores - lse), 0.0)
-            dprobs = dot(v_ref[there, :], dout, NT)
-            delta = (probs * (dprobs - row_dot)).astype(BF)
-            dv_ref[there, :] += dot(probs.astype(BF), dout, NN)
-            dk_ref[there, :] += dot(delta, query, NN)
-            return accum + dot(kt_ref[:, there], delta, NN)
-
-        accum = lax.fori_loop(lo_ref[tile], tile + 1, step, jnp.zeros((HD, TILE), F32))
+        query_pos = tile * TILE + lax.broadcasted_iota(jnp.int32, (1, TILE), 1)
+        low = max(0, tile - total // 2 // TILE) * TILE
+        there = slice(low, (tile + 1) * TILE)
+        scores = dot(k_ref[there, :], query, NT)
+        key_pos = low + lax.broadcasted_iota(jnp.int32, scores.shape, 0)
+        allowed = (key_pos >= begin) & (key_pos <= query_pos)
+        probs = jnp.where(allowed, jnp.exp(scores - lse), 0.0)
+        dprobs = dot(v_ref[there, :], dout, NT)
+        delta = (probs * (dprobs - row_dot)).astype(BF)
+        dv_ref[there, :] += dot(probs.astype(BF), dout, NN)
+        dk_ref[there, :] += dot(delta, query, NN)
+        accum = dot(kt_ref[:, there], delta, NN)
         dq_ref[here, :] = (accum * HD**-0.5).T
     sums = jnp.zeros((1, TRIPLE), F32)
     for block in range(2 * shards):
@@ -740,15 +732,16 @@
     rows = tall * 2 // 3
     half = rows // 2
     place = Place(table)
-    *weights, keep_out, send_out, lhs_ref, rhs_ref = refs
-    first = 0
-    for w_own, w_got in zip(weights[:2], weights[2:], strict=True):
-        here = slice(first, first + w_got.shape[0])
-        rhs_ref[here, : 2 * HD] = w_own[:, : 2 * HD]
-        rhs_ref[here, 2 * HD : 3 * HD] = w_own[:, 2 * HD :]
+    w_own, *mates, keep_out, send_out, lhs_ref, rhs_ref = refs
+    rhs_ref[:, : 2 * HD] = w_own[:, : 2 * HD]
+    rhs_ref[:, 2 * HD : 3 * HD] = w_own[:, 2 * HD :]
+    for at, w_got in enumerate(mates):
+        count = w_got.shape[0]
+        here = slice(0, count)
+        if len(mates) == 2:
+            here = pl.ds(pl.multiple_of((place.x ^ at) * count, count), count)
         rhs_ref[here, 3 * HD : 4 * HD] = w_got[:, 2 * HD :]
         rhs_ref[here, 4 * HD :] = w_got[:, : 2 * HD]
-        first += w_got.shape[0]
     for at in range(TEAM):
         mate = place.mate ^ TEAM_ORDER[at]
         first = at * rows
@@ -775,18 +768,15 @@
 
 def outs_kernel(table, mid_ref, lay_ref, got_lay, part_ref, got_part, lay_out, *outs, wide):
     lay_out[...] = (mid_ref[...] + lay_ref[...] + got_lay[...].astype(F32)).astype(BF)
-    rows = outs[0].shape[0]
-    place = Place(table)
-    highs = len(outs) // wide
-    for at, out in enumerate(outs):
-        if wide == 2:
-            x, high = place.x ^ (at >> 1), place.zh ^ (at & 1)
-        else:
-            x, high = at // highs, at % highs
-        first = (x * highs + high) * rows
-        if wide == 2:
-            first = pl.multiple_of(first, rows)
-        out[...] = (part_ref[pl.ds(first, rows), :] + got_part[pl.ds(first, rows), :].astype(F32)).astype(BF)
+    highs, rows, _ = outs[0].shape
+    place = Place(table)
+    for side, out in enumerate(outs):
+        for at in range(highs):
+            x, high = (place.x ^ side, place.zh ^ at) if wide == 2 else (side, at)
+            first = (x * highs + high) * rows
+            if wide == 2:
+                first = pl.multiple_of(first, rows)
+            out[at] = (part_ref[pl.ds(first, rows), :] + got_part[pl.ds(first, rows), :].astype(F32)).astype(BF)
 
 
 def after(array, *others):
@@ -897,25 +887,23 @@
     def forward(self, pieces, others, packs):
         tokens = ((self.total, HD), BF)
         tiles = (self.total // TILE, TILE)
-        whalf = ((self.width // 2, TRIPLE), BF)
+        sent = self.width // 2 if self.repeats == 1 and self.wide == 2 else self.width
         outs = call(
             partial(forward_kernel, wrows=self.wrows, chips=len(pieces), others=len(others), wide=self.wide),
             (self.table, *pieces, *others, *packs),
             [
                 *[self.piece] * 4,
-                (tiles, F32), (tiles, jnp.int32), (tiles[:1], jnp.int32),
-                whalf, whalf,
+                (tiles, F32), (tiles, jnp.int32),
+                ((self.width, TRIPLE), BF), ((sent, TRIPLE), BF),
                 tokens, tokens, tokens,
                 ((HD, self.total), F32),
             ],
-            [((HD, self.total), BF), ((self.shards, self.half, 2 * HD), BF), ((self.width, TRIPLE), BF)]
+            [((HD, self.total), BF), ((self.shards, self.half, 2 * HD), BF)]
             + [((self.shards, self.qkv_tall, 2 * HD), BF)] * (2 if self.wide == 2 else 0),
-            smem_outs=(6,),
-            limit=12 * self.repeats,
-            micros=14,
-        )
-        lse, begin, low = outs[4:7]
-        return list(outs[:4]), list(outs[7:9]), (low, *outs[9:], lse, begin)
+            limit=20 * self.repeats * self.repeats,
+            micros=7,
+        )
+        return list(outs[:4]), list(outs[6:8]), (*outs[8:], *outs[4:6])
 
     def middle(self, weights, heads):
         return call(
@@ -947,7 +935,7 @@
         return call(
             partial(up_pack_kernel, wide=self.wide),
             (self.table, dot(mids, delta, TN), delta),
-            [((TEAM, self.up_tall, self.cols), BF)] * self.sides,
+            [((self.width // (self.highs * self.wide) + TAIL, self.cols), BF)] * self.sides,
         )
 
     def down_gradient(self, acts, grads):
@@ -975,12 +963,12 @@
         )
 
     def backward(self, kept, douts):
-        low, query, keys, values, out_t, lse, begin = kept
+        query, keys, values, out_t, lse, begin = kept
         tall = self.rows + self.half
         total = ((self.total, HD), F32)
         return call(
             backward_kernel,
-            (self.table, low, *douts, query, keys, values, out_t, lse, begin),
+            (self.table, *douts, query, keys, values, out_t, lse, begin),
             [
                 ((TEAM, tall, 2 * HD), BF),
                 ((TEAM, tall, 2 * HD), BF),
@@ -994,9 +982,8 @@
                 total, total, total,
                 ((self.shards, tall, 2 * HD), BF),
             ],
-            smem=2,
-            limit=12 * self.repeats,
-            micros=12,
+            limit=14 * self.repeats * self.repeats,
+            micros=8,
         )
 
     def qkv_gradient(self, pieces, others, by_shard, sums):
@@ -1011,7 +998,14 @@
         )
 
     def up_share(self, own, got):
-        return list(call(up_share_kernel, (self.table, own, got), [((2, self.up_tall, self.cols), BF)] * 4))
+        return list(
+            call(
+                up_share_kernel,
+                (self.table, own, got),
+                [((2, self.up_tall, self.cols), BF)] * 4,
+                [((TEAM, self.wrows, self.cols), BF)],
+            )
+        )
 
     def qkv_share(self, own, got):
         return list(call(qkv_add_kernel, (self.table, own, got), [((4, self.qkv_tall, 2 * HD), BF)] * 4))
@@ -1020,13 +1014,13 @@
         return call(
             partial(outs_kernel, wide=self.wide),
             (self.table, mid, *ends),
-            [((self.rows, self.width), BF)] + [((self.wrows, self.width), BF)] * self.sides,
+            [((self.rows, self.width), BF)] + [((self.highs, self.wrows, self.width), BF)] * self.wide,
         )
 
     def inputs(self, to_own, from_mate, weights, mates):
         return call(
             input_kernel,
-            (self.table, to_own, from_mate, *weights, *mates),
+            (self.table, to_own, from_mate, weights, *mates),
             [((self.many // 2, self.width), F32), ((self.many // 2, self.width), BF)],
             [((self.many, 2 * TRIPLE), BF), ((self.width, 2 * TRIPLE), BF)],
         )
@@ -1100,47 +1094,47 @@
 
     out = after(out_b, a4)
     out_z = [lax.ppermute(out, ("zh", "zl"), apart(4, at)) for at in range(1, 4)]
-    up_z = swap(after(up_t, a4), "zh")
     grad = after(s.grad, a4)
     grad_z = swap(grad, "zl")
     att, w_head, kept = s.forward(pieces, others, [packed, packed_x])
-    *att, grad_z, up_z, o1, o2, o3 = meet(*att, grad_z, up_z, *out_z)
+    *att, grad_z, o1, o2, o3 = meet(*att, grad_z, *out_z)
     out_4 = stack([out, o1, o2, o3])
-    grad_2 = stack([grad, grad_z])
-    *got, out_x, out_y, down_z = meet(
-        *near(att), swap(out_4, "x"), swap(out_4, "y"), swap(after(down_b, att[0]), "zh")
+    *got, out_x, up_z, grad_y = meet(
+        *near(att), swap(out_4, "x"), swap(after(up_t, att[0]), "zh"), swap(after(grad, att[0]), "y")
     )
     att = mix([att[0], *got])
-    out_12 = stack([out_4, out_x, out_y])
-    *got, o1, o2, out_12c, up_x = meet(
-        *far(att),
-        swap(after(out_y[:2], att[0]), "x"),
-        swap(after(out_x[2:], att[0]), "y"),
-        swap(out_12, "c"),
-        swap(after(up_t, att[0]), "x"),
-    )
-    out_xy = stack([o1, o2])
-    grad_2y, out_xyc = swap(after(grad_2, out_xy), "y"), swap(out_xy, "c")
-    attended, mid, norm_mid, w_out = s.middle([out_12, out_xy, out_12c, out_xyc], [att[0], *got])
+    out_8 = stack([out_4, out_x])
+    *got, out_8y, up_x, out_8c = meet(
+        *far(att), swap(out_8, "y"), swap(after(up_t, att[0]), "x"), swap(out_8, "c")
+    )
+    attended, mid, norm_mid, w_out = s.middle([out_8, out_8y, out_8c, swap(out_8y, "c")], [att[0], *got])
 
     half = s.half
-    by_z, by_y, up_zx, grad_2y = meet(
-        swap(norm_mid, "zl"), swap(norm_mid, "y"), swap(after(up_z, norm_mid), "x"), grad_2y
+    grad_3 = stack([after(grad, norm_mid), grad_z, grad_y])
+    by_z, by_y, up_zx, down_z, grad_3c = meet(
+        swap(norm_mid, "zl"),
+        swap(norm_mid, "y"),
+        swap(after(up_z, norm_mid), "x"),
+        swap(after(down_b, norm_mid), "zh"),
+        swap(grad_3, "c"),
     )
     three = stack([norm_mid, by_z, by_y])
-    grad_4 = stack([grad_2, grad_2y])
-    both_one, both_two, three, down_zx, grad_4c = meet(
-        swap(by_y[:half], "zl"), swap(by_z[half:], "y"), swap(three, "c"), swap(after(down_z, by_z), "x"), swap(grad_4, "c")
+    both_one, both_two, three, down_zx, grad_one, grad_two = meet(
+        swap(by_y[:half], "zl"),
+        swap(by_z[half:], "y"),
+        swap(three, "c"),
+        swap(after(down_z, by_z), "x"),
+        swap(after(grad_y[:half], by_z), "zl"),
+        swap(after(grad_z[half:], by_z), "y"),
     )
     both = stack([both_one, both_two])
+    grad_both = stack([grad_one, grad_two])
     mids = [norm_mid, by_z, by_y, both_one, both_two, three, swap(both, "c")]
-    mate_1 = swap(after(w_head[0], both_one), "zh")
+    grads = [grad, grad_z, grad_y, grad_one, grad_two, grad_3c, swap(grad_both, "c")]
     lay_keep, lay_send, keep, send, mids, acts, delta, grads = s.feed(
-        [grad_4, grad_4c], mids, [up_t, up_z, up_x, up_zx, down_b, down_z, down_x, down_zx]
-    )
-    send, mate_1 = meet(send, mate_1)
-    got = swap(send, "c")
-    send_z, send_y, top, low = spread(s.table, keep, got)
+        grads, mids, [up_t, up_z, up_x, up_zx, down_b, down_z, down_x, down_zx]
+    )
+    send_z, send_y, top, low = spread(s.table, keep, swap(send, "c"))
     up_parts = s.up_gradient(mids, after(delta, send_z))
     got_z, got_y, *up_parts = meet(swap(send_z, "zl"), swap(send_y, "y"), *up_parts)
     send_y, send_z, top, low = narrow(s.table, top, got_z, low, got_y)
@@ -1149,13 +1143,13 @@
         swap(send_y, "y"), swap(send_z, "zl"), swap(after(up_parts[3], send_y), "x"), *down_parts
     )
     mid_delta, mid_delta_b, by_head = s.turn(mid, w_out, (top, end_top, low, end_low))
-    *got, up_near, mate_2 = meet(
+    *got, up_near, mate_1 = meet(
         *near(by_head),
         swap(after(up_parts[2], mid_delta), "x"),
         swap(after(w_head[1], mid_delta), "zh"),
     )
     by_head = mix([by_head[0], *got])
-    up_shape = (TEAM, s.up_tall, s.cols)
+    up_shape = up_parts[0].shape
     (up_send,) = call(up_add_kernel, (up_parts[1], after(up_far, by_head[0])), [(up_shape, BF)], smem=0)
     keep, send = s.out_gradient(after(lay_keep, by_head[0]), lay_send, attended, mid_delta_b)
     *got, send, down_far, up_send = meet(
@@ -1167,48 +1161,49 @@
     got_z, got_y = swap(send_z, "zl"), swap(send_y, "y")
     up_got = swap(up_send, "zh")
     down_near = swap(after(down_parts[2], send), "x")
+    mate_2 = swap(after(mate_1, send), "x")
     kept = (after(kept[0], send_z), *kept[1:])
     to_own, to_mate, by_shard, sums = s.backward(kept, douts)
-    to_own, to_mate, got_z, got_y, up_got, down_near = meet(to_own, to_mate, got_z, got_y, up_got, down_near)
+    from_mate = swap(to_mate, "zh")
+    to_own, got_z, got_y, down_near, mate_2 = meet(to_own, got_z, got_y, down_near, mate_2)
     send_y, send_z, top, low = narrow(s.table, top, got_z, low, got_y)
-    from_mate = swap(to_mate, "zh")
     (up_keep,) = call(up_add_kernel, (up_parts[0], after(up_near, to_own)), [(up_shape, BF)], smem=0)
+    qkv_own, qkv_send = s.qkv_gradient(pieces, others, after(by_shard, send_y), sums)
+    down_send = add(down_parts[1], after(down_far, send_y), BF)
+    end_top, end_low, qkv_send, up_got, down_send = meet(
+        swap(send_y, "y"), swap(send_z, "zl"), qkv_send, up_got, down_send
+    )
     ups = s.up_share(up_keep, up_got)
-    qkv_own, qkv_send = s.qkv_gradient(pieces, others, after(by_shard, ups[0]), sums)
-    end_top, end_low, qkv_send, *got = meet(
-        swap(send_y, "y"), swap(send_z, "zl"), qkv_send, *near(ups)
-    )
-    ups = mix([ups[0], *got])
-    layer_out, *outs = s.outputs(mid, (top, end_top, low, end_low))
+    ends = top, end_top, low, end_low
     down_keep = add(down_parts[0], after(down_near, end_top), F32)
-    down_send = add(down_parts[1], after(down_far, end_top), BF)
-    from_mate, qkv_got, ups_z, down_send, layer_out = meet(
-        from_mate, swap(after(qkv_send, end_top), "x"), swap(ups[1], "zl"), down_send, layer_out
-    )
-    keep, send = s.inputs(to_own, from_mate, w_head, [mate_1, mate_2])
-    qkv = s.qkv_share(qkv_own, qkv_got)
-
-    down_got = swap(after(down_send, send), "zh")
-    send, out_near, out_far, *qkv = meet(
-        swap(send, "c"), swap(after(outs[2], send), "x"), swap(after(outs[3], send), "x"), *qkv
-    )
+    from_mate, qkv_got, *got = meet(from_mate, swap(after(qkv_send, end_top), "x"), *near(ups))
+    keep, send = s.inputs(to_own, from_mate, w_head[0], [mate_1, mate_2])
+    layer_out, *outs = s.outputs(mid, [after(array, send) for array in ends])
+    qkv = s.qkv_share(qkv_own, after(qkv_got, send))
+    send, layer_out, *qkv = meet(swap(send, "c"), layer_out, *qkv)
+
     send_z, send_y, top, low = spread(s.table, keep, send)
-    out_keep, out_send = add(outs[0], after(out_near, send_z), F32), add(outs[1], after(out_far, send_z), BF)
-    got_z, got_y, out_send, *got = meet(
-        swap(send_z, "zl"), swap(send_y, "y"), out_send, *near([after(a, send_z) for a in qkv])
+    down_got = swap(after(down_send, send_z), "zh")
+    got_z, got_y, out_got, *more = meet(
+        swap(send_z, "zl"),
+        swap(send_y, "y"),
+        swap(after(outs[1], send_z), "x"),
+        *near([after(a, send_z) for a in qkv]),
     )
     send_y, send_z, top, low = narrow(s.table, top, got_z, low, got_y)
-    qkv = mix([after(qkv[0], send_y), *got])
-    up = s.up_end((after(ups[0], send_y), ups_z))
-    end_top, end_low, down_got, up_grad, *got = meet(
-        swap(send_y, "y"), swap(send_z, "zl"), down_got, up[0], *far(qkv)
-    )
-    out_got = swap(after(out_send, end_top), "zh")
+    ups = mix([after(ups[0], send_y), *got])
+    qkv = mix([after(qkv[0], send_y), *more])
+    (out_sum,) = call(sum_kernel, (outs[0], after(out_got, send_y)), [(outs[0].shape, BF)], smem=0)
+    end_top, end_low, ups_z, down_got, *more = meet(
+        swap(send_y, "y"), swap(send_z, "zl"), swap(ups[1], "zl"), down_got, *far(qkv)
+    )
+    out_got = swap(after(out_sum[1], end_top), "zh")
     grad_in = s.last((top, end_top, low, end_low), mid_delta)
+    end = s.qkv_end([qkv[0], *more])
+    up = s.up_end((ups[0], ups_z))
     down = add(down_keep, down_got, F32)
-    end = s.qkv_end([qkv[0], *got])
-    out = add(out_keep, out_got, F32)
-    return results(layer_out, grad_in, end, out, (up_grad, *up[1:]), down)
+    out = add(out_sum[0], out_got, F32)
+    return results(layer_out, grad_in, end, out, up, down)
 
 
 def local_any(*arrays, sizes):
@@ -1278,7 +1273,7 @@
     layer_out, *outs = s.outputs(
         mid, team_scatter(*s.out_gradient(lay_keep, lay_send, attended, mid_delta_b))
     )
-    keep, send = s.inputs(to_own, swap(to_mate, "zh"), w_head, [swap(array, "zh") for array in w_head])
+    keep, send = s.inputs(to_own, swap(to_mate, "zh"), w_head[0], [swap(w_head[0], "zh")])
     grad_in = s.last(team_scatter(keep, send), mid_delta)
     parts = s.qkv_gradient(pieces, others, by_shard, sums)
     own, *got = list(lax.all_to_all(jnp.stack(parts), "x", 0, 0, tiled=True))
@@ -1290,7 +1285,7 @@
         layer_out,
         grad_in,
         s.qkv_end(share(s.qkv_share(own, got[0]))),
-        to_owners(outs),
+        to_owners([part[at] for part in outs for at in range(s.highs)]),
         s.up_end((ups[0], swap(ups[1], "zl"))),
         down,
     )

time: 284 us -> 270 us (0.951)
  Pallas kernels: 62.4 us -> 50 us
  waiting for transfers between devices: 126 us -> 123 us
    pallas_call x48 -> x46, Pallas kernels: 62.4 us -> 50 us  [call(): pl.pallas_call(body, out_shape=[jax.ShapeDtypeStruct(shape, kind) for sha...]
    ppermute x55, waiting for transfers between devices: 78 us -> 74.4 us  [swap(): return lax.ppermute(array, axis, SWAP)]
    ppermute x18, waiting for transfers between devices: 25.5 us -> 28.7 us  [near(): lax.ppermute(arrays[at], ('y', 'c'), apart(4, at))]
  transfers between devices with their start and end apart: 95 -> 95, of which waited for: 45 -> 46; matrix products, arithmetic and copies ran while one was open for 1% -> 1% of each run, Pallas kernels for 17% -> 11%
where the time goes in v1:
time: 270 us; the launch traced here: 268 us
  waiting for transfers between devices  123 us (46%)
  starting transfers between devices  87.5 us (32%)
  Pallas kernels  50 us (19%)
    ppermute x55, waiting for transfers between devices, swap(): return lax.ppermute(array, axis, SWAP)  74.4 us
    pallas_call x46, Pallas kernels, call(): pl.pallas_call(body, out_shape=[jax.ShapeDtypeStruct(shape, kind) for sha...  50 us
    ppermute x55, starting transfers between devices, swap(): return lax.ppermute(array, axis, SWAP)  48.3 us
    ppermute x18, waiting for transfers between devices, near(): lax.ppermute(arrays[at], ('y', 'c'), apart(4, at))  28.7 us
    ppermute x12, waiting for transfers between devices, far(): lax.ppermute(arrays[at], ('zh', 'zl'), apart(4, at))  20.4 us
    ppermute x12, starting transfers between devices, far(): lax.ppermute(arrays[at], ('zh', 'zl'), apart(4, at))  17.7 us
    ppermute x18, starting transfers between devices, near(): lax.ppermute(arrays[at], ('y', 'c'), apart(4, at))  9.65 us
  transfers between devices with their start and end apart: 95, of which 46 were waited for; matrix products, arithmetic and copies ran while one was open for 1% of the time, Pallas kernels for 11%

profile of v1, /device:TPU:0, one launch (start us, length us, event | category | flops | bytes accessed | tf_op | source)
XLA Modules:
  0.0 267.9 jit_solution(17367631201082885889)
XLA Ops:
  1.3 3.3 %shard_map.186 = (bf16[128,1024]{1,0:T(8,128)(2,1)}, bf16[4,56,128]{2,1,0:T(8,128)(2,1)}, bf16[4,56,128]{2,1,0:T(8,128)(2,1)}, bf16[4,56,128]{2,1,0:T(8,128)(2,1...) custom-call(s32[6]{0:T(128)} %stack.24.table._, ...), custom_call_target="tpu_custom_call" | custom-call | flops 1000 | bytes 1024 | tf_op jit(solution)/shard_map/pallas_call | solution.py:95
  4.7 3.0 %collective-permute-start.1 = (bf16[128,1024]{1,0:T(8,128)(2,1)}, bf16[128,1024]{1,0:T(8,128)(2,1)S(1)}, u32[]{:S(2)}, u32[]{:S(2)}) collective-permute-start(bf16[128,1024]{1,0:T(8,128)(2,1)} %get-tuple-element.289.refs_0_), channel_id=1, source_target_pairs={{8,0},{16,8},{24,16},{28,24},{20,28},{12,20},{4,12},{0,4},{9,1},{1... | collective-permute-start | bytes 786440 | tf_op jit(solution)/shard_map/ppermute | solution.py:1076
  9.9 7.6 %collective-permute-done.3.refs_2_ = bf16[4,56,128]{2,1,0:T(8,128)(2,1)S(1)} collective-permute-done((bf16[4,56,128]{2,1,0:T(8,128)(2,1)}, bf16[4,56,128]{2,1,0:T(8,128)(2,1)S(1)}, u32[]{:S(2)}, u32[]{:S(2)}) %collective-permute-start.3) | collective-permute-done | bytes 57376 | tf_op jit(solution)/shard_map/ppermute | solution.py:800
  24.9 3.6 %collective-permute-done.7.refs_1_ = bf16[4,56,128]{2,1,0:T(8,128)(2,1)S(1)} collective-permute-done((bf16[4,56,128]{2,1,0:T(8,128)(2,1)S(1)}, bf16[4,56,128]{2,1,0:T(8,128)(2,1)S(1)}, u32[]{:S(2)}, u32[]{:S(2)}) %collective-permute-start.7) | collective-permute-done | bytes 57376 | tf_op jit(solution)/shard_map/ppermute | solution.py:804
  29.1 2.9 %collective-permute-done.9.refs_3_ = bf16[4,56,128]{2,1,0:T(8,128)(2,1)S(1)} collective-permute-done((bf16[4,56,128]{2,1,0:T(8,128)(2,1)S(1)}, bf16[4,56,128]{2,1,0:T(8,128)(2,1)S(1)}, u32[]{:S(2)}, u32[]{:S(2)}) %collective-permute-start.9) | collective-permute-done | bytes 57376 | tf_op jit(solution)/shard_map/ppermute | solution.py:804
  44.6 8.4 %collective-permute-done.17.two_ref = bf16[4,32,512]{2,1,0:T(8,128)(2,1)S(1)} collective-permute-done((bf16[4,32,512]{2,1,0:T(8,128)(2,1)S(1)}, bf16[4,32,512]{2,1,0:T(8,128)(2,1)S(1)}, u32[]{:S(2)}, u32[]{:S(2)}) %collective-permute-start.17) | collective-permute-done | bytes 131104 | tf_op jit(solution)/shard_map/ppermute | solution.py:808
  59.8 6.7 %shard_map.192 = (bf16[4,64,128]{2,1,0:T(8,128)(2,1)S(1)}, bf16[4,64,128]{2,1,0:T(8,128)(2,1)S(1)}, bf16[4,64,128]{2,1,0:T(8,128)(2,1)S(1)}, bf16[4,64,128]{2,1,...) custom-call(s32[6]{0:T(128)S(1)} %copy-done.6, ...), custom_call_target="tpu_custom_call" | custom-call | flops 7000001024 | bytes 1024 | tf_op jit(solution)/shard_map/pallas_call | solution.py:95
  73.8 5.0 %collective-permute-done.27.refs_2_ = bf16[4,64,128]{2,1,0:T(8,128)(2,1)S(1)} collective-permute-done((bf16[4,64,128]{2,1,0:T(8,128)(2,1)S(1)}, bf16[4,64,128]{2,1,0:T(8,128)(2,1)S(1)}, u32[]{:S(2)}, u32[]{:S(2)}) %collective-permute-start.27) | collective-permute-done | bytes 65568 | tf_op jit(solution)/shard_map/ppermute | solution.py:800
  78.8 2.9 %collective-permute-done.30.refs_15_ = bf16[256,512]{1,0:T(8,128)(2,1)S(1)} collective-permute-done((bf16[256,512]{1,0:T(8,128)(2,1)S(1)}, bf16[256,512]{1,0:T(8,128)(2,1)S(1)}, u32[]{:S(2)}, u32[]{:S(2)}) %collective-permute-start.30) | collective-permute-done | bytes 262176 | tf_op jit(solution)/shard_map/ppermute | solution.py:808
  91.2 4.1 %collective-permute-done.34.refs_7_ = bf16[4,64,128]{2,1,0:T(8,128)(2,1)S(1)} collective-permute-done((bf16[4,64,128]{2,1,0:T(8,128)(2,1)S(1)}, bf16[4,64,128]{2,1,0:T(8,128)(2,1)S(1)}, u32[]{:S(2)}, u32[]{:S(2)}) %collective-permute-start.34) | collective-permute-done | bytes 65568 | tf_op jit(solution)/shard_map/ppermute | solution.py:804
  104.6 3.8 %collective-permute-done.41.refs_17_ = bf16[256,512]{1,0:T(8,128)(2,1)S(1)} collective-permute-done((bf16[256,512]{1,0:T(8,128)(2,1)S(1)}, bf16[256,512]{1,0:T(8,128)(2,1)S(1)}, u32[]{:S(2)}, u32[]{:S(2)}) %collective-permute-start.41) | collective-permute-done | bytes 262176 | tf_op jit(solution)/shard_map/ppermute | solution.py:808
  108.4 6.4 %collective-permute-done.42.refs_19_ = bf16[256,512]{1,0:T(8,128)(2,1)S(1)} collective-permute-done((bf16[256,512]{1,0:T(8,128)(2,1)S(1)}, bf16[256,512]{1,0:T(8,128)(2,1)S(1)}, u32[]{:S(2)}, u32[]{:S(2)}) %collective-permute-start.42) | collective-permute-done | bytes 262176 | tf_op jit(solution)/shard_map/ppermute | solution.py:808
  129.4 6.5 %shard_map.202 = (bf16[512,1024]{1,0:T(8,128)(2,1)S(1)}, bf16[512,1024]{1,0:T(8,128)(2,1)S(1)}, f32[512,1024]{1,0:T(8,128)S(1)}, bf16[512,1024]{1,0:T(8,128)(2,1...) custom-call(s32[6]{0:T(128)S(1)} %copy-done.6, ...), custom_call_target="tpu_custom_call" | custom-call | flops 6000001024 | bytes 1024 | tf_op jit(solution)/shard_map/pallas_call | solution.py:95
  142.1 5.8 %collective-permute-done.54.got_y = bf16[2,64,1024]{2,1,0:T(8,128)(2,1)S(1)} collective-permute-done((bf16[2,64,1024]{2,1,0:T(8,128)(2,1)S(1)}, bf16[2,64,1024]{2,1,0:T(8,128)(2,1)S(1)}, u32[]{:S(2)}, u32[]{:S(2)}) %collective-permute-start.54) | collective-permute-done | bytes 262176 | tf_op jit(solution)/shard_map/ppermute | solution.py:808
  154.2 3.6 %collective-permute-done.57.got_ref = bf16[264,512]{1,0:T(8,128)(2,1)S(1)} collective-permute-done((bf16[264,512]{1,0:T(8,128)(2,1)S(1)}, bf16[264,512]{1,0:T(8,128)(2,1)S(1)}, u32[]{:S(2)}, u32[]{:S(2)}) %collective-permute-start.57) | collective-permute-done | bytes 270368 | tf_op jit(solution)/shard_map/ppermute | solution.py:808
  163.8 3.0 %collective-permute-done.59.refs_2_ = bf16[4,64,128]{2,1,0:T(8,128)(2,1)S(1)} collective-permute-done((bf16[4,64,128]{2,1,0:T(8,128)(2,1)S(1)}, bf16[4,64,128]{2,1,0:T(8,128)(2,1)S(1)}, u32[]{:S(2)}, u32[]{:S(2)}) %collective-permute-start.59) | collective-permute-done | bytes 65568 | tf_op jit(solution)/shard_map/ppermute | solution.py:800
  167.6 5.3 %collective-permute-done.62.refs_1_ = bf16[512,192]{1,0:T(8,128)(2,1)S(1)} collective-permute-done((bf16[512,192]{1,0:T(8,128)(2,1)S(1)}, bf16[512,192]{1,0:T(8,128)(2,1)S(1)}, u32[]{:S(2)}, u32[]{:S(2)}) %collective-permute-start.62) | collective-permute-done | bytes 196640 | tf_op jit(solution)/shard_map/ppermute | solution.py:808
  191.1 7.2 %shard_map.212 = (bf16[8,192,128]{2,1,0:T(8,128)(2,1)S(1)}, bf16[8,192,128]{2,1,0:T(8,128)(2,1)S(1)}, bf16[16,128,192]{2,1,0:T(8,128)(2,1)S(1)}, f32[1,192]{1,0:T(1,128)S(1)}) custom-call(s32[6]{0:T(128)S(1)} %copy-done.6, bf16[1,4,64,128]{3,2,1,0:T(8,128)(2,1)S(1)} %bitcast.49, bf16[1,4,64,128]{3,2,1,0:T(8,128)(2,1)S(1)} %bitcast.50, ...), custom_call_target="tpu_custom_call" | custom-call | flops 8000001024 | bytes 1024 | tf_op jit(solution)/shard_map/pallas_call | solution.py:95
  198.3 2.9 %collective-permute-done.69.got_y = bf16[2,128,1024]{2,1,0:T(8,128)(2,1)S(1)} collective-permute-done((bf16[2,128,1024]{2,1,0:T(8,128)(2,1)S(1)}, bf16[2,128,1024]{2,1,0:T(8,128)(2,1)S(1)}, u32[]{:S(2)}, u32[]{:S(2)}) %collective-permute-start.69) | collective-permute-done | bytes 524320 | tf_op jit(solution)/shard_map/ppermute | solution.py:808
  201.3 4.7 %collective-permute-done.68.got_z = bf16[2,128,1024]{2,1,0:T(8,128)(2,1)S(1)} collective-permute-done((bf16[2,128,1024]{2,1,0:T(8,128)(2,1)S(1)}, bf16[2,128,1024]{2,1,0:T(8,128)(2,1)S(1)}, u32[]{:S(2)}, u32[]{:S(2)}) %collective-permute-start.68) | collective-permute-done | bytes 524320 | tf_op jit(solution)/shard_map/ppermute | solution.py:808
  213.1 3.4 %collective-permute-done.74.got_part = bf16[128,1024]{1,0:T(8,128)(2,1)S(1)} collective-permute-done((bf16[128,1024]{1,0:T(8,128)(2,1)S(1)}, bf16[128,1024]{1,0:T(8,128)(2,1)S(1)}, u32[]{:S(2)}, u32[]{:S(2)}) %collective-permute-start.74) | collective-permute-done | bytes 262176 | tf_op jit(solution)/shard_map/ppermute | solution.py:808
  219.6 5.7 %collective-permute-done.72.got_ref = bf16[8,192,128]{2,1,0:T(8,128)(2,1)S(1)} collective-permute-done((bf16[8,192,128]{2,1,0:T(8,128)(2,1)S(1)}, bf16[8,192,128]{2,1,0:T(8,128)(2,1)S(1)}, u32[]{:S(2)}, u32[]{:S(2)}) %collective-permute-start.72) | collective-permute-done | bytes 393248 | tf_op jit(solution)/shard_map/ppermute | solution.py:808
  237.6 3.0 %collective-permute-done.85.refs_2_ = bf16[4,56,128]{2,1,0:T(8,128)(2,1)S(1)} collective-permute-done((bf16[4,56,128]{2,1,0:T(8,128)(2,1)S(1)}, bf16[4,56,128]{2,1,0:T(8,128)(2,1)S(1)}, u32[]{:S(2)}, u32[]{:S(2)}) %collective-permute-start.85) | collective-permute-done | bytes 57376 | tf_op jit(solution)/shard_map/ppermute | solution.py:800
  241.1 3.5 %collective-permute-done.86.refs_3_ = bf16[4,56,128]{2,1,0:T(8,128)(2,1)S(1)} collective-permute-done((bf16[4,56,128]{2,1,0:T(8,128)(2,1)S(1)}, bf16[4,56,128]{2,1,0:T(8,128)(2,1)S(1)}, u32[]{:S(2)}, u32[]{:S(2)}) %collective-permute-start.86) | collective-permute-done | bytes 57376 | tf_op jit(solution)/shard_map/ppermute | solution.py:800
  (250 shorter events, 153.6 us)
Async XLA Ops:
  4.7 12.8 %collective-permute-start.1 = (bf16[128,1024]{1,0:T(8,128)(2,1)}, bf16[128,1024]{1,0:T(8,128)(2,1)S(1)}, u32[]{:S(2)}, u32[]{:S(2)}) collective-permute-start(bf16[128,1024]{1,0:T(8,128)(2,1)} %get-tuple-element.289.refs_0_), channel_id=1, source_target_pairs={{8,0},{16,8},{24,16},{28,24},{20,28},{12,20},{4,12},{0,4},{9,1},{1... | collective-permute-start | bytes 786440 | tf_op jit(solution)/shard_map/ppermute | solution.py:1076
  17.5 14.5 %collective-permute-start.5 = (bf16[128,1024]{1,0:T(8,128)(2,1)S(1)}, bf16[128,1024]{1,0:T(8,128)(2,1)S(1)}, u32[]{:S(2)}, u32[]{:S(2)}) collective-permute-start(bf16[128,1024]{1,0:T(8,128)(2,1)S(1)} %collective-permute-done.refs_1_), channel_id=1, source_target_pairs={{0,8},{8,16},{16,24},{24,28},{28,20},{20,12},{12,4},{4,0},{1,9},{9... | collective-permute-start | bytes 786440 | tf_op jit(solution)/shard_map/ppermute | solution.py:1073
  17.6 14.4 %collective-permute-start.6 = (bf16[128,1024]{1,0:T(8,128)(2,1)S(1)}, bf16[128,1024]{1,0:T(8,128)(2,1)S(1)}, u32[]{:S(2)}, u32[]{:S(2)}) collective-permute-start(bf16[128,1024]{1,0:T(8,128)(2,1)S(1)} %collective-permute-done.1.refs_2_), channel_id=1, source_target_pairs={{8,0},{16,8},{24,16},{28,24},{20,28},{12,20},{4,12},{0,4},{9,1},{1... | collective-permute-start | bytes 786440 | tf_op jit(solution)/shard_map/ppermute | solution.py:1076
  44.4 13.7 %collective-permute-start.20 = (bf16[2,128,1024]{2,1,0:T(8,128)(2,1)S(1)}, bf16[2,128,1024]{2,1,0:T(8,128)(2,1)S(1)}, u32[]{:S(2)}, u32[]{:S(2)}) collective-permute-start(bf16[2,128,1024]{2,1,0:T(8,128)(2,1)S(1)} %shard_map.191), channel_id=1, source_target_pairs={{0,2},{2,0},{1,3},{3,1},{4,6},{6,4},{5,7},{7,5},{8,10},{10,8},{9,1... | collective-permute-start | bytes 1572872 | tf_op jit(solution)/shard_map/ppermute | solution.py:808
  53.0 13.5 %collective-permute-start.25 = (bf16[32,1024]{1,0:T(8,128)(2,1)S(1)}, bf16[32,1024]{1,0:T(8,128)(2,1)S(1)}, u32[]{:S(2)}, u32[]{:S(2)}) collective-permute-start(bf16[32,1024]{1,0:T(8,128)(2,1)S(1)} %copy-done.9), channel_id=1, source_target_pairs={{0,24},{8,16},{16,8},{24,0},{1,25},{9,17},{17,9},{25,1},{2,26},{10... | collective-permute-start | bytes 196616 | tf_op jit(solution)/shard_map/ppermute | solution.py:1096
  68.1 13.6 %collective-permute-start.30 = (bf16[256,512]{1,0:T(8,128)(2,1)S(1)}, bf16[256,512]{1,0:T(8,128)(2,1)S(1)}, u32[]{:S(2)}, u32[]{:S(2)}) collective-permute-start(bf16[256,512]{1,0:T(8,128)(2,1)S(1)} %shard_map.194.refs_14_), channel_id=1, source_target_pairs={{0,16},{16,0},{1,17},{17,1},{2,18},{18,2},{3,19},{19,3},{4,20},{20... | collective-permute-start | bytes 786440 | tf_op jit(solution)/shard_map/ppermute | solution.py:808
  68.4 13.4 %collective-permute-start.31 = (bf16[128,1024]{1,0:T(8,128)(2,1)S(1)}, bf16[128,1024]{1,0:T(8,128)(2,1)S(1)}, u32[]{:S(2)}, u32[]{:S(2)}) collective-permute-start(bf16[128,1024]{1,0:T(8,128)(2,1)S(1)} %bitcast.34), channel_id=1, source_target_pairs={{0,4},{4,0},{1,5},{5,1},{2,6},{6,2},{3,7},{7,3},{8,12},{12,8},{9,1... | collective-permute-start | bytes 786440 | tf_op jit(solution)/shard_map/ppermute | solution.py:808
  81.8 13.5 %collective-permute-start.37 = (bf16[8,32,1024]{2,1,0:T(8,128)(2,1)S(1)}, bf16[8,32,1024]{2,1,0:T(8,128)(2,1)S(1)}, u32[]{:S(2)}, u32[]{:S(2)}) collective-permute-start(bf16[8,32,1024]{2,1,0:T(8,128)(2,1)S(1)} %shard_map.195.refs_0_), channel_id=1, source_target_pairs={{0,2},{2,0},{1,3},{3,1},{4,6},{6,4},{5,7},{7,5},{8,10},{10,8},{9,1... | collective-permute-start | bytes 1572872 | tf_op jit(solution)/shard_map/ppermute | solution.py:808
  81.9 14.3 %collective-permute-start.35 = (bf16[8,32,1024]{2,1,0:T(8,128)(2,1)S(1)}, bf16[8,32,1024]{2,1,0:T(8,128)(2,1)S(1)}, u32[]{:S(2)}, u32[]{:S(2)}) collective-permute-start(bf16[8,32,1024]{2,1,0:T(8,128)(2,1)S(1)} %shard_map.195.refs_0_), channel_id=1, source_target_pairs={{0,4},{4,0},{1,5},{5,1},{2,6},{6,2},{3,7},{7,3},{8,12},{12,8},{9,1... | collective-permute-start | bytes 1572872 | tf_op jit(solution)/shard_map/ppermute | solution.py:808
  83.2 12.1 %collective-permute-start.36 = (bf16[256,512]{1,0:T(8,128)(2,1)S(1)}, bf16[256,512]{1,0:T(8,128)(2,1)S(1)}, u32[]{:S(2)}, u32[]{:S(2)}) collective-permute-start(bf16[256,512]{1,0:T(8,128)(2,1)S(1)} %shard_map.194.refs_14_), channel_id=1, source_target_pairs={{0,1},{1,0},{2,3},{3,2},{4,5},{5,4},{6,7},{7,6},{8,9},{9,8},{10,11... | collective-permute-start | bytes 786440 | tf_op jit(solution)/shard_map/ppermute | solution.py:808
  99.6 16.6 %collective-permute-start.43 = (bf16[3,128,1024]{2,1,0:T(8,128)(2,1)S(1)}, bf16[3,128,1024]{2,1,0:T(8,128)(2,1)S(1)}, u32[]{:S(2)}, u32[]{:S(2)}) collective-permute-start(bf16[3,128,1024]{2,1,0:T(8,128)(2,1)S(1)} %shard_map.198), channel_id=1, source_target_pairs={{0,2},{2,0},{1,3},{3,1},{4,6},{6,4},{5,7},{7,5},{8,10},{10,8},{9,1... | collective-permute-start | bytes 2359304 | tf_op jit(solution)/shard_map/ppermute | solution.py:808
  100.8 14.0 %collective-permute-start.42 = (bf16[256,512]{1,0:T(8,128)(2,1)S(1)}, bf16[256,512]{1,0:T(8,128)(2,1)S(1)}, u32[]{:S(2)}, u32[]{:S(2)}) collective-permute-start(bf16[256,512]{1,0:T(8,128)(2,1)S(1)} %copy-done.7), channel_id=1, source_target_pairs={{0,16},{16,0},{1,17},{17,1},{2,18},{18,2},{3,19},{19,3},{4,20},{20... | collective-permute-start | bytes 786440 | tf_op jit(solution)/shard_map/ppermute | solution.py:808
  100.8 14.0 %collective-permute-start.40 = (bf16[128,1024]{1,0:T(8,128)(2,1)S(1)}, bf16[128,1024]{1,0:T(8,128)(2,1)S(1)}, u32[]{:S(2)}, u32[]{:S(2)}) collective-permute-start(bf16[128,1024]{1,0:T(8,128)(2,1)S(1)} %get-tuple-element.365.refs_0_.refs_7_), channel_id=1, source_target_pairs={{0,4},{4,0},{1,5},{5,1},{2,6},{6,2},{3,7},{7,3},{8,12},{12,8},{9,1... | collective-permute-start | bytes 786440 | tf_op jit(solution)/shard_map/ppermute | solution.py:808
  102.1 14.1 %collective-permute-start.39 = (bf16[128,1024]{1,0:T(8,128)(2,1)S(1)}, bf16[128,1024]{1,0:T(8,128)(2,1)S(1)}, u32[]{:S(2)}, u32[]{:S(2)}) collective-permute-start(bf16[128,1024]{1,0:T(8,128)(2,1)S(1)} %get-tuple-element.365.refs_0_.refs_7_), channel_id=1, source_target_pairs={{0,8},{8,0},{1,9},{9,1},{2,10},{10,2},{3,11},{11,3},{4,12},{12,4},... | collective-permute-start | bytes 786440 | tf_op jit(solution)/shard_map/ppermute | solution.py:808
  159.6 13.3 %collective-permute-start.61 = (bf16[264,512]{1,0:T(8,128)(2,1)S(1)}, bf16[264,512]{1,0:T(8,128)(2,1)S(1)}, u32[]{:S(2)}, u32[]{:S(2)}) collective-permute-start(bf16[264,512]{1,0:T(8,128)(2,1)S(1)} %get-tuple-element.422), channel_id=1, source_target_pairs={{0,1},{1,0},{2,3},{3,2},{4,5},{5,4},{6,7},{7,6},{8,9},{9,8},{10,11... | collective-permute-start | bytes 811016 | tf_op jit(solution)/shard_map/ppermute | solution.py:808
  184.3 14.0 %collective-permute-start.70 = (bf16[128,1024]{1,0:T(8,128)(2,1)S(1)}, bf16[128,1024]{1,0:T(8,128)(2,1)S(1)}, u32[]{:S(2)}, u32[]{:S(2)}) collective-permute-start(bf16[128,1024]{1,0:T(8,128)(2,1)S(1)} %get-tuple-element.459), channel_id=1, source_target_pairs={{0,1},{1,0},{2,3},{3,2},{4,5},{5,4},{6,7},{7,6},{8,9},{9,8},{10,11... | collective-permute-start | bytes 786440 | tf_op jit(solution)/shard_map/ppermute | solution.py:808
  185.3 12.9 %collective-permute-start.71 = (bf16[512,192]{1,0:T(8,128)(2,1)S(1)}, bf16[512,192]{1,0:T(8,128)(2,1)S(1)}, u32[]{:S(2)}, u32[]{:S(2)}) collective-permute-start(bf16[512,192]{1,0:T(8,128)(2,1)S(1)} %collective-permute-done.62.refs_1_), channel_id=1, source_target_pairs={{0,1},{1,0},{2,3},{3,2},{4,5},{5,4},{6,7},{7,6},{8,9},{9,8},{10,11... | collective-permute-start | bytes 589832 | tf_op jit(solution)/shard_map/ppermute | solution.py:808
  186.3 26.8 %collective-permute-start.75 = (bf16[264,512]{1,0:T(8,128)(2,1)S(1)}, bf16[264,512]{1,0:T(8,128)(2,1)S(1)}, u32[]{:S(2)}, u32[]{:S(2)}) collective-permute-start(bf16[264,512]{1,0:T(8,128)(2,1)S(1)} %shard_map.210), channel_id=1, source_target_pairs={{0,16},{16,0},{1,17},{17,1},{2,18},{18,2},{3,19},{19,3},{4,20},{20... | collective-permute-start | bytes 811016 | tf_op jit(solution)/shard_map/ppermute | solution.py:808
  188.9 17.0 %collective-permute-start.68 = (bf16[2,128,1024]{2,1,0:T(8,128)(2,1)S(1)}, bf16[2,128,1024]{2,1,0:T(8,128)(2,1)S(1)}, u32[]{:S(2)}, u32[]{:S(2)}) collective-permute-start(bf16[2,128,1024]{2,1,0:T(8,128)(2,1)S(1)} %get-tuple-element.449), channel_id=1, source_target_pairs={{0,8},{8,0},{1,9},{9,1},{2,10},{10,2},{3,11},{11,3},{4,12},{12,4},... | collective-permute-start | bytes 1572872 | tf_op jit(solution)/shard_map/ppermute | solution.py:808
  207.9 17.4 %collective-permute-start.72 = (bf16[8,192,128]{2,1,0:T(8,128)(2,1)S(1)}, bf16[8,192,128]{2,1,0:T(8,128)(2,1)S(1)}, u32[]{:S(2)}, u32[]{:S(2)}) collective-permute-start(bf16[8,192,128]{2,1,0:T(8,128)(2,1)S(1)} %get-tuple-element.463), channel_id=1, source_target_pairs={{0,16},{16,0},{1,17},{17,1},{2,18},{18,2},{3,19},{19,3},{4,20},{20... | collective-permute-start | bytes 1179656 | tf_op jit(solution)/shard_map/ppermute | solution.py:808
  230.9 13.7 %collective-permute-start.82 = (bf16[2,64,1024]{2,1,0:T(8,128)(2,1)S(1)}, bf16[2,64,1024]{2,1,0:T(8,128)(2,1)S(1)}, u32[]{:S(2)}, u32[]{:S(2)}) collective-permute-start(bf16[2,64,1024]{2,1,0:T(8,128)(2,1)S(1)} %get-tuple-element.512), channel_id=1, source_target_pairs={{0,4},{4,0},{1,5},{5,1},{2,6},{6,2},{3,7},{7,3},{8,12},{12,8},{9,1... | collective-permute-start | bytes 786440 | tf_op jit(solution)/shard_map/ppermute | solution.py:808
  232.3 12.8 %collective-permute-start.81 = (bf16[2,64,1024]{2,1,0:T(8,128)(2,1)S(1)}, bf16[2,64,1024]{2,1,0:T(8,128)(2,1)S(1)}, u32[]{:S(2)}, u32[]{:S(2)}) collective-permute-start(bf16[2,64,1024]{2,1,0:T(8,128)(2,1)S(1)} %get-tuple-element.511), channel_id=1, source_target_pairs={{0,8},{8,0},{1,9},{9,1},{2,10},{10,2},{3,11},{11,3},{4,12},{12,4},... | collective-permute-start | bytes 786440 | tf_op jit(solution)/shard_map/ppermute | solution.py:808
  232.3 19.0 %collective-permute-start.90 = (bf16[128,1024]{1,0:T(8,128)(2,1)S(1)}, bf16[128,1024]{1,0:T(8,128)(2,1)S(1)}, u32[]{:S(2)}, u32[]{:S(2)}) collective-permute-start(bf16[128,1024]{1,0:T(8,128)(2,1)S(1)} %shard_map.215), channel_id=1, source_target_pairs={{0,16},{16,0},{1,17},{17,1},{2,18},{18,2},{3,19},{19,3},{4,20},{20... | collective-permute-start | bytes 786440 | tf_op jit(solution)/shard_map/ppermute | solution.py:808
  245.8 12.4 %collective-permute-start.87 = (bf16[64,1024]{1,0:T(8,128)(2,1)S(1)}, bf16[64,1024]{1,0:T(8,128)(2,1)S(1)}, u32[]{:S(2)}, u32[]{:S(2)}) collective-permute-start(bf16[64,1024]{1,0:T(8,128)(2,1)S(1)} %get-tuple-element.525), channel_id=1, source_target_pairs={{0,4},{4,0},{1,5},{5,1},{2,6},{6,2},{3,7},{7,3},{8,12},{12,8},{9,1... | collective-permute-start | bytes 393224 | tf_op jit(solution)/shard_map/ppermute | solution.py:808
  (86 other events, 811.5 us)

commit v2 on v1

--- a/solution.py
+++ b/solution.py
@@ -553,7 +553,7 @@
     place = Place(table)
     for far in range(4):
         for near in range(4):
-            all_ref[place.ctx ^ (far * 4 + near)] = parts[far][near]
+            all_ref[place.ctx ^ (far * 4 + near)] = parts[far][near, : all_ref.shape[1]]
     rows = own_ref.shape[0]
     half = rows // 2
     width = HEADS * HD
@@ -758,6 +758,49 @@
     keep_out[...] = dot(lhs_ref[:middle, :], rhs_ref[...], NT)
 
 
+def blend_kernel(*refs):
+    ups, qkvs, (up_keep, *outs) = refs[:4], refs[4:8], refs[8:]
+    tall = qkvs[0].shape[1]
+    rows = ups[0].shape[1]
+    for near in range(4):
+        up_keep[near] = ups[near][0]
+        for far, out in enumerate(outs):
+            out[near, :tall] = qkvs[near][far]
+        for at in range(ups[0].shape[2] // (2 * HD)):
+            first = tall + at * rows
+            outs[1][near, first : first + rows] = ups[near][1, :, at * 2 * HD : (at + 1) * 2 * HD]
+
+
+def sums_kernel(one_ref, two_ref, out_own, out_got, send_out, keep_out):
+    rows = one_ref.shape[0]
+    send_out[:rows] = (one_ref[...].astype(F32) + two_ref[...].astype(F32)).astype(BF)
+    send_out[rows:] = (out_own[1].astype(F32) + out_got[1].astype(F32)).astype(BF)
+    keep_out[...] = out_own[0].astype(F32) + out_got[0].astype(F32)
+
+
+def end_kernel(
+    table, keep_top, got_top, keep_low, got_low, mid_delta_ref, hidden_ref, gain1_ref, bias1_ref, gain2_ref, bias2_ref,
+    q0_ref, q1_ref, q2_ref, q3_ref, qkv_ref, up_one, up_ref, down_keep, out_keep, got_ref,
+    grad_out, qkv_out, qkv_gain, qkv_bias, up_out, up_gain, up_bias, down_out, out_out,
+    all_ref, up_two, sum_ref,
+):
+    last_kernel(table, keep_top, got_top, keep_low, got_low, mid_delta_ref, hidden_ref, gain1_ref, grad_out)
+    tall, rows = q0_ref.shape[1], up_one.shape[1]
+    for near in range(4):
+        for at in range(up_one.shape[2] // (2 * HD)):
+            first = tall + at * rows
+            up_two[near, :, at * 2 * HD : (at + 1) * 2 * HD] = q1_ref[near, first : first + rows]
+    qkv_end_kernel(
+        table, q0_ref, q1_ref, q2_ref, q3_ref, qkv_ref, gain1_ref, bias1_ref, qkv_out, qkv_gain, qkv_bias, all_ref, wide=2
+    )
+    up_end_kernel(
+        table, up_one, up_two, up_ref, gain2_ref, bias2_ref, up_out, up_gain, up_bias, sum_ref, runs=2, wide=2
+    )
+    rows = down_keep.shape[0]
+    down_out[...] = down_keep[...] + got_ref[:rows].astype(F32)
+    out_out[...] = out_keep[...] + got_ref[rows:].astype(F32)
+
+
 def last_kernel(_, keep_top, got_top, keep_low, got_low, mid_delta_ref, hidden_ref, gain_ref, out_ref):
     grad = jnp.concatenate(
         [keep_top[...] + got_top[...].astype(F32), keep_low[...] + got_low[...].astype(F32)], axis=0
@@ -1084,9 +1127,15 @@
     ups = [after(up, a2) for up in up_b]
     a3, b3, packed_x, *got = meet(ahead(a2), behind(b2), swap(packed, "x"), *near(ups))
     ups = mix([ups[0], *got])
-    a4, up_z, first, down_x = meet(
-        ahead(a3), swap(ups[1], "zl"), swap(after(first, a3), "c"), swap(after(down_b, a3), "x")
-    )
+    half = s.half
+    one, two, up_z, first, down_x = meet(
+        ahead(a3[:half]),
+        behind(b3[half:]),
+        swap(ups[1], "zl"),
+        swap(after(first, a3), "c"),
+        swap(after(down_b, a3), "x"),
+    )
+    a4 = stack([one, two]).reshape(s.rows, s.width)
     second = stack([a3, b3])
     (up_t,) = call(join_kernel, (s.table, ups[0], up_z, down_b), [((TEAM * s.wrows, s.cols), BF)])
     pieces = [norm_in, a1, b1, a2, b2, a3, b3, a4]
@@ -1169,41 +1218,60 @@
     send_y, send_z, top, low = narrow(s.table, top, got_z, low, got_y)
     (up_keep,) = call(up_add_kernel, (up_parts[0], after(up_near, to_own)), [(up_shape, BF)], smem=0)
     qkv_own, qkv_send = s.qkv_gradient(pieces, others, after(by_shard, send_y), sums)
-    down_send = add(down_parts[1], after(down_far, send_y), BF)
-    end_top, end_low, qkv_send, up_got, down_send = meet(
-        swap(send_y, "y"), swap(send_z, "zl"), qkv_send, up_got, down_send
+    end_top, end_low, qkv_send, up_got = meet(
+        swap(send_y, "y"), swap(send_z, "zl"), qkv_send, up_got
     )
     ups = s.up_share(up_keep, up_got)
     ends = top, end_top, low, end_low
     down_keep = add(down_parts[0], after(down_near, end_top), F32)
     from_mate, qkv_got, *got = meet(from_mate, swap(after(qkv_send, end_top), "x"), *near(ups))
     keep, send = s.inputs(to_own, from_mate, w_head[0], [mate_1, mate_2])
-    layer_out, *outs = s.outputs(mid, [after(array, send) for array in ends])
+    layer_out, *outs = s.outputs(mid, ends)
     qkv = s.qkv_share(qkv_own, after(qkv_got, send))
-    send, layer_out, *qkv = meet(swap(send, "c"), layer_out, *qkv)
+    send, out_got, *qkv = meet(swap(send, "c"), swap(after(outs[1], send), "x"), *qkv)
 
     send_z, send_y, top, low = spread(s.table, keep, send)
-    down_got = swap(after(down_send, send_z), "zh")
-    got_z, got_y, out_got, *more = meet(
-        swap(send_z, "zl"),
-        swap(send_y, "y"),
-        swap(after(outs[1], send_z), "x"),
-        *near([after(a, send_z) for a in qkv]),
+    last_send, out_keep = call(
+        sums_kernel,
+        (after(down_parts[1], send_z), down_far, outs[0], out_got),
+        [((s.ffn + s.wrows, s.width), BF), ((s.wrows, s.width), F32)],
+        smem=0,
+    )
+    last_got = swap(last_send, "zh")
+    got_z, got_y, *more = meet(
+        swap(send_z, "zl"), swap(send_y, "y"), *near([after(a, send_z) for a in qkv])
     )
     send_y, send_z, top, low = narrow(s.table, top, got_z, low, got_y)
-    ups = mix([after(ups[0], send_y), *got])
-    qkv = mix([after(qkv[0], send_y), *more])
-    (out_sum,) = call(sum_kernel, (outs[0], after(out_got, send_y)), [(outs[0].shape, BF)], smem=0)
-    end_top, end_low, ups_z, down_got, *more = meet(
-        swap(send_y, "y"), swap(send_z, "zl"), swap(ups[1], "zl"), down_got, *far(qkv)
-    )
-    out_got = swap(after(out_sum[1], end_top), "zh")
-    grad_in = s.last((top, end_top, low, end_low), mid_delta)
-    end = s.qkv_end([qkv[0], *more])
-    up = s.up_end((ups[0], ups_z))
-    down = add(down_keep, down_got, F32)
-    out = add(out_sum[0], out_got, F32)
-    return results(layer_out, grad_in, end, out, up, down)
+    piece = ((4, s.qkv_tall, 2 * HD), BF)
+    tall = s.qkv_tall + s.up_tall * s.cols // (2 * HD)
+    up_keep, *qkv = call(
+        blend_kernel,
+        (after(ups[0], send_y), *got, qkv[0], *more),
+        [((4, s.up_tall, s.cols), BF), piece, ((4, tall, 2 * HD), BF), piece, piece],
+        smem=0,
+    )
+    end_top, end_low, last_got, *more = meet(swap(send_y, "y"), swap(send_z, "zl"), last_got, *far(qkv))
+    line = ((1, s.wrows), F32)
+    outs = call(
+        end_kernel,
+        (
+            s.table, top, end_top, low, end_low, mid_delta, s.hidden, s.gain1, s.bias1, s.gain2, s.bias2,
+            qkv[0], *more, s.qkv, up_keep, s.up, down_keep, out_keep, last_got,
+        ),
+        [
+            ((s.rows, s.width), BF),
+            (s.qkv.shape, F32), line, line,
+            (s.up.shape, F32), line, line,
+            (s.down.shape, F32),
+            (s.out.shape, F32),
+        ],
+        [
+            ((HEADS, s.qkv_tall, 2 * HD), BF),
+            ((4, s.up_tall, s.cols), BF),
+            ((1, s.up.shape[1]), F32),
+        ],
+    )
+    return results(layer_out, outs[0], outs[1:4], outs[8], outs[4:7], outs[7])
 
 
 def local_any(*arrays, sizes):

time: 270 us -> 269 us (level)
  Pallas kernels: 50 us -> 46.3 us
  waiting for transfers between devices: 123 us -> 126 us
    ppermute x12, waiting for transfers between devices: 20.4 us -> 26.7 us  [far(): lax.ppermute(arrays[at], ('zh', 'zl'), apart(4, at))]
    ppermute x55 -> x53, waiting for transfers between devices: 74.4 us -> 69.8 us  [swap(): return lax.ppermute(array, axis, SWAP)]
    pallas_call x46 -> x41, Pallas kernels: 50 us -> 46.3 us  [call(): pl.pallas_call(body, out_shape=[jax.ShapeDtypeStruct(shape, kind) for sha...]
    ppermute x18, waiting for transfers between devices: 28.7 us -> 25.9 us  [near(): lax.ppermute(arrays[at], ('y', 'c'), apart(4, at))]
    ppermute x55 -> x53, starting transfers between devices: 48.3 us -> 45.9 us  [swap(): return lax.ppermute(array, axis, SWAP)]
    ppermute x3 -> x4, starting transfers between devices: 5.28 us -> 7.45 us  [behind(): return lax.ppermute(array, CHIPS, left)]
  transfers between devices with their start and end apart: 95 -> 94, of which waited for: 46 -> 45; matrix products, arithmetic and copies ran while one was open for 1% -> 1% of each run, Pallas kernels for 11% -> 9%
where the time goes in v2:
time: 269 us; the launch traced here: 266 us
  waiting for transfers between devices  126 us (47%)
  starting transfers between devices  87 us (32%)
  Pallas kernels  46.3 us (17%)
    ppermute x53, waiting for transfers between devices, swap(): return lax.ppermute(array, axis, SWAP)  69.8 us
    pallas_call x41, Pallas kernels, call(): pl.pallas_call(body, out_shape=[jax.ShapeDtypeStruct(shape, kind) for sha...  46.3 us
    ppermute x53, starting transfers between devices, swap(): return lax.ppermute(array, axis, SWAP)  45.9 us
    ppermute x12, waiting for transfers between devices, far(): lax.ppermute(arrays[at], ('zh', 'zl'), apart(4, at))  26.7 us
    ppermute x18, waiting for transfers between devices, near(): lax.ppermute(arrays[at], ('y', 'c'), apart(4, at))  25.9 us
    ppermute x12, starting transfers between devices, far(): lax.ppermute(arrays[at], ('zh', 'zl'), apart(4, at))  16.3 us
    ppermute x18, starting transfers between devices, near(): lax.ppermute(arrays[at], ('y', 'c'), apart(4, at))  10.9 us
    ppermute x4, starting transfers between devices, behind(): return lax.ppermute(array, CHIPS, left)  7.45 us
  transfers between devices with their start and end apart: 94, of which 45 were waited for; matrix products, arithmetic and copies ran while one was open for 1% of the time, Pallas kernels for 9%

profile of v2, /device:TPU:0, one launch (start us, length us, event | category | flops | bytes accessed | tf_op | source)
XLA Modules:
  0.0 266.3 jit_solution(5526685487819941717)
XLA Ops:
  1.3 3.3 %shard_map.186 = (bf16[128,1024]{1,0:T(8,128)(2,1)}, bf16[4,56,128]{2,1,0:T(8,128)(2,1)}, bf16[4,56,128]{2,1,0:T(8,128)(2,1)}, bf16[4,56,128]{2,1,0:T(8,128)(2,1...) custom-call(s32[6]{0:T(128)} %stack.24.table._, ...), custom_call_target="tpu_custom_call" | custom-call | flops 1000 | bytes 1024 | tf_op jit(solution)/shard_map/pallas_call | solution.py:95
  4.6 3.0 %collective-permute-start.1 = (bf16[128,1024]{1,0:T(8,128)(2,1)}, bf16[128,1024]{1,0:T(8,128)(2,1)S(1)}, u32[]{:S(2)}, u32[]{:S(2)}) collective-permute-start(bf16[128,1024]{1,0:T(8,128)(2,1)} %get-tuple-element.283.refs_0_), channel_id=1, source_target_pairs={{8,0},{16,8},{24,16},{28,24},{20,28},{12,20},{4,12},{0,4},{9,1},{1... | collective-permute-start | bytes 786440 | tf_op jit(solution)/shard_map/ppermute | solution.py:1119
  9.8 7.6 %collective-permute-done.3.refs_2_ = bf16[4,56,128]{2,1,0:T(8,128)(2,1)S(1)} collective-permute-done((bf16[4,56,128]{2,1,0:T(8,128)(2,1)}, bf16[4,56,128]{2,1,0:T(8,128)(2,1)S(1)}, u32[]{:S(2)}, u32[]{:S(2)}) %collective-permute-start.3) | collective-permute-done | bytes 57376 | tf_op jit(solution)/shard_map/ppermute | solution.py:843
  24.9 3.6 %collective-permute-done.7.refs_1_ = bf16[4,56,128]{2,1,0:T(8,128)(2,1)S(1)} collective-permute-done((bf16[4,56,128]{2,1,0:T(8,128)(2,1)S(1)}, bf16[4,56,128]{2,1,0:T(8,128)(2,1)S(1)}, u32[]{:S(2)}, u32[]{:S(2)}) %collective-permute-start.7) | collective-permute-done | bytes 57376 | tf_op jit(solution)/shard_map/ppermute | solution.py:847
  58.6 6.8 %shard_map.193 = (bf16[4,64,128]{2,1,0:T(8,128)(2,1)S(1)}, bf16[4,64,128]{2,1,0:T(8,128)(2,1)S(1)}, bf16[4,64,128]{2,1,0:T(8,128)(2,1)S(1)}, bf16[4,64,128]{2,1,...) custom-call(s32[6]{0:T(128)S(1)} %copy-done.7, ...), custom_call_target="tpu_custom_call" | custom-call | flops 7000001024 | bytes 1024 | tf_op jit(solution)/shard_map/pallas_call | solution.py:95
  73.1 5.3 %collective-permute-done.28.refs_2_ = bf16[4,64,128]{2,1,0:T(8,128)(2,1)S(1)} collective-permute-done((bf16[4,64,128]{2,1,0:T(8,128)(2,1)S(1)}, bf16[4,64,128]{2,1,0:T(8,128)(2,1)S(1)}, u32[]{:S(2)}, u32[]{:S(2)}) %collective-permute-start.28) | collective-permute-done | bytes 65568 | tf_op jit(solution)/shard_map/ppermute | solution.py:843
  83.5 2.9 %collective-permute-start.34 = (bf16[4,64,128]{2,1,0:T(8,128)(2,1)S(1)}, bf16[4,64,128]{2,1,0:T(8,128)(2,1)S(1)}, u32[]{:S(2)}, u32[]{:S(2)}) collective-permute-start(bf16[4,64,128]{2,1,0:T(8,128)(2,1)S(1)} %get-tuple-element.347), channel_id=1, source_target_pairs={{0,16},{8,24},{16,0},{24,8},{1,17},{9,25},{17,1},{25,9},{2,18},{10... | collective-permute-start | bytes 196616 | tf_op jit(solution)/shard_map/ppermute | solution.py:847
  90.9 3.7 %collective-permute-done.35.refs_7_ = bf16[4,64,128]{2,1,0:T(8,128)(2,1)S(1)} collective-permute-done((bf16[4,64,128]{2,1,0:T(8,128)(2,1)S(1)}, bf16[4,64,128]{2,1,0:T(8,128)(2,1)S(1)}, u32[]{:S(2)}, u32[]{:S(2)}) %collective-permute-start.35) | collective-permute-done | bytes 65568 | tf_op jit(solution)/shard_map/ppermute | solution.py:847
  101.3 2.9 %collective-permute-start.40 = (bf16[128,1024]{1,0:T(8,128)(2,1)S(1)}, bf16[128,1024]{1,0:T(8,128)(2,1)S(1)}, u32[]{:S(2)}, u32[]{:S(2)}) collective-permute-start(bf16[128,1024]{1,0:T(8,128)(2,1)S(1)} %get-tuple-element.359.refs_0_.refs_7_), channel_id=1, source_target_pairs={{0,8},{8,0},{1,9},{9,1},{2,10},{10,2},{3,11},{11,3},{4,12},{12,4},... | collective-permute-start | bytes 786440 | tf_op jit(solution)/shard_map/ppermute | solution.py:851
  104.2 3.8 %collective-permute-done.42.refs_17_ = bf16[256,512]{1,0:T(8,128)(2,1)S(1)} collective-permute-done((bf16[256,512]{1,0:T(8,128)(2,1)S(1)}, bf16[256,512]{1,0:T(8,128)(2,1)S(1)}, u32[]{:S(2)}, u32[]{:S(2)}) %collective-permute-start.42) | collective-permute-done | bytes 262176 | tf_op jit(solution)/shard_map/ppermute | solution.py:851
  108.0 6.5 %collective-permute-done.43.refs_19_ = bf16[256,512]{1,0:T(8,128)(2,1)S(1)} collective-permute-done((bf16[256,512]{1,0:T(8,128)(2,1)S(1)}, bf16[256,512]{1,0:T(8,128)(2,1)S(1)}, u32[]{:S(2)}, u32[]{:S(2)}) %collective-permute-start.43) | collective-permute-done | bytes 262176 | tf_op jit(solution)/shard_map/ppermute | solution.py:851
  129.0 6.5 %shard_map.203 = (bf16[512,1024]{1,0:T(8,128)(2,1)S(1)}, bf16[512,1024]{1,0:T(8,128)(2,1)S(1)}, f32[512,1024]{1,0:T(8,128)S(1)}, bf16[512,1024]{1,0:T(8,128)(2,1...) custom-call(s32[6]{0:T(128)S(1)} %copy-done.7, ...), custom_call_target="tpu_custom_call" | custom-call | flops 6000001024 | bytes 1024 | tf_op jit(solution)/shard_map/pallas_call | solution.py:95
  141.8 5.7 %collective-permute-done.55.got_y = bf16[2,64,1024]{2,1,0:T(8,128)(2,1)S(1)} collective-permute-done((bf16[2,64,1024]{2,1,0:T(8,128)(2,1)S(1)}, bf16[2,64,1024]{2,1,0:T(8,128)(2,1)S(1)}, u32[]{:S(2)}, u32[]{:S(2)}) %collective-permute-start.55) | collective-permute-done | bytes 262176 | tf_op jit(solution)/shard_map/ppermute | solution.py:851
  153.8 3.6 %collective-permute-done.58.got_ref = bf16[264,512]{1,0:T(8,128)(2,1)S(1)} collective-permute-done((bf16[264,512]{1,0:T(8,128)(2,1)S(1)}, bf16[264,512]{1,0:T(8,128)(2,1)S(1)}, u32[]{:S(2)}, u32[]{:S(2)}) %collective-permute-start.58) | collective-permute-done | bytes 270368 | tf_op jit(solution)/shard_map/ppermute | solution.py:851
  163.5 3.0 %collective-permute-done.60.refs_2_ = bf16[4,64,128]{2,1,0:T(8,128)(2,1)S(1)} collective-permute-done((bf16[4,64,128]{2,1,0:T(8,128)(2,1)S(1)}, bf16[4,64,128]{2,1,0:T(8,128)(2,1)S(1)}, u32[]{:S(2)}, u32[]{:S(2)}) %collective-permute-start.60) | collective-permute-done | bytes 65568 | tf_op jit(solution)/shard_map/ppermute | solution.py:843
  167.1 5.0 %collective-permute-done.63.refs_1_ = bf16[512,192]{1,0:T(8,128)(2,1)S(1)} collective-permute-done((bf16[512,192]{1,0:T(8,128)(2,1)S(1)}, bf16[512,192]{1,0:T(8,128)(2,1)S(1)}, u32[]{:S(2)}, u32[]{:S(2)}) %collective-permute-start.63) | collective-permute-done | bytes 196640 | tf_op jit(solution)/shard_map/ppermute | solution.py:851
  190.7 7.2 %shard_map.213 = (bf16[8,192,128]{2,1,0:T(8,128)(2,1)S(1)}, bf16[8,192,128]{2,1,0:T(8,128)(2,1)S(1)}, bf16[16,128,192]{2,1,0:T(8,128)(2,1)S(1)}, f32[1,192]{1,0:T(1,128)S(1)}) custom-call(s32[6]{0:T(128)S(1)} %copy-done.7, bf16[1,4,64,128]{3,2,1,0:T(8,128)(2,1)S(1)} %bitcast.47, bf16[1,4,64,128]{3,2,1,0:T(8,128)(2,1)S(1)} %bitcast.48, ...), custom_call_target="tpu_custom_call" | custom-call | flops 8000001024 | bytes 1024 | tf_op jit(solution)/shard_map/pallas_call | solution.py:95
  197.9 2.9 %collective-permute-done.70.got_y = bf16[2,128,1024]{2,1,0:T(8,128)(2,1)S(1)} collective-permute-done((bf16[2,128,1024]{2,1,0:T(8,128)(2,1)S(1)}, bf16[2,128,1024]{2,1,0:T(8,128)(2,1)S(1)}, u32[]{:S(2)}, u32[]{:S(2)}) %collective-permute-start.70) | collective-permute-done | bytes 524320 | tf_op jit(solution)/shard_map/ppermute | solution.py:851
  200.9 4.3 %collective-permute-done.69.got_z = bf16[2,128,1024]{2,1,0:T(8,128)(2,1)S(1)} collective-permute-done((bf16[2,128,1024]{2,1,0:T(8,128)(2,1)S(1)}, bf16[2,128,1024]{2,1,0:T(8,128)(2,1)S(1)}, u32[]{:S(2)}, u32[]{:S(2)}) %collective-permute-start.69) | collective-permute-done | bytes 524320 | tf_op jit(solution)/shard_map/ppermute | solution.py:851
  219.9 5.0 %collective-permute-done.76.got_ref = bf16[8,192,128]{2,1,0:T(8,128)(2,1)S(1)} collective-permute-done((bf16[8,192,128]{2,1,0:T(8,128)(2,1)S(1)}, bf16[8,192,128]{2,1,0:T(8,128)(2,1)S(1)}, u32[]{:S(2)}, u32[]{:S(2)}) %collective-permute-start.76) | collective-permute-done | bytes 393248 | tf_op jit(solution)/shard_map/ppermute | solution.py:851
  230.1 4.3 %collective-permute-done.82.out_got = bf16[2,32,1024]{2,1,0:T(8,128)(2,1)S(1)} collective-permute-done((bf16[2,32,1024]{2,1,0:T(8,128)(2,1)S(1)}, bf16[2,32,1024]{2,1,0:T(8,128)(2,1)S(1)}, u32[]{:S(2)}, u32[]{:S(2)}) %collective-permute-start.82) | collective-permute-done | bytes 131104 | tf_op jit(solution)/shard_map/ppermute | solution.py:851
  240.1 4.8 %collective-permute-done.86.refs_6_ = bf16[4,56,128]{2,1,0:T(8,128)(2,1)S(1)} collective-permute-done((bf16[4,56,128]{2,1,0:T(8,128)(2,1)S(1)}, bf16[4,56,128]{2,1,0:T(8,128)(2,1)S(1)}, u32[]{:S(2)}, u32[]{:S(2)}) %collective-permute-start.86) | collective-permute-done | bytes 57376 | tf_op jit(solution)/shard_map/ppermute | solution.py:843
  251.9 5.4 %collective-permute-done.92.q2_ref = bf16[4,56,128]{2,1,0:T(8,128)(2,1)S(1)} collective-permute-done((bf16[4,56,128]{2,1,0:T(8,128)(2,1)S(1)}, bf16[4,56,128]{2,1,0:T(8,128)(2,1)S(1)}, u32[]{:S(2)}, u32[]{:S(2)}) %collective-permute-start.92) | collective-permute-done | bytes 57376 | tf_op jit(solution)/shard_map/ppermute | solution.py:847
  259.1 4.2 %collective-permute-done.93.q3_ref = bf16[4,56,128]{2,1,0:T(8,128)(2,1)S(1)} collective-permute-done((bf16[4,56,128]{2,1,0:T(8,128)(2,1)S(1)}, bf16[4,56,128]{2,1,0:T(8,128)(2,1)S(1)}, u32[]{:S(2)}, u32[]{:S(2)}) %collective-permute-start.93) | collective-permute-done | bytes 57376 | tf_op jit(solution)/shard_map/ppermute | solution.py:847
  (244 shorter events, 153.0 us)
Async XLA Ops:
  4.6 12.8 %collective-permute-start.1 = (bf16[128,1024]{1,0:T(8,128)(2,1)}, bf16[128,1024]{1,0:T(8,128)(2,1)S(1)}, u32[]{:S(2)}, u32[]{:S(2)}) collective-permute-start(bf16[128,1024]{1,0:T(8,128)(2,1)} %get-tuple-element.283.refs_0_), channel_id=1, source_target_pairs={{8,0},{16,8},{24,16},{28,24},{20,28},{12,20},{4,12},{0,4},{9,1},{1... | collective-permute-start | bytes 786440 | tf_op jit(solution)/shard_map/ppermute | solution.py:1119
  17.5 14.5 %collective-permute-start.5 = (bf16[128,1024]{1,0:T(8,128)(2,1)S(1)}, bf16[128,1024]{1,0:T(8,128)(2,1)S(1)}, u32[]{:S(2)}, u32[]{:S(2)}) collective-permute-start(bf16[128,1024]{1,0:T(8,128)(2,1)S(1)} %collective-permute-done.refs_1_), channel_id=1, source_target_pairs={{0,8},{8,16},{16,24},{24,28},{28,20},{20,12},{12,4},{4,0},{1,9},{9... | collective-permute-start | bytes 786440 | tf_op jit(solution)/shard_map/ppermute | solution.py:1116
  17.5 14.4 %collective-permute-start.6 = (bf16[128,1024]{1,0:T(8,128)(2,1)S(1)}, bf16[128,1024]{1,0:T(8,128)(2,1)S(1)}, u32[]{:S(2)}, u32[]{:S(2)}) collective-permute-start(bf16[128,1024]{1,0:T(8,128)(2,1)S(1)} %collective-permute-done.1.refs_2_), channel_id=1, source_target_pairs={{8,0},{16,8},{24,16},{28,24},{20,28},{12,20},{4,12},{0,4},{9,1},{1... | collective-permute-start | bytes 786440 | tf_op jit(solution)/shard_map/ppermute | solution.py:1119
  44.3 14.2 %collective-permute-start.21 = (bf16[2,128,1024]{2,1,0:T(8,128)(2,1)S(1)}, bf16[2,128,1024]{2,1,0:T(8,128)(2,1)S(1)}, u32[]{:S(2)}, u32[]{:S(2)}) collective-permute-start(bf16[2,128,1024]{2,1,0:T(8,128)(2,1)S(1)} %shard_map.192), channel_id=1, source_target_pairs={{0,2},{2,0},{1,3},{3,1},{4,6},{6,4},{5,7},{7,5},{8,10},{10,8},{9,1... | collective-permute-start | bytes 1572872 | tf_op jit(solution)/shard_map/ppermute | solution.py:851
  67.7 13.7 %collective-permute-start.31 = (bf16[256,512]{1,0:T(8,128)(2,1)S(1)}, bf16[256,512]{1,0:T(8,128)(2,1)S(1)}, u32[]{:S(2)}, u32[]{:S(2)}) collective-permute-start(bf16[256,512]{1,0:T(8,128)(2,1)S(1)} %shard_map.195.refs_14_), channel_id=1, source_target_pairs={{0,16},{16,0},{1,17},{17,1},{2,18},{18,2},{3,19},{19,3},{4,20},{20... | collective-permute-start | bytes 786440 | tf_op jit(solution)/shard_map/ppermute | solution.py:851
  68.8 12.6 %collective-permute-start.32 = (bf16[128,1024]{1,0:T(8,128)(2,1)S(1)}, bf16[128,1024]{1,0:T(8,128)(2,1)S(1)}, u32[]{:S(2)}, u32[]{:S(2)}) collective-permute-start(bf16[128,1024]{1,0:T(8,128)(2,1)S(1)} %bitcast.34), channel_id=1, source_target_pairs={{0,4},{4,0},{1,5},{5,1},{2,6},{6,2},{3,7},{7,3},{8,12},{12,8},{9,1... | collective-permute-start | bytes 786440 | tf_op jit(solution)/shard_map/ppermute | solution.py:851
  81.4 13.2 %collective-permute-start.38 = (bf16[8,32,1024]{2,1,0:T(8,128)(2,1)S(1)}, bf16[8,32,1024]{2,1,0:T(8,128)(2,1)S(1)}, u32[]{:S(2)}, u32[]{:S(2)}) collective-permute-start(bf16[8,32,1024]{2,1,0:T(8,128)(2,1)S(1)} %shard_map.196.refs_0_), channel_id=1, source_target_pairs={{0,2},{2,0},{1,3},{3,1},{4,6},{6,4},{5,7},{7,5},{8,10},{10,8},{9,1... | collective-permute-start | bytes 1572872 | tf_op jit(solution)/shard_map/ppermute | solution.py:851
  81.5 14.3 %collective-permute-start.36 = (bf16[8,32,1024]{2,1,0:T(8,128)(2,1)S(1)}, bf16[8,32,1024]{2,1,0:T(8,128)(2,1)S(1)}, u32[]{:S(2)}, u32[]{:S(2)}) collective-permute-start(bf16[8,32,1024]{2,1,0:T(8,128)(2,1)S(1)} %shard_map.196.refs_0_), channel_id=1, source_target_pairs={{0,4},{4,0},{1,5},{5,1},{2,6},{6,2},{3,7},{7,3},{8,12},{12,8},{9,1... | collective-permute-start | bytes 1572872 | tf_op jit(solution)/shard_map/ppermute | solution.py:851
  82.3 12.3 %collective-permute-start.37 = (bf16[256,512]{1,0:T(8,128)(2,1)S(1)}, bf16[256,512]{1,0:T(8,128)(2,1)S(1)}, u32[]{:S(2)}, u32[]{:S(2)}) collective-permute-start(bf16[256,512]{1,0:T(8,128)(2,1)S(1)} %shard_map.195.refs_14_), channel_id=1, source_target_pairs={{0,1},{1,0},{2,3},{3,2},{4,5},{5,4},{6,7},{7,6},{8,9},{9,8},{10,11... | collective-permute-start | bytes 786440 | tf_op jit(solution)/shard_map/ppermute | solution.py:851
  99.2 16.6 %collective-permute-start.44 = (bf16[3,128,1024]{2,1,0:T(8,128)(2,1)S(1)}, bf16[3,128,1024]{2,1,0:T(8,128)(2,1)S(1)}, u32[]{:S(2)}, u32[]{:S(2)}) collective-permute-start(bf16[3,128,1024]{2,1,0:T(8,128)(2,1)S(1)} %shard_map.199), channel_id=1, source_target_pairs={{0,2},{2,0},{1,3},{3,1},{4,6},{6,4},{5,7},{7,5},{8,10},{10,8},{9,1... | collective-permute-start | bytes 2359304 | tf_op jit(solution)/shard_map/ppermute | solution.py:851
  100.3 14.2 %collective-permute-start.43 = (bf16[256,512]{1,0:T(8,128)(2,1)S(1)}, bf16[256,512]{1,0:T(8,128)(2,1)S(1)}, u32[]{:S(2)}, u32[]{:S(2)}) collective-permute-start(bf16[256,512]{1,0:T(8,128)(2,1)S(1)} %copy-done.6), channel_id=1, source_target_pairs={{0,16},{16,0},{1,17},{17,1},{2,18},{18,2},{3,19},{19,3},{4,20},{20... | collective-permute-start | bytes 786440 | tf_op jit(solution)/shard_map/ppermute | solution.py:851
  100.3 14.2 %collective-permute-start.41 = (bf16[128,1024]{1,0:T(8,128)(2,1)S(1)}, bf16[128,1024]{1,0:T(8,128)(2,1)S(1)}, u32[]{:S(2)}, u32[]{:S(2)}) collective-permute-start(bf16[128,1024]{1,0:T(8,128)(2,1)S(1)} %get-tuple-element.359.refs_0_.refs_7_), channel_id=1, source_target_pairs={{0,4},{4,0},{1,5},{5,1},{2,6},{6,2},{3,7},{7,3},{8,12},{12,8},{9,1... | collective-permute-start | bytes 786440 | tf_op jit(solution)/shard_map/ppermute | solution.py:851
  101.3 14.5 %collective-permute-start.40 = (bf16[128,1024]{1,0:T(8,128)(2,1)S(1)}, bf16[128,1024]{1,0:T(8,128)(2,1)S(1)}, u32[]{:S(2)}, u32[]{:S(2)}) collective-permute-start(bf16[128,1024]{1,0:T(8,128)(2,1)S(1)} %get-tuple-element.359.refs_0_.refs_7_), channel_id=1, source_target_pairs={{0,8},{8,0},{1,9},{9,1},{2,10},{10,2},{3,11},{11,3},{4,12},{12,4},... | collective-permute-start | bytes 786440 | tf_op jit(solution)/shard_map/ppermute | solution.py:851
  159.2 12.9 %collective-permute-start.62 = (bf16[264,512]{1,0:T(8,128)(2,1)S(1)}, bf16[264,512]{1,0:T(8,128)(2,1)S(1)}, u32[]{:S(2)}, u32[]{:S(2)}) collective-permute-start(bf16[264,512]{1,0:T(8,128)(2,1)S(1)} %get-tuple-element.418), channel_id=1, source_target_pairs={{0,1},{1,0},{2,3},{3,2},{4,5},{5,4},{6,7},{7,6},{8,9},{9,8},{10,11... | collective-permute-start | bytes 811016 | tf_op jit(solution)/shard_map/ppermute | solution.py:851
  160.1 12.1 %collective-permute-start.63 = (bf16[512,192]{1,0:T(8,128)(2,1)S(1)}, bf16[512,192]{1,0:T(8,128)(2,1)S(1)}, u32[]{:S(2)}, u32[]{:S(2)}) collective-permute-start(bf16[512,192]{1,0:T(8,128)(2,1)S(1)} %get-tuple-element.420), channel_id=1, source_target_pairs={{0,16},{16,0},{1,17},{17,1},{2,18},{18,2},{3,19},{19,3},{4,20},{20... | collective-permute-start | bytes 589832 | tf_op jit(solution)/shard_map/ppermute | solution.py:851
  183.8 14.1 %collective-permute-start.71 = (bf16[128,1024]{1,0:T(8,128)(2,1)S(1)}, bf16[128,1024]{1,0:T(8,128)(2,1)S(1)}, u32[]{:S(2)}, u32[]{:S(2)}) collective-permute-start(bf16[128,1024]{1,0:T(8,128)(2,1)S(1)} %get-tuple-element.455), channel_id=1, source_target_pairs={{0,1},{1,0},{2,3},{3,2},{4,5},{5,4},{6,7},{7,6},{8,9},{9,8},{10,11... | collective-permute-start | bytes 786440 | tf_op jit(solution)/shard_map/ppermute | solution.py:851
  185.0 12.9 %collective-permute-start.72 = (bf16[512,192]{1,0:T(8,128)(2,1)S(1)}, bf16[512,192]{1,0:T(8,128)(2,1)S(1)}, u32[]{:S(2)}, u32[]{:S(2)}) collective-permute-start(bf16[512,192]{1,0:T(8,128)(2,1)S(1)} %collective-permute-done.63.refs_1_), channel_id=1, source_target_pairs={{0,1},{1,0},{2,3},{3,2},{4,5},{5,4},{6,7},{7,6},{8,9},{9,8},{10,11... | collective-permute-start | bytes 589832 | tf_op jit(solution)/shard_map/ppermute | solution.py:851
  185.8 26.8 %collective-permute-start.75 = (bf16[264,512]{1,0:T(8,128)(2,1)S(1)}, bf16[264,512]{1,0:T(8,128)(2,1)S(1)}, u32[]{:S(2)}, u32[]{:S(2)}) collective-permute-start(bf16[264,512]{1,0:T(8,128)(2,1)S(1)} %shard_map.211), channel_id=1, source_target_pairs={{0,16},{16,0},{1,17},{17,1},{2,18},{18,2},{3,19},{19,3},{4,20},{20... | collective-permute-start | bytes 811016 | tf_op jit(solution)/shard_map/ppermute | solution.py:851
  188.5 16.7 %collective-permute-start.69 = (bf16[2,128,1024]{2,1,0:T(8,128)(2,1)S(1)}, bf16[2,128,1024]{2,1,0:T(8,128)(2,1)S(1)}, u32[]{:S(2)}, u32[]{:S(2)}) collective-permute-start(bf16[2,128,1024]{2,1,0:T(8,128)(2,1)S(1)} %get-tuple-element.445), channel_id=1, source_target_pairs={{0,8},{8,0},{1,9},{9,1},{2,10},{10,2},{3,11},{11,3},{4,12},{12,4},... | collective-permute-start | bytes 1572872 | tf_op jit(solution)/shard_map/ppermute | solution.py:851
  207.5 17.4 %collective-permute-start.76 = (bf16[8,192,128]{2,1,0:T(8,128)(2,1)S(1)}, bf16[8,192,128]{2,1,0:T(8,128)(2,1)S(1)}, u32[]{:S(2)}, u32[]{:S(2)}) collective-permute-start(bf16[8,192,128]{2,1,0:T(8,128)(2,1)S(1)} %get-tuple-element.474), channel_id=1, source_target_pairs={{0,16},{16,0},{1,17},{17,1},{2,18},{18,2},{3,19},{19,3},{4,20},{20... | collective-permute-start | bytes 1179656 | tf_op jit(solution)/shard_map/ppermute | solution.py:851
  236.1 27.2 %collective-permute-start.90 = (bf16[160,1024]{1,0:T(8,128)(2,1)S(1)}, bf16[160,1024]{1,0:T(8,128)(2,1)S(1)}, u32[]{:S(2)}, u32[]{:S(2)}) collective-permute-start(bf16[160,1024]{1,0:T(8,128)(2,1)S(1)} %get-tuple-element.519), channel_id=1, source_target_pairs={{0,16},{16,0},{1,17},{17,1},{2,18},{18,2},{3,19},{19,3},{4,20},{20... | collective-permute-start | bytes 983048 | tf_op jit(solution)/shard_map/ppermute | solution.py:851
  247.9 15.5 %collective-permute-start.91 = (bf16[4,216,128]{2,1,0:T(8,128)(2,1)S(1)}, bf16[4,216,128]{2,1,0:T(8,128)(2,1)S(1)}, u32[]{:S(2)}, u32[]{:S(2)}) collective-permute-start(bf16[4,216,128]{2,1,0:T(8,128)(2,1)S(1)} %get-tuple-element.529), channel_id=1, source_target_pairs={{0,8},{8,0},{16,24},{24,16},{1,9},{9,1},{17,25},{25,17},{2,10},{10... | collective-permute-start | bytes 663560 | tf_op jit(solution)/shard_map/ppermute | solution.py:847
  248.0 15.4 %collective-permute-start.89 = (bf16[64,1024]{1,0:T(8,128)(2,1)S(1)}, bf16[64,1024]{1,0:T(8,128)(2,1)S(1)}, u32[]{:S(2)}, u32[]{:S(2)}) collective-permute-start(bf16[64,1024]{1,0:T(8,128)(2,1)S(1)} %get-tuple-element.513), channel_id=1, source_target_pairs={{0,8},{8,0},{1,9},{9,1},{2,10},{10,2},{3,11},{11,3},{4,12},{12,4},... | collective-permute-start | bytes 393224 | tf_op jit(solution)/shard_map/ppermute | solution.py:851
  250.0 13.4 %collective-permute-start.88 = (bf16[64,1024]{1,0:T(8,128)(2,1)S(1)}, bf16[64,1024]{1,0:T(8,128)(2,1)S(1)}, u32[]{:S(2)}, u32[]{:S(2)}) collective-permute-start(bf16[64,1024]{1,0:T(8,128)(2,1)S(1)} %get-tuple-element.512), channel_id=1, source_target_pairs={{0,4},{4,0},{1,5},{5,1},{2,6},{6,2},{3,7},{7,3},{8,12},{12,8},{9,1... | collective-permute-start | bytes 393224 | tf_op jit(solution)/shard_map/ppermute | solution.py:851
  (85 other events, 863.2 us)

commit v3 on v2

--- a/solution.py
+++ b/solution.py
@@ -758,34 +758,60 @@
     keep_out[...] = dot(lhs_ref[:middle, :], rhs_ref[...], NT)
 
 
-def blend_kernel(*refs):
-    ups, qkvs, (up_keep, *outs) = refs[:4], refs[4:8], refs[8:]
-    tall = qkvs[0].shape[1]
-    rows = ups[0].shape[1]
+def blocks(count):
+    return [(slice(at * 2 * HD, (at + 1) * 2 * HD), at * 4 // count, at % (count // 4)) for at in range(count)]
+
+
+def spread_both_kernel(table, keep_ref, got_ref, share_ref, send_z, both_ref, top_out, low_out, send_y):
+    spread_kernel(table, keep_ref, got_ref, send_z, send_y, top_out, low_out)
+    tall, rows = share_ref.shape[1], send_y.shape[1]
+    both_ref[:, :tall] = share_ref[...]
+    for lanes, run, at in blocks(send_y.shape[2] // (2 * HD)):
+        for high in range(2):
+            first = tall + (2 * at + high) * rows
+            both_ref[run, first : first + rows] = send_y[high, :, lanes]
+
+
+def blend_kernel(_, top_ref, got_z, low_ref, both_ref, *refs):
+    ups, qkvs, own_ref, got_ref = refs[:4], (refs[4], refs[5], both_ref, refs[6]), refs[7], refs[8]
+    send_y, top_out, low_out, up_keep, *outs = refs[9:]
+    tall, rows, part = refs[4].shape[1], ups[0].shape[1], own_ref.shape[1] // 4
+    half = top_out.shape[0]
+    top_out[...] = top_ref[0] + got_z[0].astype(F32)
+    send_y[...] = (top_ref[1] + got_z[1].astype(F32)).astype(BF)
+    after_ups = tall + rows * (ups[0].shape[2] // (2 * HD))
+    for lanes, run, at in blocks(low_out.shape[1] // (2 * HD)):
+        first = tall + 2 * at * half
+        low_out[:, lanes] = low_ref[0, :, lanes] + both_ref[run, first : first + half].astype(F32)
+        got = both_ref[run, first + half : first + 2 * half].astype(F32)
+        to = after_ups + at * half
+        outs[1][run, to : to + half] = (low_ref[1, :, lanes] + got).astype(BF)
     for near in range(4):
         up_keep[near] = ups[near][0]
         for far, out in enumerate(outs):
-            out[near, :tall] = qkvs[near][far]
+            out[near, :tall] = qkvs[near][far, :tall]
         for at in range(ups[0].shape[2] // (2 * HD)):
             first = tall + at * rows
             outs[1][near, first : first + rows] = ups[near][1, :, at * 2 * HD : (at + 1) * 2 * HD]
-
-
-def sums_kernel(one_ref, two_ref, out_own, out_got, send_out, keep_out):
-    rows = one_ref.shape[0]
-    send_out[:rows] = (one_ref[...].astype(F32) + two_ref[...].astype(F32)).astype(BF)
-    send_out[rows:] = (out_own[1].astype(F32) + out_got[1].astype(F32)).astype(BF)
-    keep_out[...] = out_own[0].astype(F32) + out_got[0].astype(F32)
+        here = slice(near * part, (near + 1) * part)
+        total = (own_ref[1, here].astype(F32) + got_ref[1, here].astype(F32)).astype(BF)
+        for at in range(own_ref.shape[2] // (2 * HD)):
+            first = tall + at * part
+            outs[2][near, first : first + part] = total[:, at * 2 * HD : (at + 1) * 2 * HD]
 
 
 def end_kernel(
-    table, keep_top, got_top, keep_low, got_low, mid_delta_ref, hidden_ref, gain1_ref, bias1_ref, gain2_ref, bias2_ref,
-    q0_ref, q1_ref, q2_ref, q3_ref, qkv_ref, up_one, up_ref, down_keep, out_keep, got_ref,
+    table, keep_top, got_top, keep_low, mid_delta_ref, hidden_ref, gain1_ref, bias1_ref, gain2_ref, bias2_ref,
+    q0_ref, q1_ref, q2_ref, q3_ref, qkv_ref, up_one, up_ref, down_ref, down_near, down_got, out_own, out_got,
     grad_out, qkv_out, qkv_gain, qkv_bias, up_out, up_gain, up_bias, down_out, out_out,
-    all_ref, up_two, sum_ref,
+    all_ref, up_two, sum_ref, got_low,
 ):
+    tall, rows, half = q0_ref.shape[1], up_one.shape[1], got_low.shape[0]
+    after_ups = tall + rows * (up_one.shape[2] // (2 * HD))
+    for lanes, run, at in blocks(got_low.shape[1] // (2 * HD)):
+        first = after_ups + at * half
+        got_low[:, lanes] = q1_ref[run, first : first + half]
     last_kernel(table, keep_top, got_top, keep_low, got_low, mid_delta_ref, hidden_ref, gain1_ref, grad_out)
-    tall, rows = q0_ref.shape[1], up_one.shape[1]
     for near in range(4):
         for at in range(up_one.shape[2] // (2 * HD)):
             first = tall + at * rows
@@ -796,9 +822,15 @@
     up_end_kernel(
         table, up_one, up_two, up_ref, gain2_ref, bias2_ref, up_out, up_gain, up_bias, sum_ref, runs=2, wide=2
     )
-    rows = down_keep.shape[0]
-    down_out[...] = down_keep[...] + got_ref[:rows].astype(F32)
-    out_out[...] = out_keep[...] + got_ref[rows:].astype(F32)
+    down_out[...] = down_ref[...].astype(F32) + down_near[...].astype(F32) + down_got[...].astype(F32)
+    part = out_own.shape[1] // 4
+    for near in range(4):
+        rows = slice(near * part, (near + 1) * part)
+        keep = out_own[0, rows].astype(F32) + out_got[0, rows].astype(F32)
+        for at in range(out_own.shape[2] // (2 * HD)):
+            first = tall + at * part
+            lanes = slice(at * 2 * HD, (at + 1) * 2 * HD)
+            out_out[rows, lanes] = keep[:, lanes] + q2_ref[near, first : first + part].astype(F32)
 
 
 def last_kernel(_, keep_top, got_top, keep_low, got_low, mid_delta_ref, hidden_ref, gain_ref, out_ref):
@@ -870,9 +902,11 @@
     return call(spread_kernel, (table, keep, got), [((2, *shape), BF)] * 2 + [((2, *shape), F32)] * 2)
 
 
-def narrow(table, top, got_z, low, got_y):
+def narrow(table, top, got_z, low, got_y, micros=0):
     shape = top.shape[1:]
-    return call(narrow_kernel, (table, top, got_z, low, got_y), [(shape, BF)] * 2 + [(shape, F32)] * 2)
+    return call(
+        narrow_kernel, (table, top, got_z, low, got_y), [(shape, BF)] * 2 + [(shape, F32)] * 2, micros=micros
+    )
 
 
 def add(one, two, kind):
@@ -1188,75 +1222,96 @@
     got_z, got_y, *up_parts = meet(swap(send_z, "zl"), swap(send_y, "y"), *up_parts)
     send_y, send_z, top, low = narrow(s.table, top, got_z, low, got_y)
     down_parts = s.down_gradient(after(acts, send_y), grads)
-    end_top, end_low, up_far, *down_parts = meet(
-        swap(send_y, "y"), swap(send_z, "zl"), swap(after(up_parts[3], send_y), "x"), *down_parts
-    )
+    end_top, end_low, *down_parts = meet(swap(send_y, "y"), swap(send_z, "zl"), *down_parts)
     mid_delta, mid_delta_b, by_head = s.turn(mid, w_out, (top, end_top, low, end_low))
-    *got, up_near, mate_1 = meet(
+    keep, send = s.out_gradient(after(lay_keep, mid_delta), lay_send, attended, mid_delta_b)
+    *got, up_far, mate_1, keep, send = meet(
         *near(by_head),
-        swap(after(up_parts[2], mid_delta), "x"),
+        swap(after(up_parts[3], mid_delta), "x"),
         swap(after(w_head[1], mid_delta), "zh"),
+        keep,
+        send,
     )
     by_head = mix([by_head[0], *got])
     up_shape = up_parts[0].shape
     (up_send,) = call(up_add_kernel, (up_parts[1], after(up_far, by_head[0])), [(up_shape, BF)], smem=0)
-    keep, send = s.out_gradient(after(lay_keep, by_head[0]), lay_send, attended, mid_delta_b)
     *got, send, down_far, up_send = meet(
-        *far(by_head), swap(send, "c"), swap(after(down_parts[3], by_head[0]), "x"), up_send
+        *far(by_head), swap(after(send, by_head[0]), "c"), swap(after(down_parts[3], by_head[0]), "x"), up_send
     )
 
     douts = [array[None] for array in (by_head[0], *got)]
     send_z, send_y, top, low = spread(s.table, keep, send)
     got_z, got_y = swap(send_z, "zl"), swap(send_y, "y")
-    up_got = swap(up_send, "zh")
-    down_near = swap(after(down_parts[2], send), "x")
-    mate_2 = swap(after(mate_1, send), "x")
+    up_got = swap(after(up_send, send_z), "zh")
+    up_near = swap(after(up_parts[2], send_z), "x")
+    mate_2 = swap(after(mate_1, send_z), "x")
     kept = (after(kept[0], send_z), *kept[1:])
     to_own, to_mate, by_shard, sums = s.backward(kept, douts)
     from_mate = swap(to_mate, "zh")
-    to_own, got_z, got_y, down_near, mate_2 = meet(to_own, got_z, got_y, down_near, mate_2)
+    qkv_own, qkv_send = s.qkv_gradient(pieces, others, by_shard, sums)
+    to_own, got_z, got_y, up_near, mate_2, up_got, qkv_send = meet(
+        to_own, got_z, got_y, up_near, mate_2, up_got, qkv_send
+    )
     send_y, send_z, top, low = narrow(s.table, top, got_z, low, got_y)
-    (up_keep,) = call(up_add_kernel, (up_parts[0], after(up_near, to_own)), [(up_shape, BF)], smem=0)
-    qkv_own, qkv_send = s.qkv_gradient(pieces, others, after(by_shard, send_y), sums)
-    end_top, end_low, qkv_send, up_got = meet(
-        swap(send_y, "y"), swap(send_z, "zl"), qkv_send, up_got
-    )
-    ups = s.up_share(up_keep, up_got)
-    ends = top, end_top, low, end_low
-    down_keep = add(down_parts[0], after(down_near, end_top), F32)
-    from_mate, qkv_got, *got = meet(from_mate, swap(after(qkv_send, end_top), "x"), *near(ups))
+    down_send = add(down_parts[1], after(down_far, send_y), BF)
+    (up_keep,) = call(up_add_kernel, (up_parts[0], after(up_near, send_y)), [(up_shape, BF)], smem=0)
+    end_top, end_low, qkv_got, down_send, up_keep = meet(
+        swap(send_y, "y"), swap(send_z, "zl"), swap(qkv_send, "x"), down_send, up_keep
+    )
+    qkv = s.qkv_share(qkv_own, qkv_got)
+    ups = s.up_share(after(up_keep, qkv_got), up_got)
+    layer_out, *outs = s.outputs(mid, (top, end_top, low, end_low))
+    from_mate, *ups = meet(from_mate, *ups)
     keep, send = s.inputs(to_own, from_mate, w_head[0], [mate_1, mate_2])
-    layer_out, *outs = s.outputs(mid, ends)
-    qkv = s.qkv_share(qkv_own, after(qkv_got, send))
-    send, out_got, *qkv = meet(swap(send, "c"), swap(after(outs[1], send), "x"), *qkv)
-
-    send_z, send_y, top, low = spread(s.table, keep, send)
-    last_send, out_keep = call(
-        sums_kernel,
-        (after(down_parts[1], send_z), down_far, outs[0], out_got),
-        [((s.ffn + s.wrows, s.width), BF), ((s.wrows, s.width), F32)],
-        smem=0,
-    )
-    last_got = swap(last_send, "zh")
-    got_z, got_y, *more = meet(
-        swap(send_z, "zl"), swap(send_y, "y"), *near([after(a, send_z) for a in qkv])
-    )
-    send_y, send_z, top, low = narrow(s.table, top, got_z, low, got_y)
-    piece = ((4, s.qkv_tall, 2 * HD), BF)
-    tall = s.qkv_tall + s.up_tall * s.cols // (2 * HD)
-    up_keep, *qkv = call(
+    send, qkv_c, *got = meet(
+        swap(send, "c"), lax.ppermute(after(qkv[1], send), ("y", "c"), apart(4, 1)), *near([after(a, send) for a in ups])
+    )
+
+    lines = 2 * HD
+    half = (s.many // 8, s.width)
+    quarter = s.half * s.width // (4 * lines)
+    piece = ((4, s.qkv_tall, lines), BF)
+    send_z, both, top, low = call(
+        spread_both_kernel,
+        (s.table, keep, send, qkv[2]),
+        [
+            ((2, s.half, s.width), BF),
+            ((4, s.qkv_tall + 2 * quarter, lines), BF),
+            ((2, s.half, s.width), F32),
+            ((2, s.half, s.width), F32),
+        ],
+        [((2, s.half, s.width), BF)],
+    )
+    got_z, both, down_got, out_got, qkv_yc = meet(
+        swap(send_z, "zl"),
+        swap(both, "y"),
+        swap(after(down_send, send_z), "zh"),
+        swap(after(outs[1], send_z), "x"),
+        lax.ppermute(after(qkv[3], send_z), ("y", "c"), apart(4, 3)),
+    )
+    send_y, top, low, up_keep, *qkv = call(
         blend_kernel,
-        (after(ups[0], send_y), *got, qkv[0], *more),
-        [((4, s.up_tall, s.cols), BF), piece, ((4, tall, 2 * HD), BF), piece, piece],
-        smem=0,
-    )
-    end_top, end_low, last_got, *more = meet(swap(send_y, "y"), swap(send_z, "zl"), last_got, *far(qkv))
+        (s.table, top, got_z, low, both, *ups[:1], *got, qkv[0], qkv_c, qkv_yc, outs[0], out_got),
+        [
+            ((s.half, s.width), BF),
+            ((s.half, s.width), F32),
+            ((s.half, s.width), F32),
+            ((4, s.up_tall, s.cols), BF),
+            piece,
+            ((4, s.qkv_tall + s.up_tall * s.cols // lines + quarter, lines), BF),
+            ((4, s.qkv_tall + s.wrows * s.width // (4 * lines), lines), BF),
+            piece,
+        ],
+    )
+    end_top, down_near, *more = meet(
+        swap(send_y, "y"), swap(after(down_parts[2], send_y), "x"), *far(qkv)
+    )
     line = ((1, s.wrows), F32)
     outs = call(
         end_kernel,
         (
-            s.table, top, end_top, low, end_low, mid_delta, s.hidden, s.gain1, s.bias1, s.gain2, s.bias2,
-            qkv[0], *more, s.qkv, up_keep, s.up, down_keep, out_keep, last_got,
+            s.table, top, end_top, low, mid_delta, s.hidden, s.gain1, s.bias1, s.gain2, s.bias2,
+            qkv[0], *more, s.qkv, up_keep, s.up, down_parts[0], down_near, down_got, outs[0], out_got,
         ),
         [
             ((s.rows, s.width), BF),
@@ -1269,6 +1324,7 @@
             ((HEADS, s.qkv_tall, 2 * HD), BF),
             ((4, s.up_tall, s.cols), BF),
             ((1, s.up.shape[1]), F32),
+            ((s.half, s.width), BF),
         ],
     )
     return results(layer_out, outs[0], outs[1:4], outs[8], outs[4:7], outs[7])

time: 269 us -> 261 us (0.970)
  waiting for transfers between devices: 126 us -> 116 us
    ppermute x53 -> x52, waiting for transfers between devices: 69.8 us -> 60.5 us  [swap(): return lax.ppermute(array, axis, SWAP)]
    ppermute x0 -> x2, waiting for transfers between devices: none -> 5.17 us  [the longest x1 4.28 us: local(): lax.ppermute(after(qkv[3], send_z), ('y', 'c'), apart(4, 3))]
    ppermute x18 -> x15, waiting for transfers between devices: 25.9 us -> 22.1 us  [near(): lax.ppermute(arrays[at], ('y', 'c'), apart(4, at))]
    ppermute x18 -> x15, starting transfers between devices: 10.9 us -> 9.46 us  [near(): lax.ppermute(arrays[at], ('y', 'c'), apart(4, at))]
    ppermute x53 -> x52, starting transfers between devices: 45.9 us -> 46.5 us  [swap(): return lax.ppermute(array, axis, SWAP)]
    pallas_call x41 -> x39, Pallas kernels: 46.3 us -> 46.4 us  [call(): pl.pallas_call(body, out_shape=[jax.ShapeDtypeStruct(shape, kind) for sha...]
  transfers between devices with their start and end apart: 94 -> 92, of which waited for: 45 -> 46; matrix products, arithmetic and copies ran while one was open for 1% -> 1% of each run, Pallas kernels for 9% -> 10%
where the time goes in v3:
time: 261 us; the launch traced here: 258 us
  waiting for transfers between devices  116 us (44%)
  starting transfers between devices  88.9 us (34%)
  Pallas kernels  46.4 us (18%)
    ppermute x52, waiting for transfers between devices, swap(): return lax.ppermute(array, axis, SWAP)  60.5 us
    ppermute x52, starting transfers between devices, swap(): return lax.ppermute(array, axis, SWAP)  46.5 us
    pallas_call x39, Pallas kernels, call(): pl.pallas_call(body, out_shape=[jax.ShapeDtypeStruct(shape, kind) for sha...  46.4 us
    ppermute x12, waiting for transfers between devices, far(): lax.ppermute(arrays[at], ('zh', 'zl'), apart(4, at))  24.7 us
    ppermute x15, waiting for transfers between devices, near(): lax.ppermute(arrays[at], ('y', 'c'), apart(4, at))  22.1 us
    ppermute x12, starting transfers between devices, far(): lax.ppermute(arrays[at], ('zh', 'zl'), apart(4, at))  18.5 us
    ppermute x15, starting transfers between devices, near(): lax.ppermute(arrays[at], ('y', 'c'), apart(4, at))  9.46 us
    ppermute x4, starting transfers between devices, behind(): return lax.ppermute(array, CHIPS, left)  7.45 us
  transfers between devices with their start and end apart: 92, of which 46 were waited for; matrix products, arithmetic and copies ran while one was open for 1% of the time, Pallas kernels for 10%

profile of v3, /device:TPU:0, one launch (start us, length us, event | category | flops | bytes accessed | tf_op | source)
XLA Modules:
  0.0 258.3 jit_solution(10239101897082093766)
XLA Ops:
  1.3 3.3 %shard_map.186 = (bf16[128,1024]{1,0:T(8,128)(2,1)}, bf16[4,56,128]{2,1,0:T(8,128)(2,1)}, bf16[4,56,128]{2,1,0:T(8,128)(2,1)}, bf16[4,56,128]{2,1,0:T(8,128)(2,1...) custom-call(s32[6]{0:T(128)} %stack.24.table._, ...), custom_call_target="tpu_custom_call" | custom-call | flops 1000 | bytes 1024 | tf_op jit(solution)/shard_map/pallas_call | solution.py:95
  4.6 3.0 %collective-permute-start.1 = (bf16[128,1024]{1,0:T(8,128)(2,1)}, bf16[128,1024]{1,0:T(8,128)(2,1)S(1)}, u32[]{:S(2)}, u32[]{:S(2)}) collective-permute-start(bf16[128,1024]{1,0:T(8,128)(2,1)} %get-tuple-element.283.refs_0_), channel_id=1, source_target_pairs={{8,0},{16,8},{24,16},{28,24},{20,28},{12,20},{4,12},{0,4},{9,1},{1... | collective-permute-start | bytes 786440 | tf_op jit(solution)/shard_map/ppermute | solution.py:1153
  9.8 7.6 %collective-permute-done.3.refs_2_ = bf16[4,56,128]{2,1,0:T(8,128)(2,1)S(1)} collective-permute-done((bf16[4,56,128]{2,1,0:T(8,128)(2,1)}, bf16[4,56,128]{2,1,0:T(8,128)(2,1)S(1)}, u32[]{:S(2)}, u32[]{:S(2)}) %collective-permute-start.3) | collective-permute-done | bytes 57376 | tf_op jit(solution)/shard_map/ppermute | solution.py:875
  20.6 2.9 %collective-permute-start.8 = (bf16[4,56,128]{2,1,0:T(8,128)(2,1)S(1)}, bf16[4,56,128]{2,1,0:T(8,128)(2,1)S(1)}, u32[]{:S(2)}, u32[]{:S(2)}) collective-permute-start(bf16[4,56,128]{2,1,0:T(8,128)(2,1)S(1)} %get-tuple-element.294), channel_id=1, source_target_pairs={{0,16},{8,24},{16,0},{24,8},{1,17},{9,25},{17,1},{25,9},{2,18},{10... | collective-permute-start | bytes 172040 | tf_op jit(solution)/shard_map/ppermute | solution.py:879
  24.9 3.6 %collective-permute-done.7.refs_1_ = bf16[4,56,128]{2,1,0:T(8,128)(2,1)S(1)} collective-permute-done((bf16[4,56,128]{2,1,0:T(8,128)(2,1)S(1)}, bf16[4,56,128]{2,1,0:T(8,128)(2,1)S(1)}, u32[]{:S(2)}, u32[]{:S(2)}) %collective-permute-start.7) | collective-permute-done | bytes 57376 | tf_op jit(solution)/shard_map/ppermute | solution.py:879
  29.0 2.9 %collective-permute-done.9.refs_3_ = bf16[4,56,128]{2,1,0:T(8,128)(2,1)S(1)} collective-permute-done((bf16[4,56,128]{2,1,0:T(8,128)(2,1)S(1)}, bf16[4,56,128]{2,1,0:T(8,128)(2,1)S(1)}, u32[]{:S(2)}, u32[]{:S(2)}) %collective-permute-start.9) | collective-permute-done | bytes 57376 | tf_op jit(solution)/shard_map/ppermute | solution.py:879
  58.6 6.8 %shard_map.193 = (bf16[4,64,128]{2,1,0:T(8,128)(2,1)S(1)}, bf16[4,64,128]{2,1,0:T(8,128)(2,1)S(1)}, bf16[4,64,128]{2,1,0:T(8,128)(2,1)S(1)}, bf16[4,64,128]{2,1,...) custom-call(s32[6]{0:T(128)S(1)} %copy-done.7, ...), custom_call_target="tpu_custom_call" | custom-call | flops 7000001024 | bytes 1024 | tf_op jit(solution)/shard_map/pallas_call | solution.py:95
  73.2 5.3 %collective-permute-done.28.refs_2_ = bf16[4,64,128]{2,1,0:T(8,128)(2,1)S(1)} collective-permute-done((bf16[4,64,128]{2,1,0:T(8,128)(2,1)S(1)}, bf16[4,64,128]{2,1,0:T(8,128)(2,1)S(1)}, u32[]{:S(2)}, u32[]{:S(2)}) %collective-permute-start.28) | collective-permute-done | bytes 65568 | tf_op jit(solution)/shard_map/ppermute | solution.py:875
  78.5 2.9 %collective-permute-done.31.refs_15_ = bf16[256,512]{1,0:T(8,128)(2,1)S(1)} collective-permute-done((bf16[256,512]{1,0:T(8,128)(2,1)S(1)}, bf16[256,512]{1,0:T(8,128)(2,1)S(1)}, u32[]{:S(2)}, u32[]{:S(2)}) %collective-permute-start.31) | collective-permute-done | bytes 262176 | tf_op jit(solution)/shard_map/ppermute | solution.py:883
  83.5 2.9 %collective-permute-start.34 = (bf16[4,64,128]{2,1,0:T(8,128)(2,1)S(1)}, bf16[4,64,128]{2,1,0:T(8,128)(2,1)S(1)}, u32[]{:S(2)}, u32[]{:S(2)}) collective-permute-start(bf16[4,64,128]{2,1,0:T(8,128)(2,1)S(1)} %get-tuple-element.347), channel_id=1, source_target_pairs={{0,16},{8,24},{16,0},{24,8},{1,17},{9,25},{17,1},{25,9},{2,18},{10... | collective-permute-start | bytes 196616 | tf_op jit(solution)/shard_map/ppermute | solution.py:879
  90.9 3.7 %collective-permute-done.35.refs_7_ = bf16[4,64,128]{2,1,0:T(8,128)(2,1)S(1)} collective-permute-done((bf16[4,64,128]{2,1,0:T(8,128)(2,1)S(1)}, bf16[4,64,128]{2,1,0:T(8,128)(2,1)S(1)}, u32[]{:S(2)}, u32[]{:S(2)}) %collective-permute-start.35) | collective-permute-done | bytes 65568 | tf_op jit(solution)/shard_map/ppermute | solution.py:879
  101.4 2.9 %collective-permute-start.40 = (bf16[128,1024]{1,0:T(8,128)(2,1)S(1)}, bf16[128,1024]{1,0:T(8,128)(2,1)S(1)}, u32[]{:S(2)}, u32[]{:S(2)}) collective-permute-start(bf16[128,1024]{1,0:T(8,128)(2,1)S(1)} %get-tuple-element.360.refs_0_.refs_7_), channel_id=1, source_target_pairs={{0,8},{8,0},{1,9},{9,1},{2,10},{10,2},{3,11},{11,3},{4,12},{12,4},... | collective-permute-start | bytes 786440 | tf_op jit(solution)/shard_map/ppermute | solution.py:883
  104.3 3.8 %collective-permute-done.42.refs_17_ = bf16[256,512]{1,0:T(8,128)(2,1)S(1)} collective-permute-done((bf16[256,512]{1,0:T(8,128)(2,1)S(1)}, bf16[256,512]{1,0:T(8,128)(2,1)S(1)}, u32[]{:S(2)}, u32[]{:S(2)}) %collective-permute-start.42) | collective-permute-done | bytes 262176 | tf_op jit(solution)/shard_map/ppermute | solution.py:883
  108.0 6.5 %collective-permute-done.43.refs_19_ = bf16[256,512]{1,0:T(8,128)(2,1)S(1)} collective-permute-done((bf16[256,512]{1,0:T(8,128)(2,1)S(1)}, bf16[256,512]{1,0:T(8,128)(2,1)S(1)}, u32[]{:S(2)}, u32[]{:S(2)}) %collective-permute-start.43) | collective-permute-done | bytes 262176 | tf_op jit(solution)/shard_map/ppermute | solution.py:883
  129.0 6.5 %shard_map.203 = (bf16[512,1024]{1,0:T(8,128)(2,1)S(1)}, bf16[512,1024]{1,0:T(8,128)(2,1)S(1)}, f32[512,1024]{1,0:T(8,128)S(1)}, bf16[512,1024]{1,0:T(8,128)(2,1...) custom-call(s32[6]{0:T(128)S(1)} %copy-done.7, ...), custom_call_target="tpu_custom_call" | custom-call | flops 6000001024 | bytes 1024 | tf_op jit(solution)/shard_map/pallas_call | solution.py:95
  141.9 5.7 %collective-permute-done.55.got_y = bf16[2,64,1024]{2,1,0:T(8,128)(2,1)S(1)} collective-permute-done((bf16[2,64,1024]{2,1,0:T(8,128)(2,1)S(1)}, bf16[2,64,1024]{2,1,0:T(8,128)(2,1)S(1)}, u32[]{:S(2)}, u32[]{:S(2)}) %collective-permute-start.55) | collective-permute-done | bytes 262176 | tf_op jit(solution)/shard_map/ppermute | solution.py:883
  164.5 4.4 %collective-permute-done.62.refs_1_ = bf16[512,192]{1,0:T(8,128)(2,1)S(1)} collective-permute-done((bf16[512,192]{1,0:T(8,128)(2,1)S(1)}, bf16[512,192]{1,0:T(8,128)(2,1)S(1)}, u32[]{:S(2)}, u32[]{:S(2)}) %collective-permute-start.62) | collective-permute-done | bytes 196640 | tf_op jit(solution)/shard_map/ppermute | solution.py:883
  186.2 7.2 %shard_map.213 = (bf16[8,192,128]{2,1,0:T(8,128)(2,1)S(1)}, bf16[8,192,128]{2,1,0:T(8,128)(2,1)S(1)}, bf16[16,128,192]{2,1,0:T(8,128)(2,1)S(1)}, f32[1,192]{1,0:T(1,128)S(1)}) custom-call(s32[6]{0:T(128)S(1)} %copy-done.7, bf16[1,4,64,128]{3,2,1,0:T(8,128)(2,1)S(1)} %bitcast.47, bf16[1,4,64,128]{3,2,1,0:T(8,128)(2,1)S(1)} %bitcast.48, ...), custom_call_target="tpu_custom_call" | custom-call | flops 8000001024 | bytes 1024 | tf_op jit(solution)/shard_map/pallas_call | solution.py:95
  200.5 3.1 %collective-permute-start.74 = (bf16[128,1024]{1,0:T(8,128)(2,1)S(1)}, bf16[128,1024]{1,0:T(8,128)(2,1)S(1)}, u32[]{:S(2)}, u32[]{:S(2)}) collective-permute-start(bf16[128,1024]{1,0:T(8,128)(2,1)S(1)} %get-tuple-element.469), channel_id=1, source_target_pairs={{0,8},{8,0},{1,9},{9,1},{2,10},{10,2},{3,11},{11,3},{4,12},{12,4},... | collective-permute-start | bytes 786440 | tf_op jit(solution)/shard_map/ppermute | solution.py:883
  205.8 4.9 %collective-permute-done.75.got_ref = bf16[16,56,128]{2,1,0:T(8,128)(2,1)S(1)} collective-permute-done((bf16[16,56,128]{2,1,0:T(8,128)(2,1)S(1)}, bf16[16,56,128]{2,1,0:T(8,128)(2,1)S(1)}, u32[]{:S(2)}, u32[]{:S(2)}) %collective-permute-start.75) | collective-permute-done | bytes 229408 | tf_op jit(solution)/shard_map/ppermute | solution.py:883
  211.8 3.3 %collective-permute-done.76.got_ref = bf16[8,192,128]{2,1,0:T(8,128)(2,1)S(1)} collective-permute-done((bf16[8,192,128]{2,1,0:T(8,128)(2,1)S(1)}, bf16[8,192,128]{2,1,0:T(8,128)(2,1)S(1)}, u32[]{:S(2)}, u32[]{:S(2)}) %collective-permute-start.76) | collective-permute-done | bytes 393248 | tf_op jit(solution)/shard_map/ppermute | solution.py:883
  230.9 4.3 %collective-permute-done.86.refs_6_ = bf16[4,56,128]{2,1,0:T(8,128)(2,1)S(1)} collective-permute-done((bf16[4,56,128]{2,1,0:T(8,128)(2,1)S(1)}, bf16[4,56,128]{2,1,0:T(8,128)(2,1)S(1)}, u32[]{:S(2)}, u32[]{:S(2)}) %collective-permute-start.86) | collective-permute-done | bytes 57376 | tf_op jit(solution)/shard_map/ppermute | solution.py:1290
  235.2 5.1 %collective-permute-done.84.down_got = bf16[128,1024]{1,0:T(8,128)(2,1)S(1)} collective-permute-done((bf16[128,1024]{1,0:T(8,128)(2,1)S(1)}, bf16[128,1024]{1,0:T(8,128)(2,1)S(1)}, u32[]{:S(2)}, u32[]{:S(2)}) %collective-permute-start.84) | collective-permute-done | bytes 262176 | tf_op jit(solution)/shard_map/ppermute | solution.py:883
  247.5 7.7 %collective-permute-done.91.q3_ref = bf16[4,56,128]{2,1,0:T(8,128)(2,1)S(1)} collective-permute-done((bf16[4,56,128]{2,1,0:T(8,128)(2,1)S(1)}, bf16[4,56,128]{2,1,0:T(8,128)(2,1)S(1)}, u32[]{:S(2)}, u32[]{:S(2)}) %collective-permute-start.91) | collective-permute-done | bytes 57376 | tf_op jit(solution)/shard_map/ppermute | solution.py:879
  (238 shorter events, 146.3 us)
Async XLA Ops:
  4.6 12.8 %collective-permute-start.1 = (bf16[128,1024]{1,0:T(8,128)(2,1)}, bf16[128,1024]{1,0:T(8,128)(2,1)S(1)}, u32[]{:S(2)}, u32[]{:S(2)}) collective-permute-start(bf16[128,1024]{1,0:T(8,128)(2,1)} %get-tuple-element.283.refs_0_), channel_id=1, source_target_pairs={{8,0},{16,8},{24,16},{28,24},{20,28},{12,20},{4,12},{0,4},{9,1},{1... | collective-permute-start | bytes 786440 | tf_op jit(solution)/shard_map/ppermute | solution.py:1153
  17.5 14.5 %collective-permute-start.5 = (bf16[128,1024]{1,0:T(8,128)(2,1)S(1)}, bf16[128,1024]{1,0:T(8,128)(2,1)S(1)}, u32[]{:S(2)}, u32[]{:S(2)}) collective-permute-start(bf16[128,1024]{1,0:T(8,128)(2,1)S(1)} %collective-permute-done.refs_1_), channel_id=1, source_target_pairs={{0,8},{8,16},{16,24},{24,28},{28,20},{20,12},{12,4},{4,0},{1,9},{9... | collective-permute-start | bytes 786440 | tf_op jit(solution)/shard_map/ppermute | solution.py:1150
  17.6 14.4 %collective-permute-start.6 = (bf16[128,1024]{1,0:T(8,128)(2,1)S(1)}, bf16[128,1024]{1,0:T(8,128)(2,1)S(1)}, u32[]{:S(2)}, u32[]{:S(2)}) collective-permute-start(bf16[128,1024]{1,0:T(8,128)(2,1)S(1)} %collective-permute-done.1.refs_2_), channel_id=1, source_target_pairs={{8,0},{16,8},{24,16},{28,24},{20,28},{12,20},{4,12},{0,4},{9,1},{1... | collective-permute-start | bytes 786440 | tf_op jit(solution)/shard_map/ppermute | solution.py:1153
  44.3 14.2 %collective-permute-start.21 = (bf16[2,128,1024]{2,1,0:T(8,128)(2,1)S(1)}, bf16[2,128,1024]{2,1,0:T(8,128)(2,1)S(1)}, u32[]{:S(2)}, u32[]{:S(2)}) collective-permute-start(bf16[2,128,1024]{2,1,0:T(8,128)(2,1)S(1)} %shard_map.192), channel_id=1, source_target_pairs={{0,2},{2,0},{1,3},{3,1},{4,6},{6,4},{5,7},{7,5},{8,10},{10,8},{9,1... | collective-permute-start | bytes 1572872 | tf_op jit(solution)/shard_map/ppermute | solution.py:883
  67.7 13.7 %collective-permute-start.31 = (bf16[256,512]{1,0:T(8,128)(2,1)S(1)}, bf16[256,512]{1,0:T(8,128)(2,1)S(1)}, u32[]{:S(2)}, u32[]{:S(2)}) collective-permute-start(bf16[256,512]{1,0:T(8,128)(2,1)S(1)} %shard_map.195.refs_14_), channel_id=1, source_target_pairs={{0,16},{16,0},{1,17},{17,1},{2,18},{18,2},{3,19},{19,3},{4,20},{20... | collective-permute-start | bytes 786440 | tf_op jit(solution)/shard_map/ppermute | solution.py:883
  68.8 12.6 %collective-permute-start.32 = (bf16[128,1024]{1,0:T(8,128)(2,1)S(1)}, bf16[128,1024]{1,0:T(8,128)(2,1)S(1)}, u32[]{:S(2)}, u32[]{:S(2)}) collective-permute-start(bf16[128,1024]{1,0:T(8,128)(2,1)S(1)} %bitcast.34), channel_id=1, source_target_pairs={{0,4},{4,0},{1,5},{5,1},{2,6},{6,2},{3,7},{7,3},{8,12},{12,8},{9,1... | collective-permute-start | bytes 786440 | tf_op jit(solution)/shard_map/ppermute | solution.py:883
  81.4 13.2 %collective-permute-start.38 = (bf16[8,32,1024]{2,1,0:T(8,128)(2,1)S(1)}, bf16[8,32,1024]{2,1,0:T(8,128)(2,1)S(1)}, u32[]{:S(2)}, u32[]{:S(2)}) collective-permute-start(bf16[8,32,1024]{2,1,0:T(8,128)(2,1)S(1)} %shard_map.196.refs_0_), channel_id=1, source_target_pairs={{0,2},{2,0},{1,3},{3,1},{4,6},{6,4},{5,7},{7,5},{8,10},{10,8},{9,1... | collective-permute-start | bytes 1572872 | tf_op jit(solution)/shard_map/ppermute | solution.py:883
  81.5 14.3 %collective-permute-start.36 = (bf16[8,32,1024]{2,1,0:T(8,128)(2,1)S(1)}, bf16[8,32,1024]{2,1,0:T(8,128)(2,1)S(1)}, u32[]{:S(2)}, u32[]{:S(2)}) collective-permute-start(bf16[8,32,1024]{2,1,0:T(8,128)(2,1)S(1)} %shard_map.196.refs_0_), channel_id=1, source_target_pairs={{0,4},{4,0},{1,5},{5,1},{2,6},{6,2},{3,7},{7,3},{8,12},{12,8},{9,1... | collective-permute-start | bytes 1572872 | tf_op jit(solution)/shard_map/ppermute | solution.py:883
  99.2 16.6 %collective-permute-start.44 = (bf16[3,128,1024]{2,1,0:T(8,128)(2,1)S(1)}, bf16[3,128,1024]{2,1,0:T(8,128)(2,1)S(1)}, u32[]{:S(2)}, u32[]{:S(2)}) collective-permute-start(bf16[3,128,1024]{2,1,0:T(8,128)(2,1)S(1)} %shard_map.199), channel_id=1, source_target_pairs={{0,2},{2,0},{1,3},{3,1},{4,6},{6,4},{5,7},{7,5},{8,10},{10,8},{9,1... | collective-permute-start | bytes 2359304 | tf_op jit(solution)/shard_map/ppermute | solution.py:883
  100.3 14.3 %collective-permute-start.43 = (bf16[256,512]{1,0:T(8,128)(2,1)S(1)}, bf16[256,512]{1,0:T(8,128)(2,1)S(1)}, u32[]{:S(2)}, u32[]{:S(2)}) collective-permute-start(bf16[256,512]{1,0:T(8,128)(2,1)S(1)} %copy-done.6), channel_id=1, source_target_pairs={{0,16},{16,0},{1,17},{17,1},{2,18},{18,2},{3,19},{19,3},{4,20},{20... | collective-permute-start | bytes 786440 | tf_op jit(solution)/shard_map/ppermute | solution.py:883
  100.3 14.3 %collective-permute-start.41 = (bf16[128,1024]{1,0:T(8,128)(2,1)S(1)}, bf16[128,1024]{1,0:T(8,128)(2,1)S(1)}, u32[]{:S(2)}, u32[]{:S(2)}) collective-permute-start(bf16[128,1024]{1,0:T(8,128)(2,1)S(1)} %get-tuple-element.360.refs_0_.refs_7_), channel_id=1, source_target_pairs={{0,4},{4,0},{1,5},{5,1},{2,6},{6,2},{3,7},{7,3},{8,12},{12,8},{9,1... | collective-permute-start | bytes 786440 | tf_op jit(solution)/shard_map/ppermute | solution.py:883
  101.4 14.4 %collective-permute-start.40 = (bf16[128,1024]{1,0:T(8,128)(2,1)S(1)}, bf16[128,1024]{1,0:T(8,128)(2,1)S(1)}, u32[]{:S(2)}, u32[]{:S(2)}) collective-permute-start(bf16[128,1024]{1,0:T(8,128)(2,1)S(1)} %get-tuple-element.360.refs_0_.refs_7_), channel_id=1, source_target_pairs={{0,8},{8,0},{1,9},{9,1},{2,10},{10,2},{3,11},{11,3},{4,12},{12,4},... | collective-permute-start | bytes 786440 | tf_op jit(solution)/shard_map/ppermute | solution.py:883
  155.7 13.2 %collective-permute-start.61 = (bf16[264,512]{1,0:T(8,128)(2,1)S(1)}, bf16[264,512]{1,0:T(8,128)(2,1)S(1)}, u32[]{:S(2)}, u32[]{:S(2)}) collective-permute-start(bf16[264,512]{1,0:T(8,128)(2,1)S(1)} %get-tuple-element.414), channel_id=1, source_target_pairs={{0,1},{1,0},{2,3},{3,2},{4,5},{5,4},{6,7},{7,6},{8,9},{9,8},{10,11... | collective-permute-start | bytes 811016 | tf_op jit(solution)/shard_map/ppermute | solution.py:883
  180.2 19.5 %collective-permute-start.68 = (bf16[2,128,1024]{2,1,0:T(8,128)(2,1)S(1)}, bf16[2,128,1024]{2,1,0:T(8,128)(2,1)S(1)}, u32[]{:S(2)}, u32[]{:S(2)}) collective-permute-start(bf16[2,128,1024]{2,1,0:T(8,128)(2,1)S(1)} %get-tuple-element.446), channel_id=1, source_target_pairs={{0,8},{8,0},{1,9},{9,1},{2,10},{10,2},{3,11},{11,3},{4,12},{12,4},... | collective-permute-start | bytes 1572872 | tf_op jit(solution)/shard_map/ppermute | solution.py:883
  182.3 15.6 %collective-permute-start.70 = (bf16[264,512]{1,0:T(8,128)(2,1)S(1)}, bf16[264,512]{1,0:T(8,128)(2,1)S(1)}, u32[]{:S(2)}, u32[]{:S(2)}) collective-permute-start(bf16[264,512]{1,0:T(8,128)(2,1)S(1)} %get-tuple-element.456), channel_id=1, source_target_pairs={{0,1},{1,0},{2,3},{3,2},{4,5},{5,4},{6,7},{7,6},{8,9},{9,8},{10,11... | collective-permute-start | bytes 811016 | tf_op jit(solution)/shard_map/ppermute | solution.py:883
  183.6 16.2 %collective-permute-start.72 = (bf16[264,512]{1,0:T(8,128)(2,1)S(1)}, bf16[264,512]{1,0:T(8,128)(2,1)S(1)}, u32[]{:S(2)}, u32[]{:S(2)}) collective-permute-start(bf16[264,512]{1,0:T(8,128)(2,1)S(1)} %shard_map.211), channel_id=1, source_target_pairs={{0,16},{16,0},{1,17},{17,1},{2,18},{18,2},{3,19},{19,3},{4,20},{20... | collective-permute-start | bytes 811016 | tf_op jit(solution)/shard_map/ppermute | solution.py:883
  184.9 14.9 %collective-permute-start.69 = (bf16[2,128,1024]{2,1,0:T(8,128)(2,1)S(1)}, bf16[2,128,1024]{2,1,0:T(8,128)(2,1)S(1)}, u32[]{:S(2)}, u32[]{:S(2)}) collective-permute-start(bf16[2,128,1024]{2,1,0:T(8,128)(2,1)S(1)} %get-tuple-element.454), channel_id=1, source_target_pairs={{0,4},{4,0},{1,5},{5,1},{2,6},{6,2},{3,7},{7,3},{8,12},{12,8},{9,1... | collective-permute-start | bytes 1572872 | tf_op jit(solution)/shard_map/ppermute | solution.py:883
  193.4 21.7 %collective-permute-start.76 = (bf16[8,192,128]{2,1,0:T(8,128)(2,1)S(1)}, bf16[8,192,128]{2,1,0:T(8,128)(2,1)S(1)}, u32[]{:S(2)}, u32[]{:S(2)}) collective-permute-start(bf16[8,192,128]{2,1,0:T(8,128)(2,1)S(1)} %get-tuple-element.482), channel_id=1, source_target_pairs={{0,16},{16,0},{1,17},{17,1},{2,18},{18,2},{3,19},{19,3},{4,20},{20... | collective-permute-start | bytes 1179656 | tf_op jit(solution)/shard_map/ppermute | solution.py:883
  225.1 15.4 %collective-permute-start.83 = (bf16[4,312,128]{2,1,0:T(8,128)(2,1)S(1)}, bf16[4,312,128]{2,1,0:T(8,128)(2,1)S(1)}, u32[]{:S(2)}, u32[]{:S(2)}) collective-permute-start(bf16[4,312,128]{2,1,0:T(8,128)(2,1)S(1)} %get-tuple-element.509), channel_id=1, source_target_pairs={{0,4},{4,0},{1,5},{5,1},{2,6},{6,2},{3,7},{7,3},{8,12},{12,8},{9,1... | collective-permute-start | bytes 958472 | tf_op jit(solution)/shard_map/ppermute | solution.py:883
  225.7 14.5 %collective-permute-start.84 = (bf16[128,1024]{1,0:T(8,128)(2,1)S(1)}, bf16[128,1024]{1,0:T(8,128)(2,1)S(1)}, u32[]{:S(2)}, u32[]{:S(2)}) collective-permute-start(bf16[128,1024]{1,0:T(8,128)(2,1)S(1)} %shard_map.216), channel_id=1, source_target_pairs={{0,16},{16,0},{1,17},{17,1},{2,18},{18,2},{3,19},{19,3},{4,20},{20... | collective-permute-start | bytes 786440 | tf_op jit(solution)/shard_map/ppermute | solution.py:883
  225.7 14.7 %collective-permute-start.82 = (bf16[2,64,1024]{2,1,0:T(8,128)(2,1)S(1)}, bf16[2,64,1024]{2,1,0:T(8,128)(2,1)S(1)}, u32[]{:S(2)}, u32[]{:S(2)}) collective-permute-start(bf16[2,64,1024]{2,1,0:T(8,128)(2,1)S(1)} %get-tuple-element.508), channel_id=1, source_target_pairs={{0,8},{8,0},{1,9},{9,1},{2,10},{10,2},{3,11},{11,3},{4,12},{12,4},... | collective-permute-start | bytes 786440 | tf_op jit(solution)/shard_map/ppermute | solution.py:883
  241.2 14.1 %collective-permute-start.89 = (bf16[4,344,128]{2,1,0:T(8,128)(2,1)S(1)}, bf16[4,344,128]{2,1,0:T(8,128)(2,1)S(1)}, u32[]{:S(2)}, u32[]{:S(2)}) collective-permute-start(bf16[4,344,128]{2,1,0:T(8,128)(2,1)S(1)} %get-tuple-element.532), channel_id=1, source_target_pairs={{0,8},{8,0},{16,24},{24,16},{1,9},{9,1},{17,25},{25,17},{2,10},{10... | collective-permute-start | bytes 1056776 | tf_op jit(solution)/shard_map/ppermute | solution.py:879
  241.2 14.0 %collective-permute-start.88 = (bf16[128,1024]{1,0:T(8,128)(2,1)S(1)}, bf16[128,1024]{1,0:T(8,128)(2,1)S(1)}, u32[]{:S(2)}, u32[]{:S(2)}) collective-permute-start(bf16[128,1024]{1,0:T(8,128)(2,1)S(1)} %get-tuple-element.531), channel_id=1, source_target_pairs={{0,1},{1,0},{2,3},{3,2},{4,5},{5,4},{6,7},{7,6},{8,9},{9,8},{10,11... | collective-permute-start | bytes 786440 | tf_op jit(solution)/shard_map/ppermute | solution.py:883
  242.4 12.8 %collective-permute-start.87 = (bf16[64,1024]{1,0:T(8,128)(2,1)S(1)}, bf16[64,1024]{1,0:T(8,128)(2,1)S(1)}, u32[]{:S(2)}, u32[]{:S(2)}) collective-permute-start(bf16[64,1024]{1,0:T(8,128)(2,1)S(1)} %get-tuple-element.529), channel_id=1, source_target_pairs={{0,4},{4,0},{1,5},{5,1},{2,6},{6,2},{3,7},{7,3},{8,12},{12,8},{9,1... | collective-permute-start | bytes 393224 | tf_op jit(solution)/shard_map/ppermute | solution.py:883
  (83 other events, 845.9 us)

commit v4 on v3

--- a/solution.py
+++ b/solution.py
@@ -343,10 +343,22 @@
     norm_out[...] = (normed * gain_ref[...] + bias_ref[...]).astype(BF)
 
 
-def feed_kernel(table, *refs, grads, mids, wide, groups):
+def pair_kernel(mid_ref, mid_z, mid_y, grad_z, grad_y, three, send_z, send_y):
+    half = send_z.shape[1]
+    for at, ref in enumerate((mid_ref, mid_z, mid_y)):
+        three[at] = ref[...]
+    send_z[0], send_z[1] = mid_y[:half, :], grad_y[:half, :]
+    send_y[0], send_y[1] = mid_z[half:, :], grad_z[half:, :]
+
+
+def feed_kernel(table, *refs, grads, mids, wide, groups, paired):
     grads, mids, refs = refs[:grads], refs[grads : grads + mids], refs[grads + mids :]
     *weights, lay_keep, lay_send, mnd_keep, mnd_send, mid_out, act_out, delta_out, grad_out, up_ref, down_ref = refs
     place = Place(table)
+    if paired:
+        pairs = [mids[at] for at in (3, 4, 6, 7)]
+        grads = [*grads[:3], *[ref.at[1] for ref in pairs[:2]], grads[3], *[ref.at[1] for ref in pairs[2:]]]
+        mids = [*mids[:3], *[ref.at[0] for ref in pairs[:2]], mids[5], *[ref.at[0] for ref in pairs[2:]]]
     for out, arrays in ((grad_out, grads), (mid_out, mids)):
         first = 0
         for ref in arrays:
@@ -1000,7 +1012,8 @@
         inner = ((self.many, self.cols), BF)
         return call(
             partial(
-                feed_kernel, grads=len(grads), mids=len(mids), wide=self.wide, groups=self.highs * self.wide
+                feed_kernel, grads=len(grads), mids=len(mids), wide=self.wide, groups=self.highs * self.wide,
+                paired=len(mids) > len(grads),
             ),
             (self.table, *grads, *mids, *weights),
             [(half, BF), (half, BF), (half, F32), (half, BF), (full, BF), inner, inner, (full, BF)],
@@ -1201,19 +1214,17 @@
         swap(after(down_b, norm_mid), "zh"),
         swap(grad_3, "c"),
     )
-    three = stack([norm_mid, by_z, by_y])
-    both_one, both_two, three, down_zx, grad_one, grad_two = meet(
-        swap(by_y[:half], "zl"),
-        swap(by_z[half:], "y"),
-        swap(three, "c"),
-        swap(after(down_z, by_z), "x"),
-        swap(after(grad_y[:half], by_z), "zl"),
-        swap(after(grad_z[half:], by_z), "y"),
-    )
-    both = stack([both_one, both_two])
-    grad_both = stack([grad_one, grad_two])
-    mids = [norm_mid, by_z, by_y, both_one, both_two, three, swap(both, "c")]
-    grads = [grad, grad_z, grad_y, grad_one, grad_two, grad_3c, swap(grad_both, "c")]
+    three, send_z, send_y = call(
+        pair_kernel,
+        (norm_mid, by_z, by_y, grad_z, grad_y),
+        [((3, s.rows, s.width), BF)] + [((2, s.half, s.width), BF)] * 2,
+        smem=0,
+    )
+    pair_z, pair_y, three, down_zx = meet(
+        swap(send_z, "zl"), swap(send_y, "y"), swap(three, "c"), swap(after(down_z, send_z), "x")
+    )
+    mids = [norm_mid, by_z, by_y, pair_z, pair_y, three, swap(pair_z, "c"), swap(pair_y, "c")]
+    grads = [grad, grad_z, grad_y, grad_3c]
     lay_keep, lay_send, keep, send, mids, acts, delta, grads = s.feed(
         grads, mids, [up_t, up_z, up_x, up_zx, down_b, down_z, down_x, down_zx]
     )

time: 261 us -> 259 us (level)
  starting transfers between devices: 88.9 us -> 85.9 us
    ppermute x52 -> x50, starting transfers between devices: 46.5 us -> 43.5 us  [swap(): return lax.ppermute(array, axis, SWAP)]
    ppermute x52 -> x50, waiting for transfers between devices: 60.5 us -> 63.1 us  [swap(): return lax.ppermute(array, axis, SWAP)]
    pallas_call x39 -> x37, Pallas kernels: 46.4 us -> 46.4 us  [call(): pl.pallas_call(body, out_shape=[jax.ShapeDtypeStruct(shape, kind) for sha...]
  transfers between devices with their start and end apart: 92 -> 90, of which waited for: 46 -> 45; matrix products, arithmetic and copies ran while one was open for 1% -> 1% of each run, Pallas kernels for 10% -> 10%
where the time goes in v4:
time: 259 us; the launch traced here: 257 us
  waiting for transfers between devices  118 us (46%)
  starting transfers between devices  85.9 us (33%)
  Pallas kernels  46.4 us (18%)
    ppermute x50, waiting for transfers between devices, swap(): return lax.ppermute(array, axis, SWAP)  63.1 us
    pallas_call x37, Pallas kernels, call(): pl.pallas_call(body, out_shape=[jax.ShapeDtypeStruct(shape, kind) for sha...  46.4 us
    ppermute x50, starting transfers between devices, swap(): return lax.ppermute(array, axis, SWAP)  43.5 us
    ppermute x12, waiting for transfers between devices, far(): lax.ppermute(arrays[at], ('zh', 'zl'), apart(4, at))  24.5 us
    ppermute x15, waiting for transfers between devices, near(): lax.ppermute(arrays[at], ('y', 'c'), apart(4, at))  21.5 us
    ppermute x12, starting transfers between devices, far(): lax.ppermute(arrays[at], ('zh', 'zl'), apart(4, at))  18.5 us
    ppermute x15, starting transfers between devices, near(): lax.ppermute(arrays[at], ('y', 'c'), apart(4, at))  9.2 us
    ppermute x4, starting transfers between devices, behind(): return lax.ppermute(array, CHIPS, left)  7.45 us
  transfers between devices with their start and end apart: 90, of which 45 were waited for; matrix products, arithmetic and copies ran while one was open for 1% of the time, Pallas kernels for 10%

profile of v4, /device:TPU:0, one launch (start us, length us, event | category | flops | bytes accessed | tf_op | source)
XLA Modules:
  0.0 257.0 jit_solution(14610054937015350070)
XLA Ops:
  1.3 3.3 %shard_map.186 = (bf16[128,1024]{1,0:T(8,128)(2,1)}, bf16[4,56,128]{2,1,0:T(8,128)(2,1)}, bf16[4,56,128]{2,1,0:T(8,128)(2,1)}, bf16[4,56,128]{2,1,0:T(8,128)(2,1...) custom-call(s32[6]{0:T(128)} %stack.24.table._, ...), custom_call_target="tpu_custom_call" | custom-call | flops 1000 | bytes 1024 | tf_op jit(solution)/shard_map/pallas_call | solution.py:95
  4.6 3.0 %collective-permute-start.1 = (bf16[128,1024]{1,0:T(8,128)(2,1)}, bf16[128,1024]{1,0:T(8,128)(2,1)S(1)}, u32[]{:S(2)}, u32[]{:S(2)}) collective-permute-start(bf16[128,1024]{1,0:T(8,128)(2,1)} %get-tuple-element.282.refs_0_), channel_id=1, source_target_pairs={{8,0},{16,8},{24,16},{28,24},{20,28},{12,20},{4,12},{0,4},{9,1},{1... | collective-permute-start | bytes 786440 | tf_op jit(solution)/shard_map/ppermute | solution.py:1166
  9.8 7.6 %collective-permute-done.3.refs_2_ = bf16[4,56,128]{2,1,0:T(8,128)(2,1)S(1)} collective-permute-done((bf16[4,56,128]{2,1,0:T(8,128)(2,1)}, bf16[4,56,128]{2,1,0:T(8,128)(2,1)S(1)}, u32[]{:S(2)}, u32[]{:S(2)}) %collective-permute-start.3) | collective-permute-done | bytes 57376 | tf_op jit(solution)/shard_map/ppermute | solution.py:887
  20.5 2.9 %collective-permute-start.8 = (bf16[4,56,128]{2,1,0:T(8,128)(2,1)S(1)}, bf16[4,56,128]{2,1,0:T(8,128)(2,1)S(1)}, u32[]{:S(2)}, u32[]{:S(2)}) collective-permute-start(bf16[4,56,128]{2,1,0:T(8,128)(2,1)S(1)} %get-tuple-element.293), channel_id=1, source_target_pairs={{0,16},{8,24},{16,0},{24,8},{1,17},{9,25},{17,1},{25,9},{2,18},{10... | collective-permute-start | bytes 172040 | tf_op jit(solution)/shard_map/ppermute | solution.py:891
  24.8 3.6 %collective-permute-done.7.refs_1_ = bf16[4,56,128]{2,1,0:T(8,128)(2,1)S(1)} collective-permute-done((bf16[4,56,128]{2,1,0:T(8,128)(2,1)S(1)}, bf16[4,56,128]{2,1,0:T(8,128)(2,1)S(1)}, u32[]{:S(2)}, u32[]{:S(2)}) %collective-permute-start.7) | collective-permute-done | bytes 57376 | tf_op jit(solution)/shard_map/ppermute | solution.py:891
  29.0 2.9 %collective-permute-done.9.refs_3_ = bf16[4,56,128]{2,1,0:T(8,128)(2,1)S(1)} collective-permute-done((bf16[4,56,128]{2,1,0:T(8,128)(2,1)S(1)}, bf16[4,56,128]{2,1,0:T(8,128)(2,1)S(1)}, u32[]{:S(2)}, u32[]{:S(2)}) %collective-permute-start.9) | collective-permute-done | bytes 57376 | tf_op jit(solution)/shard_map/ppermute | solution.py:891
  58.6 6.8 %shard_map.193 = (bf16[4,64,128]{2,1,0:T(8,128)(2,1)S(1)}, bf16[4,64,128]{2,1,0:T(8,128)(2,1)S(1)}, bf16[4,64,128]{2,1,0:T(8,128)(2,1)S(1)}, bf16[4,64,128]{2,1,...) custom-call(s32[6]{0:T(128)S(1)} %copy-done.7, ...), custom_call_target="tpu_custom_call" | custom-call | flops 7000001024 | bytes 1024 | tf_op jit(solution)/shard_map/pallas_call | solution.py:95
  73.1 5.3 %collective-permute-done.28.refs_2_ = bf16[4,64,128]{2,1,0:T(8,128)(2,1)S(1)} collective-permute-done((bf16[4,64,128]{2,1,0:T(8,128)(2,1)S(1)}, bf16[4,64,128]{2,1,0:T(8,128)(2,1)S(1)}, u32[]{:S(2)}, u32[]{:S(2)}) %collective-permute-start.28) | collective-permute-done | bytes 65568 | tf_op jit(solution)/shard_map/ppermute | solution.py:887
  78.4 2.9 %collective-permute-done.31.refs_13_ = bf16[256,512]{1,0:T(8,128)(2,1)S(1)} collective-permute-done((bf16[256,512]{1,0:T(8,128)(2,1)S(1)}, bf16[256,512]{1,0:T(8,128)(2,1)S(1)}, u32[]{:S(2)}, u32[]{:S(2)}) %collective-permute-start.31) | collective-permute-done | bytes 262176 | tf_op jit(solution)/shard_map/ppermute | solution.py:895
  83.5 2.9 %collective-permute-start.34 = (bf16[4,64,128]{2,1,0:T(8,128)(2,1)S(1)}, bf16[4,64,128]{2,1,0:T(8,128)(2,1)S(1)}, u32[]{:S(2)}, u32[]{:S(2)}) collective-permute-start(bf16[4,64,128]{2,1,0:T(8,128)(2,1)S(1)} %get-tuple-element.346), channel_id=1, source_target_pairs={{0,16},{8,24},{16,0},{24,8},{1,17},{9,25},{17,1},{25,9},{2,18},{10... | collective-permute-start | bytes 196616 | tf_op jit(solution)/shard_map/ppermute | solution.py:891
  90.9 3.7 %collective-permute-done.35.refs_7_ = bf16[4,64,128]{2,1,0:T(8,128)(2,1)S(1)} collective-permute-done((bf16[4,64,128]{2,1,0:T(8,128)(2,1)S(1)}, bf16[4,64,128]{2,1,0:T(8,128)(2,1)S(1)}, u32[]{:S(2)}, u32[]{:S(2)}) %collective-permute-start.35) | collective-permute-done | bytes 65568 | tf_op jit(solution)/shard_map/ppermute | solution.py:891
  101.3 2.9 %collective-permute-start.40 = (bf16[128,1024]{1,0:T(8,128)(2,1)S(1)}, bf16[128,1024]{1,0:T(8,128)(2,1)S(1)}, u32[]{:S(2)}, u32[]{:S(2)}) collective-permute-start(bf16[128,1024]{1,0:T(8,128)(2,1)S(1)} %get-tuple-element.359.mid_ref.refs_4_), channel_id=1, source_target_pairs={{0,8},{8,0},{1,9},{9,1},{2,10},{10,2},{3,11},{11,3},{4,12},{12,4},... | collective-permute-start | bytes 786440 | tf_op jit(solution)/shard_map/ppermute | solution.py:895
  104.2 3.8 %collective-permute-done.42.refs_15_ = bf16[256,512]{1,0:T(8,128)(2,1)S(1)} collective-permute-done((bf16[256,512]{1,0:T(8,128)(2,1)S(1)}, bf16[256,512]{1,0:T(8,128)(2,1)S(1)}, u32[]{:S(2)}, u32[]{:S(2)}) %collective-permute-start.42) | collective-permute-done | bytes 262176 | tf_op jit(solution)/shard_map/ppermute | solution.py:895
  108.0 6.5 %collective-permute-done.43.refs_17_ = bf16[256,512]{1,0:T(8,128)(2,1)S(1)} collective-permute-done((bf16[256,512]{1,0:T(8,128)(2,1)S(1)}, bf16[256,512]{1,0:T(8,128)(2,1)S(1)}, u32[]{:S(2)}, u32[]{:S(2)}) %collective-permute-start.43) | collective-permute-done | bytes 262176 | tf_op jit(solution)/shard_map/ppermute | solution.py:895
  117.4 7.2 %collective-permute-done.48.refs_19_ = bf16[256,512]{1,0:T(8,128)(2,1)S(1)} collective-permute-done((bf16[256,512]{1,0:T(8,128)(2,1)S(1)}, bf16[256,512]{1,0:T(8,128)(2,1)S(1)}, u32[]{:S(2)}, u32[]{:S(2)}) %collective-permute-start.48) | collective-permute-done | bytes 262176 | tf_op jit(solution)/shard_map/ppermute | solution.py:895
  127.4 6.5 %shard_map.201 = (bf16[512,1024]{1,0:T(8,128)(2,1)S(1)}, bf16[512,1024]{1,0:T(8,128)(2,1)S(1)}, f32[512,1024]{1,0:T(8,128)S(1)}, bf16[512,1024]{1,0:T(8,128)(2,1...) custom-call(s32[6]{0:T(128)S(1)} %copy-done.7, ...), custom_call_target="tpu_custom_call" | custom-call | flops 6000001024 | bytes 1024 | tf_op jit(solution)/shard_map/pallas_call | solution.py:95
  141.4 4.5 %collective-permute-done.53.got_y = bf16[2,64,1024]{2,1,0:T(8,128)(2,1)S(1)} collective-permute-done((bf16[2,64,1024]{2,1,0:T(8,128)(2,1)S(1)}, bf16[2,64,1024]{2,1,0:T(8,128)(2,1)S(1)}, u32[]{:S(2)}, u32[]{:S(2)}) %collective-permute-start.53) | collective-permute-done | bytes 262176 | tf_op jit(solution)/shard_map/ppermute | solution.py:895
  163.3 5.3 %collective-permute-done.60.refs_1_ = bf16[512,192]{1,0:T(8,128)(2,1)S(1)} collective-permute-done((bf16[512,192]{1,0:T(8,128)(2,1)S(1)}, bf16[512,192]{1,0:T(8,128)(2,1)S(1)}, u32[]{:S(2)}, u32[]{:S(2)}) %collective-permute-start.60) | collective-permute-done | bytes 196640 | tf_op jit(solution)/shard_map/ppermute | solution.py:895
  175.0 3.4 %collective-permute-done.62 = bf16[4,64,128]{2,1,0:T(8,128)(2,1)S(1)} collective-permute-done((bf16[4,64,128]{2,1,0:T(8,128)(2,1)S(1)}, bf16[4,64,128]{2,1,0:T(8,128)(2,1)S(1)}, u32[]{:S(2)}, u32[]{:S(2)}) %collective-permute-start.62) | collective-permute-done | bytes 65568 | tf_op jit(solution)/shard_map/ppermute | solution.py:891
  184.7 7.2 %shard_map.211 = (bf16[8,192,128]{2,1,0:T(8,128)(2,1)S(1)}, bf16[8,192,128]{2,1,0:T(8,128)(2,1)S(1)}, bf16[16,128,192]{2,1,0:T(8,128)(2,1)S(1)}, f32[1,192]{1,0:T(1,128)S(1)}) custom-call(s32[6]{0:T(128)S(1)} %copy-done.7, bf16[1,4,64,128]{3,2,1,0:T(8,128)(2,1)S(1)} %bitcast.47, bf16[1,4,64,128]{3,2,1,0:T(8,128)(2,1)S(1)} %bitcast.48, ...), custom_call_target="tpu_custom_call" | custom-call | flops 8000001024 | bytes 1024 | tf_op jit(solution)/shard_map/pallas_call | solution.py:95
  204.5 5.0 %collective-permute-done.73.got_ref = bf16[16,56,128]{2,1,0:T(8,128)(2,1)S(1)} collective-permute-done((bf16[16,56,128]{2,1,0:T(8,128)(2,1)S(1)}, bf16[16,56,128]{2,1,0:T(8,128)(2,1)S(1)}, u32[]{:S(2)}, u32[]{:S(2)}) %collective-permute-start.73) | collective-permute-done | bytes 229408 | tf_op jit(solution)/shard_map/ppermute | solution.py:895
  229.8 4.2 %collective-permute-done.84.refs_6_ = bf16[4,56,128]{2,1,0:T(8,128)(2,1)S(1)} collective-permute-done((bf16[4,56,128]{2,1,0:T(8,128)(2,1)S(1)}, bf16[4,56,128]{2,1,0:T(8,128)(2,1)S(1)}, u32[]{:S(2)}, u32[]{:S(2)}) %collective-permute-start.84) | collective-permute-done | bytes 57376 | tf_op jit(solution)/shard_map/ppermute | solution.py:1301
  234.0 4.9 %collective-permute-done.82.down_got = bf16[128,1024]{1,0:T(8,128)(2,1)S(1)} collective-permute-done((bf16[128,1024]{1,0:T(8,128)(2,1)S(1)}, bf16[128,1024]{1,0:T(8,128)(2,1)S(1)}, u32[]{:S(2)}, u32[]{:S(2)}) %collective-permute-start.82) | collective-permute-done | bytes 262176 | tf_op jit(solution)/shard_map/ppermute | solution.py:895
  246.4 7.5 %collective-permute-done.89.q3_ref = bf16[4,56,128]{2,1,0:T(8,128)(2,1)S(1)} collective-permute-done((bf16[4,56,128]{2,1,0:T(8,128)(2,1)S(1)}, bf16[4,56,128]{2,1,0:T(8,128)(2,1)S(1)}, u32[]{:S(2)}, u32[]{:S(2)}) %collective-permute-start.89) | collective-permute-done | bytes 57376 | tf_op jit(solution)/shard_map/ppermute | solution.py:891
  (228 shorter events, 141.5 us)
Async XLA Ops:
  4.6 12.8 %collective-permute-start.1 = (bf16[128,1024]{1,0:T(8,128)(2,1)}, bf16[128,1024]{1,0:T(8,128)(2,1)S(1)}, u32[]{:S(2)}, u32[]{:S(2)}) collective-permute-start(bf16[128,1024]{1,0:T(8,128)(2,1)} %get-tuple-element.282.refs_0_), channel_id=1, source_target_pairs={{8,0},{16,8},{24,16},{28,24},{20,28},{12,20},{4,12},{0,4},{9,1},{1... | collective-permute-start | bytes 786440 | tf_op jit(solution)/shard_map/ppermute | solution.py:1166
  17.5 14.5 %collective-permute-start.5 = (bf16[128,1024]{1,0:T(8,128)(2,1)S(1)}, bf16[128,1024]{1,0:T(8,128)(2,1)S(1)}, u32[]{:S(2)}, u32[]{:S(2)}) collective-permute-start(bf16[128,1024]{1,0:T(8,128)(2,1)S(1)} %collective-permute-done.refs_1_), channel_id=1, source_target_pairs={{0,8},{8,16},{16,24},{24,28},{28,20},{20,12},{12,4},{4,0},{1,9},{9... | collective-permute-start | bytes 786440 | tf_op jit(solution)/shard_map/ppermute | solution.py:1163
  17.5 14.4 %collective-permute-start.6 = (bf16[128,1024]{1,0:T(8,128)(2,1)S(1)}, bf16[128,1024]{1,0:T(8,128)(2,1)S(1)}, u32[]{:S(2)}, u32[]{:S(2)}) collective-permute-start(bf16[128,1024]{1,0:T(8,128)(2,1)S(1)} %collective-permute-done.1.refs_2_), channel_id=1, source_target_pairs={{8,0},{16,8},{24,16},{28,24},{20,28},{12,20},{4,12},{0,4},{9,1},{1... | collective-permute-start | bytes 786440 | tf_op jit(solution)/shard_map/ppermute | solution.py:1166
  44.3 14.2 %collective-permute-start.21 = (bf16[2,128,1024]{2,1,0:T(8,128)(2,1)S(1)}, bf16[2,128,1024]{2,1,0:T(8,128)(2,1)S(1)}, u32[]{:S(2)}, u32[]{:S(2)}) collective-permute-start(bf16[2,128,1024]{2,1,0:T(8,128)(2,1)S(1)} %shard_map.192), channel_id=1, source_target_pairs={{0,2},{2,0},{1,3},{3,1},{4,6},{6,4},{5,7},{7,5},{8,10},{10,8},{9,1... | collective-permute-start | bytes 1572872 | tf_op jit(solution)/shard_map/ppermute | solution.py:895
  67.7 13.7 %collective-permute-start.31 = (bf16[256,512]{1,0:T(8,128)(2,1)S(1)}, bf16[256,512]{1,0:T(8,128)(2,1)S(1)}, u32[]{:S(2)}, u32[]{:S(2)}) collective-permute-start(bf16[256,512]{1,0:T(8,128)(2,1)S(1)} %shard_map.195.refs_12_), channel_id=1, source_target_pairs={{0,16},{16,0},{1,17},{17,1},{2,18},{18,2},{3,19},{19,3},{4,20},{20... | collective-permute-start | bytes 786440 | tf_op jit(solution)/shard_map/ppermute | solution.py:895
  68.8 12.6 %collective-permute-start.32 = (bf16[128,1024]{1,0:T(8,128)(2,1)S(1)}, bf16[128,1024]{1,0:T(8,128)(2,1)S(1)}, u32[]{:S(2)}, u32[]{:S(2)}) collective-permute-start(bf16[128,1024]{1,0:T(8,128)(2,1)S(1)} %bitcast.34), channel_id=1, source_target_pairs={{0,4},{4,0},{1,5},{5,1},{2,6},{6,2},{3,7},{7,3},{8,12},{12,8},{9,1... | collective-permute-start | bytes 786440 | tf_op jit(solution)/shard_map/ppermute | solution.py:895
  81.4 13.2 %collective-permute-start.38 = (bf16[8,32,1024]{2,1,0:T(8,128)(2,1)S(1)}, bf16[8,32,1024]{2,1,0:T(8,128)(2,1)S(1)}, u32[]{:S(2)}, u32[]{:S(2)}) collective-permute-start(bf16[8,32,1024]{2,1,0:T(8,128)(2,1)S(1)} %shard_map.196.refs_0_), channel_id=1, source_target_pairs={{0,2},{2,0},{1,3},{3,1},{4,6},{6,4},{5,7},{7,5},{8,10},{10,8},{9,1... | collective-permute-start | bytes 1572872 | tf_op jit(solution)/shard_map/ppermute | solution.py:895
  81.5 14.3 %collective-permute-start.36 = (bf16[8,32,1024]{2,1,0:T(8,128)(2,1)S(1)}, bf16[8,32,1024]{2,1,0:T(8,128)(2,1)S(1)}, u32[]{:S(2)}, u32[]{:S(2)}) collective-permute-start(bf16[8,32,1024]{2,1,0:T(8,128)(2,1)S(1)} %shard_map.196.refs_0_), channel_id=1, source_target_pairs={{0,4},{4,0},{1,5},{5,1},{2,6},{6,2},{3,7},{7,3},{8,12},{12,8},{9,1... | collective-permute-start | bytes 1572872 | tf_op jit(solution)/shard_map/ppermute | solution.py:895
  99.2 16.6 %collective-permute-start.44 = (bf16[3,128,1024]{2,1,0:T(8,128)(2,1)S(1)}, bf16[3,128,1024]{2,1,0:T(8,128)(2,1)S(1)}, u32[]{:S(2)}, u32[]{:S(2)}) collective-permute-start(bf16[3,128,1024]{2,1,0:T(8,128)(2,1)S(1)} %shard_map.199), channel_id=1, source_target_pairs={{0,2},{2,0},{1,3},{3,1},{4,6},{6,4},{5,7},{7,5},{8,10},{10,8},{9,1... | collective-permute-start | bytes 2359304 | tf_op jit(solution)/shard_map/ppermute | solution.py:895
  100.3 14.2 %collective-permute-start.43 = (bf16[256,512]{1,0:T(8,128)(2,1)S(1)}, bf16[256,512]{1,0:T(8,128)(2,1)S(1)}, u32[]{:S(2)}, u32[]{:S(2)}) collective-permute-start(bf16[256,512]{1,0:T(8,128)(2,1)S(1)} %copy-done.6), channel_id=1, source_target_pairs={{0,16},{16,0},{1,17},{17,1},{2,18},{18,2},{3,19},{19,3},{4,20},{20... | collective-permute-start | bytes 786440 | tf_op jit(solution)/shard_map/ppermute | solution.py:895
  100.3 14.2 %collective-permute-start.41 = (bf16[128,1024]{1,0:T(8,128)(2,1)S(1)}, bf16[128,1024]{1,0:T(8,128)(2,1)S(1)}, u32[]{:S(2)}, u32[]{:S(2)}) collective-permute-start(bf16[128,1024]{1,0:T(8,128)(2,1)S(1)} %get-tuple-element.359.mid_ref.refs_4_), channel_id=1, source_target_pairs={{0,4},{4,0},{1,5},{5,1},{2,6},{6,2},{3,7},{7,3},{8,12},{12,8},{9,1... | collective-permute-start | bytes 786440 | tf_op jit(solution)/shard_map/ppermute | solution.py:895
  101.3 14.4 %collective-permute-start.40 = (bf16[128,1024]{1,0:T(8,128)(2,1)S(1)}, bf16[128,1024]{1,0:T(8,128)(2,1)S(1)}, u32[]{:S(2)}, u32[]{:S(2)}) collective-permute-start(bf16[128,1024]{1,0:T(8,128)(2,1)S(1)} %get-tuple-element.359.mid_ref.refs_4_), channel_id=1, source_target_pairs={{0,8},{8,0},{1,9},{9,1},{2,10},{10,2},{3,11},{11,3},{4,12},{12,4},... | collective-permute-start | bytes 786440 | tf_op jit(solution)/shard_map/ppermute | solution.py:895
  155.0 13.7 %collective-permute-start.59 = (bf16[264,512]{1,0:T(8,128)(2,1)S(1)}, bf16[264,512]{1,0:T(8,128)(2,1)S(1)}, u32[]{:S(2)}, u32[]{:S(2)}) collective-permute-start(bf16[264,512]{1,0:T(8,128)(2,1)S(1)} %get-tuple-element.412), channel_id=1, source_target_pairs={{0,1},{1,0},{2,3},{3,2},{4,5},{5,4},{6,7},{7,6},{8,9},{9,8},{10,11... | collective-permute-start | bytes 811016 | tf_op jit(solution)/shard_map/ppermute | solution.py:895
  179.4 19.7 %collective-permute-start.66 = (bf16[2,128,1024]{2,1,0:T(8,128)(2,1)S(1)}, bf16[2,128,1024]{2,1,0:T(8,128)(2,1)S(1)}, u32[]{:S(2)}, u32[]{:S(2)}) collective-permute-start(bf16[2,128,1024]{2,1,0:T(8,128)(2,1)S(1)} %get-tuple-element.444), channel_id=1, source_target_pairs={{0,8},{8,0},{1,9},{9,1},{2,10},{10,2},{3,11},{11,3},{4,12},{12,4},... | collective-permute-start | bytes 1572872 | tf_op jit(solution)/shard_map/ppermute | solution.py:895
  181.7 14.4 %collective-permute-start.68 = (bf16[264,512]{1,0:T(8,128)(2,1)S(1)}, bf16[264,512]{1,0:T(8,128)(2,1)S(1)}, u32[]{:S(2)}, u32[]{:S(2)}) collective-permute-start(bf16[264,512]{1,0:T(8,128)(2,1)S(1)} %get-tuple-element.454), channel_id=1, source_target_pairs={{0,1},{1,0},{2,3},{3,2},{4,5},{5,4},{6,7},{7,6},{8,9},{9,8},{10,11... | collective-permute-start | bytes 811016 | tf_op jit(solution)/shard_map/ppermute | solution.py:895
  182.7 16.2 %collective-permute-start.70 = (bf16[264,512]{1,0:T(8,128)(2,1)S(1)}, bf16[264,512]{1,0:T(8,128)(2,1)S(1)}, u32[]{:S(2)}, u32[]{:S(2)}) collective-permute-start(bf16[264,512]{1,0:T(8,128)(2,1)S(1)} %shard_map.209), channel_id=1, source_target_pairs={{0,16},{16,0},{1,17},{17,1},{2,18},{18,2},{3,19},{19,3},{4,20},{20... | collective-permute-start | bytes 811016 | tf_op jit(solution)/shard_map/ppermute | solution.py:895
  184.0 14.9 %collective-permute-start.67 = (bf16[2,128,1024]{2,1,0:T(8,128)(2,1)S(1)}, bf16[2,128,1024]{2,1,0:T(8,128)(2,1)S(1)}, u32[]{:S(2)}, u32[]{:S(2)}) collective-permute-start(bf16[2,128,1024]{2,1,0:T(8,128)(2,1)S(1)} %get-tuple-element.452), channel_id=1, source_target_pairs={{0,4},{4,0},{1,5},{5,1},{2,6},{6,2},{3,7},{7,3},{8,12},{12,8},{9,1... | collective-permute-start | bytes 1572872 | tf_op jit(solution)/shard_map/ppermute | solution.py:895
  191.9 22.6 %collective-permute-start.74 = (bf16[8,192,128]{2,1,0:T(8,128)(2,1)S(1)}, bf16[8,192,128]{2,1,0:T(8,128)(2,1)S(1)}, u32[]{:S(2)}, u32[]{:S(2)}) collective-permute-start(bf16[8,192,128]{2,1,0:T(8,128)(2,1)S(1)} %get-tuple-element.480), channel_id=1, source_target_pairs={{0,16},{16,0},{1,17},{17,1},{2,18},{18,2},{3,19},{19,3},{4,20},{20... | collective-permute-start | bytes 1179656 | tf_op jit(solution)/shard_map/ppermute | solution.py:895
  223.8 15.3 %collective-permute-start.81 = (bf16[4,312,128]{2,1,0:T(8,128)(2,1)S(1)}, bf16[4,312,128]{2,1,0:T(8,128)(2,1)S(1)}, u32[]{:S(2)}, u32[]{:S(2)}) collective-permute-start(bf16[4,312,128]{2,1,0:T(8,128)(2,1)S(1)} %get-tuple-element.507), channel_id=1, source_target_pairs={{0,4},{4,0},{1,5},{5,1},{2,6},{6,2},{3,7},{7,3},{8,12},{12,8},{9,1... | collective-permute-start | bytes 958472 | tf_op jit(solution)/shard_map/ppermute | solution.py:895
  224.8 14.1 %collective-permute-start.82 = (bf16[128,1024]{1,0:T(8,128)(2,1)S(1)}, bf16[128,1024]{1,0:T(8,128)(2,1)S(1)}, u32[]{:S(2)}, u32[]{:S(2)}) collective-permute-start(bf16[128,1024]{1,0:T(8,128)(2,1)S(1)} %shard_map.214), channel_id=1, source_target_pairs={{0,16},{16,0},{1,17},{17,1},{2,18},{18,2},{3,19},{19,3},{4,20},{20... | collective-permute-start | bytes 786440 | tf_op jit(solution)/shard_map/ppermute | solution.py:895
  224.8 14.3 %collective-permute-start.80 = (bf16[2,64,1024]{2,1,0:T(8,128)(2,1)S(1)}, bf16[2,64,1024]{2,1,0:T(8,128)(2,1)S(1)}, u32[]{:S(2)}, u32[]{:S(2)}) collective-permute-start(bf16[2,64,1024]{2,1,0:T(8,128)(2,1)S(1)} %get-tuple-element.506), channel_id=1, source_target_pairs={{0,8},{8,0},{1,9},{9,1},{2,10},{10,2},{3,11},{11,3},{4,12},{12,4},... | collective-permute-start | bytes 786440 | tf_op jit(solution)/shard_map/ppermute | solution.py:895
  239.8 14.1 %collective-permute-start.87 = (bf16[4,344,128]{2,1,0:T(8,128)(2,1)S(1)}, bf16[4,344,128]{2,1,0:T(8,128)(2,1)S(1)}, u32[]{:S(2)}, u32[]{:S(2)}) collective-permute-start(bf16[4,344,128]{2,1,0:T(8,128)(2,1)S(1)} %get-tuple-element.530), channel_id=1, source_target_pairs={{0,8},{8,0},{16,24},{24,16},{1,9},{9,1},{17,25},{25,17},{2,10},{10... | collective-permute-start | bytes 1056776 | tf_op jit(solution)/shard_map/ppermute | solution.py:891
  239.9 14.1 %collective-permute-start.86 = (bf16[128,1024]{1,0:T(8,128)(2,1)S(1)}, bf16[128,1024]{1,0:T(8,128)(2,1)S(1)}, u32[]{:S(2)}, u32[]{:S(2)}) collective-permute-start(bf16[128,1024]{1,0:T(8,128)(2,1)S(1)} %get-tuple-element.529), channel_id=1, source_target_pairs={{0,1},{1,0},{2,3},{3,2},{4,5},{5,4},{6,7},{7,6},{8,9},{9,8},{10,11... | collective-permute-start | bytes 786440 | tf_op jit(solution)/shard_map/ppermute | solution.py:895
  240.9 13.1 %collective-permute-start.85 = (bf16[64,1024]{1,0:T(8,128)(2,1)S(1)}, bf16[64,1024]{1,0:T(8,128)(2,1)S(1)}, u32[]{:S(2)}, u32[]{:S(2)}) collective-permute-start(bf16[64,1024]{1,0:T(8,128)(2,1)S(1)} %get-tuple-element.527), channel_id=1, source_target_pairs={{0,4},{4,0},{1,5},{5,1},{2,6},{6,2},{3,7},{7,3},{8,12},{12,8},{9,1... | collective-permute-start | bytes 393224 | tf_op jit(solution)/shard_map/ppermute | solution.py:895
  (81 other events, 832.2 us)

commit v5 on v4

--- a/solution.py
+++ b/solution.py
@@ -1253,7 +1253,7 @@
     douts = [array[None] for array in (by_head[0], *got)]
     send_z, send_y, top, low = spread(s.table, keep, send)
     got_z, got_y = swap(send_z, "zl"), swap(send_y, "y")
-    up_got = swap(after(up_send, send_z), "zh")
+    up_got = swap(up_send, "zh")
     up_near = swap(after(up_parts[2], send_z), "x")
     mate_2 = swap(after(mate_1, send_z), "x")
     kept = (after(kept[0], send_z), *kept[1:])

time: 259 us -> 259 us (level)
  no operation moved by 1% of the time
where the time goes in v5:
time: 259 us; the launch traced here: 257 us
  waiting for transfers between devices  118 us (46%)
  starting transfers between devices  85.9 us (33%)
  Pallas kernels  46.4 us (18%)
    ppermute x50, waiting for transfers between devices, swap(): return lax.ppermute(array, axis, SWAP)  63.1 us
    pallas_call x37, Pallas kernels, call(): pl.pallas_call(body, out_shape=[jax.ShapeDtypeStruct(shape, kind) for sha...  46.4 us
    ppermute x50, starting transfers between devices, swap(): return lax.ppermute(array, axis, SWAP)  43.5 us
    ppermute x12, waiting for transfers between devices, far(): lax.ppermute(arrays[at], ('zh', 'zl'), apart(4, at))  24.5 us
    ppermute x15, waiting for transfers between devices, near(): lax.ppermute(arrays[at], ('y', 'c'), apart(4, at))  21.5 us
    ppermute x12, starting transfers between devices, far(): lax.ppermute(arrays[at], ('zh', 'zl'), apart(4, at))  18.5 us
    ppermute x15, starting transfers between devices, near(): lax.ppermute(arrays[at], ('y', 'c'), apart(4, at))  9.2 us
    ppermute x4, starting transfers between devices, behind(): return lax.ppermute(array, CHIPS, left)  7.45 us
  transfers between devices with their start and end apart: 90, of which 45 were waited for; matrix products, arithmetic and copies ran while one was open for 1% of the time, Pallas kernels for 10%

profile of v5, /device:TPU:0, one launch (start us, length us, event | category | flops | bytes accessed | tf_op | source)
XLA Modules:
  0.0 257.0 jit_solution(14610054937015350070)
XLA Ops:
  1.3 3.3 %shard_map.186 = (bf16[128,1024]{1,0:T(8,128)(2,1)}, bf16[4,56,128]{2,1,0:T(8,128)(2,1)}, bf16[4,56,128]{2,1,0:T(8,128)(2,1)}, bf16[4,56,128]{2,1,0:T(8,128)(2,1...) custom-call(s32[6]{0:T(128)} %stack.24.table._, ...), custom_call_target="tpu_custom_call" | custom-call | flops 1000 | bytes 1024 | tf_op jit(solution)/shard_map/pallas_call | solution.py:95
  4.6 3.0 %collective-permute-start.1 = (bf16[128,1024]{1,0:T(8,128)(2,1)}, bf16[128,1024]{1,0:T(8,128)(2,1)S(1)}, u32[]{:S(2)}, u32[]{:S(2)}) collective-permute-start(bf16[128,1024]{1,0:T(8,128)(2,1)} %get-tuple-element.281.refs_0_), channel_id=1, source_target_pairs={{8,0},{16,8},{24,16},{28,24},{20,28},{12,20},{4,12},{0,4},{9,1},{1... | collective-permute-start | bytes 786440 | tf_op jit(solution)/shard_map/ppermute | solution.py:1166
  9.8 7.6 %collective-permute-done.3.refs_2_ = bf16[4,56,128]{2,1,0:T(8,128)(2,1)S(1)} collective-permute-done((bf16[4,56,128]{2,1,0:T(8,128)(2,1)}, bf16[4,56,128]{2,1,0:T(8,128)(2,1)S(1)}, u32[]{:S(2)}, u32[]{:S(2)}) %collective-permute-start.3) | collective-permute-done | bytes 57376 | tf_op jit(solution)/shard_map/ppermute | solution.py:887
  20.5 2.9 %collective-permute-start.8 = (bf16[4,56,128]{2,1,0:T(8,128)(2,1)S(1)}, bf16[4,56,128]{2,1,0:T(8,128)(2,1)S(1)}, u32[]{:S(2)}, u32[]{:S(2)}) collective-permute-start(bf16[4,56,128]{2,1,0:T(8,128)(2,1)S(1)} %get-tuple-element.292), channel_id=1, source_target_pairs={{0,16},{8,24},{16,0},{24,8},{1,17},{9,25},{17,1},{25,9},{2,18},{10... | collective-permute-start | bytes 172040 | tf_op jit(solution)/shard_map/ppermute | solution.py:891
  24.8 3.6 %collective-permute-done.7.refs_1_ = bf16[4,56,128]{2,1,0:T(8,128)(2,1)S(1)} collective-permute-done((bf16[4,56,128]{2,1,0:T(8,128)(2,1)S(1)}, bf16[4,56,128]{2,1,0:T(8,128)(2,1)S(1)}, u32[]{:S(2)}, u32[]{:S(2)}) %collective-permute-start.7) | collective-permute-done | bytes 57376 | tf_op jit(solution)/shard_map/ppermute | solution.py:891
  29.0 2.9 %collective-permute-done.9.refs_3_ = bf16[4,56,128]{2,1,0:T(8,128)(2,1)S(1)} collective-permute-done((bf16[4,56,128]{2,1,0:T(8,128)(2,1)S(1)}, bf16[4,56,128]{2,1,0:T(8,128)(2,1)S(1)}, u32[]{:S(2)}, u32[]{:S(2)}) %collective-permute-start.9) | collective-permute-done | bytes 57376 | tf_op jit(solution)/shard_map/ppermute | solution.py:891
  58.6 6.8 %shard_map.193 = (bf16[4,64,128]{2,1,0:T(8,128)(2,1)S(1)}, bf16[4,64,128]{2,1,0:T(8,128)(2,1)S(1)}, bf16[4,64,128]{2,1,0:T(8,128)(2,1)S(1)}, bf16[4,64,128]{2,1,...) custom-call(s32[6]{0:T(128)S(1)} %copy-done.7, ...), custom_call_target="tpu_custom_call" | custom-call | flops 7000001024 | bytes 1024 | tf_op jit(solution)/shard_map/pallas_call | solution.py:95
  73.1 5.3 %collective-permute-done.28.refs_2_ = bf16[4,64,128]{2,1,0:T(8,128)(2,1)S(1)} collective-permute-done((bf16[4,64,128]{2,1,0:T(8,128)(2,1)S(1)}, bf16[4,64,128]{2,1,0:T(8,128)(2,1)S(1)}, u32[]{:S(2)}, u32[]{:S(2)}) %collective-permute-start.28) | collective-permute-done | bytes 65568 | tf_op jit(solution)/shard_map/ppermute | solution.py:887
  78.4 2.9 %collective-permute-done.31.refs_13_ = bf16[256,512]{1,0:T(8,128)(2,1)S(1)} collective-permute-done((bf16[256,512]{1,0:T(8,128)(2,1)S(1)}, bf16[256,512]{1,0:T(8,128)(2,1)S(1)}, u32[]{:S(2)}, u32[]{:S(2)}) %collective-permute-start.31) | collective-permute-done | bytes 262176 | tf_op jit(solution)/shard_map/ppermute | solution.py:895
  83.5 2.9 %collective-permute-start.34 = (bf16[4,64,128]{2,1,0:T(8,128)(2,1)S(1)}, bf16[4,64,128]{2,1,0:T(8,128)(2,1)S(1)}, u32[]{:S(2)}, u32[]{:S(2)}) collective-permute-start(bf16[4,64,128]{2,1,0:T(8,128)(2,1)S(1)} %get-tuple-element.345), channel_id=1, source_target_pairs={{0,16},{8,24},{16,0},{24,8},{1,17},{9,25},{17,1},{25,9},{2,18},{10... | collective-permute-start | bytes 196616 | tf_op jit(solution)/shard_map/ppermute | solution.py:891
  90.9 3.7 %collective-permute-done.35.refs_7_ = bf16[4,64,128]{2,1,0:T(8,128)(2,1)S(1)} collective-permute-done((bf16[4,64,128]{2,1,0:T(8,128)(2,1)S(1)}, bf16[4,64,128]{2,1,0:T(8,128)(2,1)S(1)}, u32[]{:S(2)}, u32[]{:S(2)}) %collective-permute-start.35) | collective-permute-done | bytes 65568 | tf_op jit(solution)/shard_map/ppermute | solution.py:891
  101.3 2.9 %collective-permute-start.40 = (bf16[128,1024]{1,0:T(8,128)(2,1)S(1)}, bf16[128,1024]{1,0:T(8,128)(2,1)S(1)}, u32[]{:S(2)}, u32[]{:S(2)}) collective-permute-start(bf16[128,1024]{1,0:T(8,128)(2,1)S(1)} %get-tuple-element.358.mid_ref.refs_4_), channel_id=1, source_target_pairs={{0,8},{8,0},{1,9},{9,1},{2,10},{10,2},{3,11},{11,3},{4,12},{12,4},... | collective-permute-start | bytes 786440 | tf_op jit(solution)/shard_map/ppermute | solution.py:895
  104.2 3.8 %collective-permute-done.42.refs_15_ = bf16[256,512]{1,0:T(8,128)(2,1)S(1)} collective-permute-done((bf16[256,512]{1,0:T(8,128)(2,1)S(1)}, bf16[256,512]{1,0:T(8,128)(2,1)S(1)}, u32[]{:S(2)}, u32[]{:S(2)}) %collective-permute-start.42) | collective-permute-done | bytes 262176 | tf_op jit(solution)/shard_map/ppermute | solution.py:895
  108.0 6.5 %collective-permute-done.43.refs_17_ = bf16[256,512]{1,0:T(8,128)(2,1)S(1)} collective-permute-done((bf16[256,512]{1,0:T(8,128)(2,1)S(1)}, bf16[256,512]{1,0:T(8,128)(2,1)S(1)}, u32[]{:S(2)}, u32[]{:S(2)}) %collective-permute-start.43) | collective-permute-done | bytes 262176 | tf_op jit(solution)/shard_map/ppermute | solution.py:895
  117.4 7.2 %collective-permute-done.48.refs_19_ = bf16[256,512]{1,0:T(8,128)(2,1)S(1)} collective-permute-done((bf16[256,512]{1,0:T(8,128)(2,1)S(1)}, bf16[256,512]{1,0:T(8,128)(2,1)S(1)}, u32[]{:S(2)}, u32[]{:S(2)}) %collective-permute-start.48) | collective-permute-done | bytes 262176 | tf_op jit(solution)/shard_map/ppermute | solution.py:895
  127.4 6.5 %shard_map.201 = (bf16[512,1024]{1,0:T(8,128)(2,1)S(1)}, bf16[512,1024]{1,0:T(8,128)(2,1)S(1)}, f32[512,1024]{1,0:T(8,128)S(1)}, bf16[512,1024]{1,0:T(8,128)(2,1...) custom-call(s32[6]{0:T(128)S(1)} %copy-done.7, ...), custom_call_target="tpu_custom_call" | custom-call | flops 6000001024 | bytes 1024 | tf_op jit(solution)/shard_map/pallas_call | solution.py:95
  141.4 4.5 %collective-permute-done.53.got_y = bf16[2,64,1024]{2,1,0:T(8,128)(2,1)S(1)} collective-permute-done((bf16[2,64,1024]{2,1,0:T(8,128)(2,1)S(1)}, bf16[2,64,1024]{2,1,0:T(8,128)(2,1)S(1)}, u32[]{:S(2)}, u32[]{:S(2)}) %collective-permute-start.53) | collective-permute-done | bytes 262176 | tf_op jit(solution)/shard_map/ppermute | solution.py:895
  163.3 5.3 %collective-permute-done.60.refs_1_ = bf16[512,192]{1,0:T(8,128)(2,1)S(1)} collective-permute-done((bf16[512,192]{1,0:T(8,128)(2,1)S(1)}, bf16[512,192]{1,0:T(8,128)(2,1)S(1)}, u32[]{:S(2)}, u32[]{:S(2)}) %collective-permute-start.60) | collective-permute-done | bytes 196640 | tf_op jit(solution)/shard_map/ppermute | solution.py:895
  175.0 3.4 %collective-permute-done.62 = bf16[4,64,128]{2,1,0:T(8,128)(2,1)S(1)} collective-permute-done((bf16[4,64,128]{2,1,0:T(8,128)(2,1)S(1)}, bf16[4,64,128]{2,1,0:T(8,128)(2,1)S(1)}, u32[]{:S(2)}, u32[]{:S(2)}) %collective-permute-start.62) | collective-permute-done | bytes 65568 | tf_op jit(solution)/shard_map/ppermute | solution.py:891
  184.7 7.2 %shard_map.211 = (bf16[8,192,128]{2,1,0:T(8,128)(2,1)S(1)}, bf16[8,192,128]{2,1,0:T(8,128)(2,1)S(1)}, bf16[16,128,192]{2,1,0:T(8,128)(2,1)S(1)}, f32[1,192]{1,0:T(1,128)S(1)}) custom-call(s32[6]{0:T(128)S(1)} %copy-done.7, bf16[1,4,64,128]{3,2,1,0:T(8,128)(2,1)S(1)} %bitcast.47, bf16[1,4,64,128]{3,2,1,0:T(8,128)(2,1)S(1)} %bitcast.48, ...), custom_call_target="tpu_custom_call" | custom-call | flops 8000001024 | bytes 1024 | tf_op jit(solution)/shard_map/pallas_call | solution.py:95
  204.5 5.0 %collective-permute-done.73.got_ref = bf16[16,56,128]{2,1,0:T(8,128)(2,1)S(1)} collective-permute-done((bf16[16,56,128]{2,1,0:T(8,128)(2,1)S(1)}, bf16[16,56,128]{2,1,0:T(8,128)(2,1)S(1)}, u32[]{:S(2)}, u32[]{:S(2)}) %collective-permute-start.73) | collective-permute-done | bytes 229408 | tf_op jit(solution)/shard_map/ppermute | solution.py:895
  229.8 4.2 %collective-permute-done.84.refs_6_ = bf16[4,56,128]{2,1,0:T(8,128)(2,1)S(1)} collective-permute-done((bf16[4,56,128]{2,1,0:T(8,128)(2,1)S(1)}, bf16[4,56,128]{2,1,0:T(8,128)(2,1)S(1)}, u32[]{:S(2)}, u32[]{:S(2)}) %collective-permute-start.84) | collective-permute-done | bytes 57376 | tf_op jit(solution)/shard_map/ppermute | solution.py:1301
  234.0 4.9 %collective-permute-done.82.down_got = bf16[128,1024]{1,0:T(8,128)(2,1)S(1)} collective-permute-done((bf16[128,1024]{1,0:T(8,128)(2,1)S(1)}, bf16[128,1024]{1,0:T(8,128)(2,1)S(1)}, u32[]{:S(2)}, u32[]{:S(2)}) %collective-permute-start.82) | collective-permute-done | bytes 262176 | tf_op jit(solution)/shard_map/ppermute | solution.py:895
  246.4 7.5 %collective-permute-done.89.q3_ref = bf16[4,56,128]{2,1,0:T(8,128)(2,1)S(1)} collective-permute-done((bf16[4,56,128]{2,1,0:T(8,128)(2,1)S(1)}, bf16[4,56,128]{2,1,0:T(8,128)(2,1)S(1)}, u32[]{:S(2)}, u32[]{:S(2)}) %collective-permute-start.89) | collective-permute-done | bytes 57376 | tf_op jit(solution)/shard_map/ppermute | solution.py:891
  (228 shorter events, 141.5 us)
Async XLA Ops:
  4.6 12.8 %collective-permute-start.1 = (bf16[128,1024]{1,0:T(8,128)(2,1)}, bf16[128,1024]{1,0:T(8,128)(2,1)S(1)}, u32[]{:S(2)}, u32[]{:S(2)}) collective-permute-start(bf16[128,1024]{1,0:T(8,128)(2,1)} %get-tuple-element.281.refs_0_), channel_id=1, source_target_pairs={{8,0},{16,8},{24,16},{28,24},{20,28},{12,20},{4,12},{0,4},{9,1},{1... | collective-permute-start | bytes 786440 | tf_op jit(solution)/shard_map/ppermute | solution.py:1166
  17.5 14.5 %collective-permute-start.5 = (bf16[128,1024]{1,0:T(8,128)(2,1)S(1)}, bf16[128,1024]{1,0:T(8,128)(2,1)S(1)}, u32[]{:S(2)}, u32[]{:S(2)}) collective-permute-start(bf16[128,1024]{1,0:T(8,128)(2,1)S(1)} %collective-permute-done.refs_1_), channel_id=1, source_target_pairs={{0,8},{8,16},{16,24},{24,28},{28,20},{20,12},{12,4},{4,0},{1,9},{9... | collective-permute-start | bytes 786440 | tf_op jit(solution)/shard_map/ppermute | solution.py:1163
  17.5 14.4 %collective-permute-start.6 = (bf16[128,1024]{1,0:T(8,128)(2,1)S(1)}, bf16[128,1024]{1,0:T(8,128)(2,1)S(1)}, u32[]{:S(2)}, u32[]{:S(2)}) collective-permute-start(bf16[128,1024]{1,0:T(8,128)(2,1)S(1)} %collective-permute-done.1.refs_2_), channel_id=1, source_target_pairs={{8,0},{16,8},{24,16},{28,24},{20,28},{12,20},{4,12},{0,4},{9,1},{1... | collective-permute-start | bytes 786440 | tf_op jit(solution)/shard_map/ppermute | solution.py:1166
  44.3 14.2 %collective-permute-start.21 = (bf16[2,128,1024]{2,1,0:T(8,128)(2,1)S(1)}, bf16[2,128,1024]{2,1,0:T(8,128)(2,1)S(1)}, u32[]{:S(2)}, u32[]{:S(2)}) collective-permute-start(bf16[2,128,1024]{2,1,0:T(8,128)(2,1)S(1)} %shard_map.192), channel_id=1, source_target_pairs={{0,2},{2,0},{1,3},{3,1},{4,6},{6,4},{5,7},{7,5},{8,10},{10,8},{9,1... | collective-permute-start | bytes 1572872 | tf_op jit(solution)/shard_map/ppermute | solution.py:895
  67.7 13.7 %collective-permute-start.31 = (bf16[256,512]{1,0:T(8,128)(2,1)S(1)}, bf16[256,512]{1,0:T(8,128)(2,1)S(1)}, u32[]{:S(2)}, u32[]{:S(2)}) collective-permute-start(bf16[256,512]{1,0:T(8,128)(2,1)S(1)} %shard_map.195.refs_12_), channel_id=1, source_target_pairs={{0,16},{16,0},{1,17},{17,1},{2,18},{18,2},{3,19},{19,3},{4,20},{20... | collective-permute-start | bytes 786440 | tf_op jit(solution)/shard_map/ppermute | solution.py:895
  68.8 12.6 %collective-permute-start.32 = (bf16[128,1024]{1,0:T(8,128)(2,1)S(1)}, bf16[128,1024]{1,0:T(8,128)(2,1)S(1)}, u32[]{:S(2)}, u32[]{:S(2)}) collective-permute-start(bf16[128,1024]{1,0:T(8,128)(2,1)S(1)} %bitcast.34), channel_id=1, source_target_pairs={{0,4},{4,0},{1,5},{5,1},{2,6},{6,2},{3,7},{7,3},{8,12},{12,8},{9,1... | collective-permute-start | bytes 786440 | tf_op jit(solution)/shard_map/ppermute | solution.py:895
  81.4 13.2 %collective-permute-start.38 = (bf16[8,32,1024]{2,1,0:T(8,128)(2,1)S(1)}, bf16[8,32,1024]{2,1,0:T(8,128)(2,1)S(1)}, u32[]{:S(2)}, u32[]{:S(2)}) collective-permute-start(bf16[8,32,1024]{2,1,0:T(8,128)(2,1)S(1)} %shard_map.196.refs_0_), channel_id=1, source_target_pairs={{0,2},{2,0},{1,3},{3,1},{4,6},{6,4},{5,7},{7,5},{8,10},{10,8},{9,1... | collective-permute-start | bytes 1572872 | tf_op jit(solution)/shard_map/ppermute | solution.py:895
  81.5 14.3 %collective-permute-start.36 = (bf16[8,32,1024]{2,1,0:T(8,128)(2,1)S(1)}, bf16[8,32,1024]{2,1,0:T(8,128)(2,1)S(1)}, u32[]{:S(2)}, u32[]{:S(2)}) collective-permute-start(bf16[8,32,1024]{2,1,0:T(8,128)(2,1)S(1)} %shard_map.196.refs_0_), channel_id=1, source_target_pairs={{0,4},{4,0},{1,5},{5,1},{2,6},{6,2},{3,7},{7,3},{8,12},{12,8},{9,1... | collective-permute-start | bytes 1572872 | tf_op jit(solution)/shard_map/ppermute | solution.py:895
  99.2 16.6 %collective-permute-start.44 = (bf16[3,128,1024]{2,1,0:T(8,128)(2,1)S(1)}, bf16[3,128,1024]{2,1,0:T(8,128)(2,1)S(1)}, u32[]{:S(2)}, u32[]{:S(2)}) collective-permute-start(bf16[3,128,1024]{2,1,0:T(8,128)(2,1)S(1)} %shard_map.199), channel_id=1, source_target_pairs={{0,2},{2,0},{1,3},{3,1},{4,6},{6,4},{5,7},{7,5},{8,10},{10,8},{9,1... | collective-permute-start | bytes 2359304 | tf_op jit(solution)/shard_map/ppermute | solution.py:895
  100.3 14.2 %collective-permute-start.43 = (bf16[256,512]{1,0:T(8,128)(2,1)S(1)}, bf16[256,512]{1,0:T(8,128)(2,1)S(1)}, u32[]{:S(2)}, u32[]{:S(2)}) collective-permute-start(bf16[256,512]{1,0:T(8,128)(2,1)S(1)} %copy-done.6), channel_id=1, source_target_pairs={{0,16},{16,0},{1,17},{17,1},{2,18},{18,2},{3,19},{19,3},{4,20},{20... | collective-permute-start | bytes 786440 | tf_op jit(solution)/shard_map/ppermute | solution.py:895
  100.3 14.2 %collective-permute-start.41 = (bf16[128,1024]{1,0:T(8,128)(2,1)S(1)}, bf16[128,1024]{1,0:T(8,128)(2,1)S(1)}, u32[]{:S(2)}, u32[]{:S(2)}) collective-permute-start(bf16[128,1024]{1,0:T(8,128)(2,1)S(1)} %get-tuple-element.358.mid_ref.refs_4_), channel_id=1, source_target_pairs={{0,4},{4,0},{1,5},{5,1},{2,6},{6,2},{3,7},{7,3},{8,12},{12,8},{9,1... | collective-permute-start | bytes 786440 | tf_op jit(solution)/shard_map/ppermute | solution.py:895
  101.3 14.4 %collective-permute-start.40 = (bf16[128,1024]{1,0:T(8,128)(2,1)S(1)}, bf16[128,1024]{1,0:T(8,128)(2,1)S(1)}, u32[]{:S(2)}, u32[]{:S(2)}) collective-permute-start(bf16[128,1024]{1,0:T(8,128)(2,1)S(1)} %get-tuple-element.358.mid_ref.refs_4_), channel_id=1, source_target_pairs={{0,8},{8,0},{1,9},{9,1},{2,10},{10,2},{3,11},{11,3},{4,12},{12,4},... | collective-permute-start | bytes 786440 | tf_op jit(solution)/shard_map/ppermute | solution.py:895
  155.0 13.7 %collective-permute-start.59 = (bf16[264,512]{1,0:T(8,128)(2,1)S(1)}, bf16[264,512]{1,0:T(8,128)(2,1)S(1)}, u32[]{:S(2)}, u32[]{:S(2)}) collective-permute-start(bf16[264,512]{1,0:T(8,128)(2,1)S(1)} %get-tuple-element.411), channel_id=1, source_target_pairs={{0,1},{1,0},{2,3},{3,2},{4,5},{5,4},{6,7},{7,6},{8,9},{9,8},{10,11... | collective-permute-start | bytes 811016 | tf_op jit(solution)/shard_map/ppermute | solution.py:895
  179.4 19.7 %collective-permute-start.66 = (bf16[2,128,1024]{2,1,0:T(8,128)(2,1)S(1)}, bf16[2,128,1024]{2,1,0:T(8,128)(2,1)S(1)}, u32[]{:S(2)}, u32[]{:S(2)}) collective-permute-start(bf16[2,128,1024]{2,1,0:T(8,128)(2,1)S(1)} %get-tuple-element.443), channel_id=1, source_target_pairs={{0,8},{8,0},{1,9},{9,1},{2,10},{10,2},{3,11},{11,3},{4,12},{12,4},... | collective-permute-start | bytes 1572872 | tf_op jit(solution)/shard_map/ppermute | solution.py:895
  181.7 14.4 %collective-permute-start.68 = (bf16[264,512]{1,0:T(8,128)(2,1)S(1)}, bf16[264,512]{1,0:T(8,128)(2,1)S(1)}, u32[]{:S(2)}, u32[]{:S(2)}) collective-permute-start(bf16[264,512]{1,0:T(8,128)(2,1)S(1)} %get-tuple-element.453), channel_id=1, source_target_pairs={{0,1},{1,0},{2,3},{3,2},{4,5},{5,4},{6,7},{7,6},{8,9},{9,8},{10,11... | collective-permute-start | bytes 811016 | tf_op jit(solution)/shard_map/ppermute | solution.py:895
  182.7 16.2 %collective-permute-start.70 = (bf16[264,512]{1,0:T(8,128)(2,1)S(1)}, bf16[264,512]{1,0:T(8,128)(2,1)S(1)}, u32[]{:S(2)}, u32[]{:S(2)}) collective-permute-start(bf16[264,512]{1,0:T(8,128)(2,1)S(1)} %shard_map.209), channel_id=1, source_target_pairs={{0,16},{16,0},{1,17},{17,1},{2,18},{18,2},{3,19},{19,3},{4,20},{20... | collective-permute-start | bytes 811016 | tf_op jit(solution)/shard_map/ppermute | solution.py:895
  184.0 14.9 %collective-permute-start.67 = (bf16[2,128,1024]{2,1,0:T(8,128)(2,1)S(1)}, bf16[2,128,1024]{2,1,0:T(8,128)(2,1)S(1)}, u32[]{:S(2)}, u32[]{:S(2)}) collective-permute-start(bf16[2,128,1024]{2,1,0:T(8,128)(2,1)S(1)} %get-tuple-element.451), channel_id=1, source_target_pairs={{0,4},{4,0},{1,5},{5,1},{2,6},{6,2},{3,7},{7,3},{8,12},{12,8},{9,1... | collective-permute-start | bytes 1572872 | tf_op jit(solution)/shard_map/ppermute | solution.py:895
  191.9 22.6 %collective-permute-start.74 = (bf16[8,192,128]{2,1,0:T(8,128)(2,1)S(1)}, bf16[8,192,128]{2,1,0:T(8,128)(2,1)S(1)}, u32[]{:S(2)}, u32[]{:S(2)}) collective-permute-start(bf16[8,192,128]{2,1,0:T(8,128)(2,1)S(1)} %get-tuple-element.478), channel_id=1, source_target_pairs={{0,16},{16,0},{1,17},{17,1},{2,18},{18,2},{3,19},{19,3},{4,20},{20... | collective-permute-start | bytes 1179656 | tf_op jit(solution)/shard_map/ppermute | solution.py:895
  223.8 15.3 %collective-permute-start.81 = (bf16[4,312,128]{2,1,0:T(8,128)(2,1)S(1)}, bf16[4,312,128]{2,1,0:T(8,128)(2,1)S(1)}, u32[]{:S(2)}, u32[]{:S(2)}) collective-permute-start(bf16[4,312,128]{2,1,0:T(8,128)(2,1)S(1)} %get-tuple-element.505), channel_id=1, source_target_pairs={{0,4},{4,0},{1,5},{5,1},{2,6},{6,2},{3,7},{7,3},{8,12},{12,8},{9,1... | collective-permute-start | bytes 958472 | tf_op jit(solution)/shard_map/ppermute | solution.py:895
  224.8 14.1 %collective-permute-start.82 = (bf16[128,1024]{1,0:T(8,128)(2,1)S(1)}, bf16[128,1024]{1,0:T(8,128)(2,1)S(1)}, u32[]{:S(2)}, u32[]{:S(2)}) collective-permute-start(bf16[128,1024]{1,0:T(8,128)(2,1)S(1)} %shard_map.214), channel_id=1, source_target_pairs={{0,16},{16,0},{1,17},{17,1},{2,18},{18,2},{3,19},{19,3},{4,20},{20... | collective-permute-start | bytes 786440 | tf_op jit(solution)/shard_map/ppermute | solution.py:895
  224.8 14.3 %collective-permute-start.80 = (bf16[2,64,1024]{2,1,0:T(8,128)(2,1)S(1)}, bf16[2,64,1024]{2,1,0:T(8,128)(2,1)S(1)}, u32[]{:S(2)}, u32[]{:S(2)}) collective-permute-start(bf16[2,64,1024]{2,1,0:T(8,128)(2,1)S(1)} %get-tuple-element.504), channel_id=1, source_target_pairs={{0,8},{8,0},{1,9},{9,1},{2,10},{10,2},{3,11},{11,3},{4,12},{12,4},... | collective-permute-start | bytes 786440 | tf_op jit(solution)/shard_map/ppermute | solution.py:895
  239.8 14.1 %collective-permute-start.87 = (bf16[4,344,128]{2,1,0:T(8,128)(2,1)S(1)}, bf16[4,344,128]{2,1,0:T(8,128)(2,1)S(1)}, u32[]{:S(2)}, u32[]{:S(2)}) collective-permute-start(bf16[4,344,128]{2,1,0:T(8,128)(2,1)S(1)} %get-tuple-element.528), channel_id=1, source_target_pairs={{0,8},{8,0},{16,24},{24,16},{1,9},{9,1},{17,25},{25,17},{2,10},{10... | collective-permute-start | bytes 1056776 | tf_op jit(solution)/shard_map/ppermute | solution.py:891
  239.9 14.1 %collective-permute-start.86 = (bf16[128,1024]{1,0:T(8,128)(2,1)S(1)}, bf16[128,1024]{1,0:T(8,128)(2,1)S(1)}, u32[]{:S(2)}, u32[]{:S(2)}) collective-permute-start(bf16[128,1024]{1,0:T(8,128)(2,1)S(1)} %get-tuple-element.527), channel_id=1, source_target_pairs={{0,1},{1,0},{2,3},{3,2},{4,5},{5,4},{6,7},{7,6},{8,9},{9,8},{10,11... | collective-permute-start | bytes 786440 | tf_op jit(solution)/shard_map/ppermute | solution.py:895
  240.9 13.1 %collective-permute-start.85 = (bf16[64,1024]{1,0:T(8,128)(2,1)S(1)}, bf16[64,1024]{1,0:T(8,128)(2,1)S(1)}, u32[]{:S(2)}, u32[]{:S(2)}) collective-permute-start(bf16[64,1024]{1,0:T(8,128)(2,1)S(1)} %get-tuple-element.525), channel_id=1, source_target_pairs={{0,4},{4,0},{1,5},{5,1},{2,6},{6,2},{3,7},{7,3},{8,12},{12,8},{9,1... | collective-permute-start | bytes 393224 | tf_op jit(solution)/shard_map/ppermute | solution.py:895
  (81 other events, 832.2 us)
